TPU v7x, 32 devices: a whole 2x2x4 slice. The times are simulated.
32 devices in a mesh: space: 4 (over y, core), vel: 8 (over z, x).
Axes of the slice: x: 2, y: 2, z: 4, core: 2. Of those that a mesh axis runs over, the one named last changes fastest.
Arguments:
- distribution: float32 [6, 1024, 4096], P(None, 'space', 'vel'), may hold values from -4 to 4
- corners: float32 [2, 3, 1024], P(None, None, 'space'), may hold values from -1 to 49, as said below
- neighbour: int32 [3, 1024], P(None, 'space'), may hold values from -1 to 767, as said below
- boundary_faces: int32 [4, 2, 80], P('space'), may hold values from -1 to 767, as said below
- collision_rate: float32 [1024], P('space'), may hold values from 1 to 20
Outputs:
- advanced: float32 [6, 1024, 4096], P(None, 'space', 'vel')
Inputs may be any that keep to these rules, and one draw needn't show every extreme that they name: corners[:, k, e] are the coordinates of corner k of triangle e, counterclockwise; triangles sharing an edge hold its two corners at equal coordinates; every det_e is 0.1 or more. neighbour[m, e] = m' 256 + e' names the face of a triangle of the same partition that shares face m of triangle e and runs along it the other way; -1 where the triangle on the other side lies in another partition or the face lies on the domain's two ends. boundary_faces[p, 0] and boundary_faces[p, 1] list local face numbers of partition p whose other side lies in partition p - 1 (for p = 0, the domain's lower end) and p + 1 (for the last partition, the upper end); slot k of p's second list and slot k of p + 1's first list are the two sides of one edge, run the other way; a slot is -1 in both lists or in neither; every face with neighbour -1 stands in exactly one slot; each list's live slots come first; some list has all 80 slots live.
All inputs are finite; a program needn't handle non-finite values. Where the computation divides by a largest or mean magnitude, that divisor is 1e-20 or more.
Results may differ from a plain program's by a relative error of at most 0.0003.
Values sent between devices are 32-bit elements; how exact they have to be, the bound alone decides.
No kernel may reach another device: no remote copies, remote signals or barrier semaphores. Data moves between devices by JAX's collectives and lax.ppermute only.
A program may use at most 128 MiB of HBM per device.

v0:
```python
import math

import jax
import jax.numpy as jnp
import numpy as np
from jax import lax
from jax.experimental import pallas as pl
from jax.experimental.pallas import tpu as pltpu
from jax.sharding import PartitionSpec as P

VGRID = 64
velocity_limit = 6.0
time_step = 0.012
viscous_conductive_ratio = 2.0 / 3.0
density_floor = 0.1
kelvin_lower_limit = 0.2
skew_multiplier_limit = 0.9
slope_floor = 0.01

LANE = 128
SUB = 8
PITCH = 16
MODES = 6
TERMS = 32
f32 = jnp.float32
bf16 = jnp.bfloat16


def monomial_integral(power_r, power_s):
    return math.factorial(power_r) * math.factorial(power_s) / math.factorial(power_r + power_s + 2)


def dg_tables():
    powers = [(0, 0), (1, 0), (0, 1), (2, 0), (1, 1), (0, 2)]
    gram = np.array(
        [[monomial_integral(a[0] + b[0], a[1] + b[1]) for b in powers] for a in powers]
    )
    coeffs = np.linalg.inv(np.linalg.cholesky(gram))
    deriv_r = np.zeros((6, 6))
    deriv_s = np.zeros((6, 6))
    for i, a in enumerate(powers):
        for j, b in enumerate(powers):
            if a[0] > 0:
                deriv_r[i, j] = a[0] * monomial_integral(a[0] - 1 + b[0], a[1] + b[1])
            if a[1] > 0:
                deriv_s[i, j] = a[1] * monomial_integral(a[0] + b[0], a[1] - 1 + b[1])
    stiff_r = coeffs @ deriv_r @ coeffs.T
    stiff_s = coeffs @ deriv_s @ coeffs.T

    def evaluate(location):
        return coeffs @ np.array([location[0] ** p[0] * location[1] ** p[1] for p in powers])

    vertices = np.array([[0.0, 0.0], [1.0, 0.0], [0.0, 1.0]])
    offset = math.sqrt(0.15)
    positions = np.array([0.5 - offset, 0.5, 0.5 + offset])
    weights = np.array([5.0, 8.0, 5.0]) / 18.0
    traces = np.zeros((3, 3, 6))
    for m in range(3):
        for q in range(3):
            along = positions[q]
            traces[m, q] = evaluate((1.0 - along) * vertices[m] + along * vertices[(m + 1) % 3])
    legendre = np.stack(
        [
            np.ones(3),
            math.sqrt(3.0) * (2.0 * positions - 1.0),
            math.sqrt(5.0) * (6.0 * positions**2 - 6.0 * positions + 1.0),
        ]
    )
    edge = np.einsum("lq,q,mqj->mlj", legendre, weights, traces)
    node_list = [(0.0, 0.0), (1.0, 0.0), (0.0, 1.0), (0.5, 0.0), (0.5, 0.5), (0.0, 0.5)]
    nodal = np.array([evaluate(np.array(n)) for n in node_list])
    inverse = np.linalg.inv(nodal)
    return stiff_r, stiff_s, traces, edge, nodal, inverse


KR, KS, TR, EDGE, NODAL, INVERSE = dg_tables()


def k(value):
    return float(np.float32(value))


def edge_parts(z):
    z0, z1, z2, z3, z4, z5 = z
    b = EDGE[0]
    a0 = z0 * k(b[0, 0])
    even = (
        a0 + z1 * k(b[0, 1]) + z3 * k(b[0, 3]) + z5 * k(b[0, 5]),
        z1 * k(b[1, 1]) + z3 * k(b[1, 3]) + z5 * k(b[1, 5]),
        z3 * k(b[2, 3]) + z5 * k(b[2, 5]),
    )
    odd = (
        z2 * k(-b[0, 2]) + z4 * k(-b[0, 4]),
        z2 * k(-b[1, 2]) + z4 * k(-b[1, 4]),
        z4 * k(-b[2, 4]),
    )
    c = EDGE[2]
    last = (
        a0 + z1 * k(c[0, 1]) + z3 * k(c[0, 3]),
        z2 * k(c[1, 2]) + z4 * k(c[1, 4]),
        z5 * k(c[2, 5]),
    )
    return a0, even, odd, last


def table_values(z):
    _, even, odd, last = edge_parts(z)
    return (
        (even[0] - odd[0], odd[1] - even[1], even[2] - odd[2]),
        (even[0] + odd[0], even[1] + odd[1], even[2] + odd[2]),
        (last[0], -last[1], last[2]),
    )


def tile(ref, row, chunk):
    return ref[pl.ds(row, SUB), pl.ds(chunk * LANE, LANE)]


def put_table(tbl, z, row, elems, chunk):
    for m, values in enumerate(table_values(z)):
        for level, value in enumerate(values):
            start = (m * elems + row) * PITCH + level * 4 + chunk
            tbl[pl.ds(start, SUB, stride=PITCH), :] = value


def fetch_rows(tbl, stage, base, index_of, pitch):
    for i in range(SUB):
        start = pl.multiple_of(index_of(i) * pitch, pitch)
        stage[pl.ds(base + i * pitch, pitch), :] = tbl[pl.ds(start, pitch), :]


def pack_faces(tbl, stage, lists, outs, slots):
    chunks = outs[0].shape[2] // LANE
    for side, out in enumerate(outs):

        def body(g, _, side=side, out=out):
            row = pl.multiple_of(g * SUB, SUB)
            fetch_rows(tbl, stage, 0, lambda i: jnp.maximum(lists[side, row + i], 0), PITCH)
            for level in range(3):
                for c in range(chunks):
                    out[level, pl.ds(row, SUB), pl.ds(c * LANE, LANE)] = stage[
                        pl.ds(level * 4 + c, SUB, stride=PITCH), :
                    ]
            return 0

        lax.fori_loop(0, slots // SUB, body, 0)


def grid_rows(first, shape):
    index = first + lax.broadcasted_iota(jnp.int32, shape, len(shape) - 1)
    spacing = 2.0 * velocity_limit / VGRID
    x = -velocity_limit + ((index // VGRID).astype(f32) + 0.5) * spacing
    y = -velocity_limit + ((index % VGRID).astype(f32) + 0.5) * spacing
    return x, y, spacing


def split3(value):
    high = value.astype(bf16).astype(f32)
    rest = value - high
    middle = rest.astype(bf16).astype(f32)
    return high, middle, (rest - middle).astype(bf16).astype(f32)


def put_moments(first, read_mode, out):
    vel = read_mode(0).shape[1]
    x, y, spacing = grid_rows(first, (SUB, vel))
    row = lax.broadcasted_iota(jnp.int32, (SUB, vel), 0)
    square = x * x + y * y
    weights = jnp.ones_like(x)
    for index, value in enumerate((x, y, x * x, x * y, y * y, x * square, y * square)):
        weights = jnp.where(row == index + 1, value, weights)
    weights = weights * (spacing * spacing)
    parts = split3(weights)
    stacked = jnp.concatenate([*parts, jnp.zeros_like(x)], axis=0).astype(bf16)
    for j in range(MODES):
        value = read_mode(j)
        high = value.astype(bf16)
        low = (value - high.astype(f32)).astype(bf16)
        dims = (((1,), (1,)), ((), ()))
        total = lax.dot_general(stacked, high, dims, preferred_element_type=f32)
        total = total + lax.dot_general(stacked, low, dims, preferred_element_type=f32)
        out[pl.ds(j * SUB, SUB), :] = total[0:8] + total[8:16] + total[16:24]


def open_kernel(lists, first, z_ref, neigh_ref, mom, low, up, src, tbl, stage):
    elems = z_ref.shape[1]
    chunks = z_ref.shape[2] // LANE
    slots = lists.shape[1]
    faces = 3 * elems

    def fill(g, _):
        row = pl.multiple_of(g * SUB, SUB)
        for c in range(chunks):
            z = [z_ref[j, pl.ds(row, SUB), pl.ds(c * LANE, LANE)] for j in range(MODES)]
            put_table(tbl, z, row, elems, c)
        return 0

    lax.fori_loop(0, elems // SUB, fill, 0)
    pack_faces(tbl, stage, lists, (low, up), slots)
    put_moments(first[0], lambda j: z_ref[j], mom)

    shape = neigh_ref.shape
    face = lax.broadcasted_iota(jnp.int32, shape, 0) * elems + lax.broadcasted_iota(jnp.int32, shape, 1)

    def mark(slot, found):
        found = jnp.where(face == lists[0, slot], faces + slot, found)
        return jnp.where(face == lists[1, slot], faces + slots + slot, found)

    src[...] = lax.fori_loop(0, slots, mark, neigh_ref[...])


def node_parameters(mom, rate, elems):
    shape = (SUB, elems)
    row = lax.broadcasted_iota(jnp.int32, shape, 0)

    def column(values):
        out = jnp.full(shape, k(values[0]), f32)
        for n in range(1, MODES):
            out = jnp.where(row == n, k(values[n]), out)
        return out

    columns = [column(NODAL[:, j]) for j in range(MODES)]
    R = []
    for index in range(8):
        total = columns[0] * mom[index : index + 1, :]
        for j in range(1, MODES):
            total = total + columns[j] * mom[j * SUB + index : j * SUB + index + 1, :]
        R.append(total)
    zeroth, mass_x, mass_y, flux_xx, flux_xy, flux_yy, third_x, third_y = R
    density = jnp.maximum(zeroth, density_floor)
    ux = mass_x / density
    uy = mass_y / density
    drift_sq = ux * ux + uy * uy
    drift_mass = ux * mass_x + uy * mass_y
    trace = flux_xx + flux_yy
    kelvin = jnp.maximum(
        (trace - 2.0 * drift_mass + drift_sq * zeroth) / (2.0 * density), kelvin_lower_limit
    )
    qx = 0.5 * (
        third_x
        - 2.0 * (flux_xx * ux + flux_xy * uy)
        + mass_x * drift_sq
        - ux * trace
        + 2.0 * ux * drift_mass
        - ux * drift_sq * zeroth
    )
    qy = 0.5 * (
        third_y
        - 2.0 * (flux_xy * ux + flux_yy * uy)
        + mass_y * drift_sq
        - uy * trace
        + 2.0 * uy * drift_mass
        - uy * drift_sq * zeroth
    )
    nu = time_step * rate * density
    over = 1.0 / kelvin
    weight = (1.0 - viscous_conductive_ratio) / (4.0 * density * kelvin * kelvin)
    qx = qx * weight
    qy = qy * weight
    excess = (over * drift_sq - 4.0, -2.0 * over * ux, -2.0 * over * uy, over, over)
    amplitude = jnp.log(nu * density * over * k(1.0 / (2.0 * math.pi)))
    exponent = (
        amplitude - 0.5 * over * drift_sq,
        over * ux,
        over * uy,
        -0.5 * over,
        -0.5 * over,
    )
    skew = (-(qx * ux + qy * uy), qx, qy)
    return nu, excess, exponent, skew, row


def put_basis(first, basis, vel):
    rows = TERMS * SUB
    x, y, _ = grid_rows(first, (1, vel))
    xx = x * x
    yy = y * y
    xx_high = xx.astype(bf16).astype(f32)
    yy_high = yy.astype(bf16).astype(f32)
    monomials = (jnp.ones_like(x), x, y, xx_high, xx - xx_high, yy_high, yy - yy_high)
    row = lax.broadcasted_iota(jnp.int32, (SUB, vel), 0)
    zero = jnp.zeros((2 * SUB, vel), bf16)
    for n in range(SUB):
        mine = row == n
        for pair in range(rows // (2 * SUB)):
            halves = []
            for term in (2 * pair, 2 * pair + 1):
                which = term // 3
                halves.append(
                    jnp.where(mine, monomials[which], 0.0)
                    if which < len(monomials)
                    else jnp.zeros((SUB, vel), f32)
                )
            value = jnp.concatenate(halves, axis=0).astype(bf16) if 2 * pair // 3 < 7 else zero
            basis[pl.ds(pair * 2 * SUB, 2 * SUB), pl.ds(n * vel, vel)] = value


def spread(form, elems):
    pieces = []
    for index, value in enumerate(form):
        parts = split3(value)
        pieces += parts
        if index >= 3:
            pieces += parts
    pieces.append(jnp.zeros((TERMS * SUB - SUB * len(pieces), elems), f32))
    return jnp.concatenate(pieces, axis=0).T.astype(bf16)


def update_kernel(src, lists, first, *refs, section):
    if section == 0:
        z_ref, low, up, m0, m1, m2, m3, rate, corner, out, mlow, mup = refs[:12]
        base_ref = None
        scratch = refs[12:]
    else:
        base_ref, z_ref, low, up, m0, m1, m2, m3, rate, corner, out, mlow, mup = refs[:13]
        scratch = refs[13:]
    tbl, stage, mtbl, basis, qn, qa, ql, nus = scratch
    elems, vel = z_ref.shape[1:]
    chunks = vel // LANE
    slots = lists.shape[1]
    faces = 3 * elems

    def fill(g, _):
        row = pl.multiple_of(g * SUB, SUB)
        for c in range(chunks):
            z = [z_ref[j, pl.ds(row, SUB), pl.ds(c * LANE, LANE)] for j in range(MODES)]
            put_table(tbl, z, row, elems, c)
        return 0

    lax.fori_loop(0, elems // SUB, fill, 0)

    def fill_border(g, _):
        row = pl.multiple_of(g * SUB, SUB)
        for side, halo in enumerate((low, up)):
            for level in range(3):
                for c in range(chunks):
                    start = (faces + side * slots + row) * PITCH + level * 4 + c
                    tbl[pl.ds(start, SUB, stride=PITCH), :] = halo[
                        level, pl.ds(row, SUB), pl.ds(c * LANE, LANE)
                    ]
        return 0

    lax.fori_loop(0, slots // SUB, fill_border, 0)

    put_basis(first[0], basis, vel)
    moments = (m0[...] + m1[...]) + (m2[...] + m3[...])
    nu, excess, exponent, skew, row8 = node_parameters(moments, rate[...], elems)
    cx = [corner[i : i + 1, :] for i in range(3)]
    cy = [corner[3 + i : 4 + i, :] for i in range(3)]
    det = (cx[1] - cx[0]) * (cy[2] - cy[0]) - (cx[2] - cx[0]) * (cy[1] - cy[0])
    step = time_step / det
    flow0 = (-step * (cy[1] - cy[0]), step * (cx[1] - cx[0]))
    flow2 = (-step * (cy[0] - cy[2]), step * (cx[0] - cx[2]))
    linear = [
        jnp.where(row8 == 6, f0, jnp.where(row8 == 7, f2, s))
        for f0, f2, s in zip((0.0, *flow0), (0.0, *flow2), skew)
    ]
    for form, target in ((excess, qn), (exponent, qa), (linear, ql)):
        target[...] = jnp.dot(
            spread(form, elems), basis[:, pl.ds(0, target.shape[1])], preferred_element_type=f32
        )
    nus[...] = jnp.concatenate([nu, jnp.zeros((LANE - SUB, elems), f32)], axis=0).T

    B0, B2, V = EDGE[0], EDGE[2], INVERSE

    def group(g, _):
        row = pl.multiple_of(g * SUB, SUB)
        for m in range(3):
            fetch_rows(tbl, stage, m * SUB * PITCH, lambda i: src[m, row + i], PITCH)
        nu_cols = [jnp.broadcast_to(nus[pl.ds(row, SUB), n : n + 1], (SUB, LANE)) for n in range(MODES)]
        for c in range(chunks):
            lanes = pl.ds(c * LANE, LANE)
            z = [z_ref[j, pl.ds(row, SUB), lanes] for j in range(MODES)]
            z0, z1, z2, z3, z4, z5 = z

            def beside(m, level):
                return stage[pl.ds(m * SUB * PITCH + level * 4 + c, SUB, stride=PITCH), :]

            def form(ref, n):
                return ref[pl.ds(row, SUB), pl.ds(n * vel + c * LANE, LANE)]

            a0, even, odd, last = edge_parts(z)
            gs = form(ql, 6)
            gr = form(ql, 7)
            g1 = -(gs + gr)
            out0 = gs < 0.0
            out1 = g1 < 0.0
            out2 = gr < 0.0
            V0 = [gs * jnp.where(out0, even[i] - odd[i], beside(0, i)) for i in range(3)]
            W0 = [
                g1 * jnp.where(out1, even[0] + odd[0], beside(1, 0)),
                g1 * jnp.where(out1, even[1] + odd[1], -beside(1, 1)),
                g1 * jnp.where(out1, even[2] + odd[2], beside(1, 2)),
            ]
            X = [gr * jnp.where(out2, last[i], beside(2, i)) for i in range(3)]
            S = [a + b for a, b in zip(V0, W0)]
            D = [b - a for a, b in zip(V0, W0)]

            h = gr + 2.0 * gs
            vol1 = (gr * z0) * k(KR[1, 0])
            vol2 = (h * z0) * k(KR[2, 0])
            vol3 = gr * (z0 * k(KR[3, 0]) + z1 * k(KR[3, 1]))
            vol4 = h * (z0 * k(KR[4, 0]) + z1 * k(KR[4, 1])) + gr * (z2 * k(KR[4, 2]))
            vol5 = gr * (z0 * k(KR[5, 0]) + z1 * k(KR[5, 1])) + h * (z2 * k(KR[5, 2]))

            N = NODAL
            e02 = last[0] + z5 * k(N[0, 5])
            o02 = z2 * k(N[2, 2]) + z4 * k(N[2, 4])
            e34 = a0 + z1 * k(N[3, 1]) + z3 * k(N[3, 3]) + z5 * k(N[3, 5])
            o34 = z2 * k(N[4, 2]) + z4 * k(N[4, 4])
            F = [
                e02 - o02,
                a0 + z1 * k(N[1, 1]) + z3 * k(N[1, 3]),
                e02 + o02,
                e34 - o34,
                e34 + o34,
                last[0] + z5 * k(N[5, 5]),
            ]
            H = []
            for n in range(MODES):
                skewed = jnp.minimum(
                    jnp.maximum(form(ql, n) * form(qn, n), -skew_multiplier_limit), skew_multiplier_limit
                )
                H.append(jnp.exp(form(qa, n)) * (1.0 + skewed) - nu_cols[n] * F[n])
            s02 = H[0] + H[2]
            d20 = H[2] - H[0]
            s34 = H[3] + H[4]
            d43 = H[4] - H[3]
            col0 = (s34 + H[5]) * k(V[0, 3])
            col1 = s02 * k(V[1, 0]) + H[1] * k(V[1, 1]) + s34 * k(V[1, 3]) + H[5] * k(V[1, 5])
            col2 = d20 * k(V[2, 2]) + d43 * k(V[2, 4])
            col3 = (s02 + H[5]) * k(V[3, 0]) + (H[1] - s34) * k(V[3, 1])
            col4 = d20 * k(V[4, 2]) + d43 * k(V[4, 4])
            col5 = s02 * k(V[5, 0]) + H[5] * k(V[5, 5])

            new = [
                z0 + (S[0] + X[0]) * k(B0[0, 0]) + col0,
                z1 + S[0] * k(B0[0, 1]) + S[1] * k(B0[1, 1]) + X[0] * k(B2[0, 1]) + vol1 + col1,
                z2 + D[0] * k(-B0[0, 2]) + D[1] * k(-B0[1, 2]) + X[1] * k(B2[1, 2]) + vol2 + col2,
                z3
                + S[0] * k(B0[0, 3])
                + S[1] * k(B0[1, 3])
                + S[2] * k(B0[2, 3])
                + X[0] * k(B2[0, 3])
                + vol3
                + col3,
                z4
                + D[0] * k(-B0[0, 4])
                + D[1] * k(-B0[1, 4])
                + D[2] * k(-B0[2, 4])
                + X[1] * k(B2[1, 4])
                + vol4
                + col4,
                z5
                + S[0] * k(B0[0, 5])
                + S[1] * k(B0[1, 5])
                + S[2] * k(B0[2, 5])
                + X[2] * k(B2[2, 5])
                + vol5
                + col5,
            ]
            for j in range(MODES):
                value = new[j]
                if section == 1:
                    value = 0.5 * (base_ref[j, pl.ds(row, SUB), lanes] + value)
                out[j, pl.ds(row, SUB), lanes] = value
                if j == 0:
                    mtbl[pl.ds(row * SUB + c, SUB, stride=SUB), :] = value
        return 0

    lax.fori_loop(0, elems // SUB, group, 0)

    for side, target in enumerate((mlow, mup)):

        def pack(g, _, side=side, target=target):
            row = pl.multiple_of(g * SUB, SUB)
            fetch_rows(
                mtbl, stage, 0, lambda i: jnp.maximum(lists[side, row + i], 0) % elems, SUB
            )
            for c in range(chunks):
                target[pl.ds(row, SUB), pl.ds(c * LANE, LANE)] = stage[pl.ds(c, SUB, stride=SUB), :]
            return 0

        lax.fori_loop(0, slots // SUB, pack, 0)


def limit_kernel(src, lists, first, z_ref, mlow, mup, out, *refs, section):
    if section == 0:
        mom, low, up, mtbl, stage, tbl = refs
    else:
        mtbl, stage = refs
    elems, vel = z_ref.shape[1:]
    chunks = vel // LANE
    slots = lists.shape[1]
    faces = 3 * elems

    def fill(g, _):
        row = pl.multiple_of(g * SUB, SUB)
        for c in range(chunks):
            mtbl[pl.ds(row * SUB + c, SUB, stride=SUB), :] = z_ref[
                0, pl.ds(row, SUB), pl.ds(c * LANE, LANE)
            ]
        return 0

    lax.fori_loop(0, elems // SUB, fill, 0)

    def fill_border(g, _):
        row = pl.multiple_of(g * SUB, SUB)
        for side, halo in enumerate((mlow, mup)):
            for c in range(chunks):
                start = (elems + side * slots + row) * SUB + c
                mtbl[pl.ds(start, SUB, stride=SUB), :] = tile(halo, row, c)
        return 0

    lax.fori_loop(0, slots // SUB, fill_border, 0)

    def source(value):
        return jnp.where(value < faces, value % elems, value - 2 * elems)

    def group(g, _):
        row = pl.multiple_of(g * SUB, SUB)
        for m in range(3):
            fetch_rows(mtbl, stage, m * SUB * SUB, lambda i: source(src[m, row + i]), SUB)
        for c in range(chunks):
            lanes = pl.ds(c * LANE, LANE)
            z = [z_ref[j, pl.ds(row, SUB), lanes] for j in range(MODES)]
            gaps = [
                jnp.abs(stage[pl.ds(m * SUB * SUB + c, SUB, stride=SUB), :] - z[0]) for m in range(3)
            ]
            bound = k(math.sqrt(2.0)) * jnp.maximum(jnp.maximum(gaps[0], gaps[1]), gaps[2])
            size1 = jnp.abs(z[1])
            size2 = jnp.abs(z[2])
            size4 = jnp.abs(z[4])
            linear = None
            quadric = None
            for m, q in ((0, 0), (0, 1), (0, 2), (2, 0), (2, 1)):
                t = TR[m, q]
                if q != 1:
                    value = size1 * k(abs(t[1])) + size2 * k(abs(t[2]))
                    linear = value if linear is None else jnp.maximum(linear, value)
                value = jnp.abs(z[3] * k(t[3]) + z[5] * k(t[5]))
                if abs(t[4]) > 1e-9:
                    value = value + size4 * k(abs(t[4]))
                quadric = value if quadric is None else jnp.maximum(quadric, value)
            theta1 = jnp.minimum(1.0, bound / jnp.maximum(linear, slope_floor))
            theta2 = jnp.minimum(theta1, bound / jnp.maximum(quadric, slope_floor))
            z = [z[0], z[1] * theta1, z[2] * theta1, z[3] * theta2, z[4] * theta2, z[5] * theta2]
            for j in range(MODES):
                out[j, pl.ds(row, SUB), lanes] = z[j]
            if section == 0:
                put_table(tbl, z, row, elems, c)
        return 0

    lax.fori_loop(0, elems // SUB, group, 0)
    if section == 0:
        pack_faces(tbl, stage, lists, (low, up), slots)
        put_moments(first[0], lambda j: out[j], mom)


def passed_along(value, axis, by):
    peers = lax.axis_size(axis)
    pairs = [(i, i + by) for i in range(peers) if 0 <= i + by < peers]
    return lax.ppermute(value, axis, pairs)


def swapped(value, bits):
    peers = lax.axis_size("vel")
    return lax.ppermute(value, "vel", [(i, i ^ bits) for i in range(peers)])


def moment_parts(partial):
    paired = partial + swapped(partial, 1)
    return [paired, swapped(paired, 2), swapped(paired, 4), swapped(paired, 6)]


def on_device(distribution, corners, neighbour, boundary_faces, collision_rate):
    modes, elems, vel = distribution.shape
    slots = boundary_faces.shape[2]
    lists = boundary_faces[0]
    first = (lax.axis_index("vel") * vel).astype(jnp.int32).reshape(1)
    rows = 3 * elems + 2 * slots
    S = jax.ShapeDtypeStruct
    state = S((modes, elems, vel), f32)
    halo = S((3, slots, vel), f32)
    means = S((slots, vel), f32)
    mom = S((modes * SUB, elems), f32)
    smem = pl.BlockSpec(memory_space=pltpu.SMEM)
    vmem = pl.BlockSpec(memory_space=pltpu.VMEM)
    params = pltpu.CompilerParams(vmem_limit_bytes=58 << 20)

    def table(count, pitch):
        return pltpu.VMEM((count * pitch, LANE), f32)

    stage = pltpu.VMEM((3 * SUB * PITCH, LANE), f32)

    mom1, low1, up1, src = pl.pallas_call(
        open_kernel,
        out_shape=(mom, halo, halo, S(neighbour.shape, jnp.int32)),
        in_specs=[smem, smem, vmem, vmem],
        out_specs=(vmem,) * 4,
        scratch_shapes=[table(3 * elems, PITCH), stage],
        compiler_params=params,
        name="open",
    )(lists, first, distribution, neighbour)

    rate = collision_rate.reshape(1, elems)
    flat_corners = corners.reshape(6, elems)

    def update(section, current, low, up, partial):
        from_lower = passed_along(up, "space", 1)
        from_upper = passed_along(low, "space", -1)
        arrays = [distribution] if section else []
        arrays += [current, from_lower, from_upper, *moment_parts(partial), rate, flat_corners]
        out, mlow, mup = pl.pallas_call(
            lambda *refs: update_kernel(*refs, section=section),
            out_shape=(state, means, means),
            in_specs=[smem, smem, smem] + [vmem] * len(arrays),
            out_specs=(vmem,) * 3,
            scratch_shapes=[
                table(rows, PITCH),
                stage,
                table(elems, SUB),
                pltpu.VMEM((TERMS * SUB, SUB * vel), bf16),
                pltpu.VMEM((elems, MODES * vel), f32),
                pltpu.VMEM((elems, MODES * vel), f32),
                pltpu.VMEM((elems, SUB * vel), f32),
                pltpu.VMEM((elems, LANE), f32),
            ],
            compiler_params=params,
            name=f"update{section}",
        )(src, lists, first, *arrays)
        return out, passed_along(mup, "space", 1), passed_along(mlow, "space", -1)

    def limit(section, updated, from_lower, from_upper):
        shapes = (state, mom, halo, halo) if section == 0 else (state,)
        scratch = [table(elems + 2 * slots, SUB), stage]
        if section == 0:
            scratch.append(table(3 * elems, PITCH))
        return pl.pallas_call(
            lambda *refs: limit_kernel(*refs, section=section),
            out_shape=shapes,
            in_specs=[smem, smem, smem] + [vmem] * 3,
            out_specs=(vmem,) * len(shapes),
            scratch_shapes=scratch,
            compiler_params=params,
            name=f"limit{section}",
        )(src, lists, first, updated, from_lower, from_upper)

    section, mom2, low2, up2 = limit(0, *update(0, distribution, low1, up1, mom1))
    (advanced,) = limit(1, *update(1, section, low2, up2, mom2))
    return advanced


def solution(mesh):
    in_specs = (
        P(None, "space", "vel"),
        P(None, None, "space"),
        P(None, "space"),
        P("space", None, None),
        P("space"),
    )
    return jax.shard_map(
        on_device, mesh=mesh, in_specs=in_specs, out_specs=P(None, "space", "vel"), check_vma=False
    )
```

profile of v0, /device:TPU:1, one launch (start us, length us, event | category | flops | bytes accessed | tf_op | source)
XLA Modules:
  0.0 118.6 jit_solution(5762822874474722023)
XLA Ops:
  0.0 7.1 %open.1 = (f32[48,256]{1,0:T(8,128)}, f32[3,80,512]{2,1,0:T(8,128)}, f32[3,80,512]{2,1,0:T(8,128)}, s32[3,256]{1,0:T(4,128)}) custom-call(s32[2,80]{1,0:T(2,128)} %bitcast.3, s32[1]{0:T(128)} %bitcast.1.first.refs_2_, f32[6,256,512]{2,1,0:T(8,128)} %refs_3_.3, s32[3,256]{1,0:T(4,128)} %neigh_ref.1), custom_call_target="tpu_custom_call" | custom-call | tf_op jit(solution)/shard_map/open/pallas_call | solution.py:596
  7.2 4.5 %collective-permute-start = (f32[3,80,512]{2,1,0:T(8,128)}, f32[3,80,512]{2,1,0:T(8,128)S(1)}, u32[]{:S(2)}, u32[]{:S(2)}) collective-permute-start(f32[3,80,512]{2,1,0:T(8,128)} %get-tuple-element.20), channel_id=1, source_target_pairs={{0,8},{8,16},{16,24},{1,9},{9,17},{17,25},{2,10},{10,18},{18,26},{... | collective-permute-start | bytes 1474568 | tf_op jit(solution)/shard_map/ppermute | solution.py:563
  11.7 1.9 %collective-permute-start.1 = (f32[3,80,512]{2,1,0:T(8,128)}, f32[3,80,512]{2,1,0:T(8,128)S(1)}, u32[]{:S(2)}, u32[]{:S(2)}) collective-permute-start(f32[3,80,512]{2,1,0:T(8,128)} %get-tuple-element.21), channel_id=1, source_target_pairs={{8,0},{16,8},{24,16},{9,1},{17,9},{25,17},{10,2},{18,10},{26,18},{... | collective-permute-start | bytes 1474568 | tf_op jit(solution)/shard_map/ppermute | solution.py:563
  13.6 1.3 %collective-permute-start.2 = (f32[48,256]{1,0:T(8,128)}, f32[48,256]{1,0:T(8,128)S(1)}, u32[]{:S(2)}, u32[]{:S(2)}) collective-permute-start(f32[48,256]{1,0:T(8,128)} %get-tuple-element.22), channel_id=1, source_target_pairs={{0,1},{1,0},{2,3},{3,2},{4,5},{5,4},{6,7},{7,6},{8,9},{9,8},{10,11... | collective-permute-start | bytes 147464 | tf_op jit(solution)/shard_map/ppermute | solution.py:568
  14.9 1.9 %collective-permute-done.2 = f32[48,256]{1,0:T(8,128)S(1)} collective-permute-done((f32[48,256]{1,0:T(8,128)}, f32[48,256]{1,0:T(8,128)S(1)}, u32[]{:S(2)}, u32[]{:S(2)}) %collective-permute-start.2) | collective-permute-done | bytes 49184 | tf_op jit(solution)/shard_map/ppermute | solution.py:568
  16.8 0.8 add.6.refs_6_
  17.6 3.4 %collective-permute-start.5 = (f32[48,256]{1,0:T(8,128)S(1)}, f32[48,256]{1,0:T(8,128)S(1)}, u32[]{:S(2)}, u32[]{:S(2)}) collective-permute-start(f32[48,256]{1,0:T(8,128)S(1)} %add.6.refs_6_), channel_id=1, source_target_pairs={{0,6},{1,7},{2,4},{3,5},{4,2},{5,3},{6,0},{7,1},{8,14},{9,15},{10,... | collective-permute-start | bytes 147464 | tf_op jit(solution)/shard_map/ppermute | solution.py:568
  21.0 0.0 collective-permute-start.4
  21.0 0.4 collective-permute-start.3
  21.4 0.6 reshape.11.refs_11_.refs_12_
  22.0 0.6 collective-permute-done.5.refs_9_
  22.6 3.1 %collective-permute-done.4.refs_8_ = f32[48,256]{1,0:T(8,128)S(1)} collective-permute-done((f32[48,256]{1,0:T(8,128)S(1)}, f32[48,256]{1,0:T(8,128)S(1)}, u32[]{:S(2)}, u32[]{:S(2)}) %collective-permute-start.4) | collective-permute-done | bytes 49184 | tf_op jit(solution)/shard_map/ppermute | solution.py:568
  25.8 0.1 collective-permute-done.3.refs_7_
  25.8 0.0 collective-permute-done.refs_4_
  25.8 0.0 collective-permute-done.1.refs_5_
  25.9 0.5 copy-done.12
  26.4 0.1 copy-done.14
  26.5 0.2 copy-done
  26.6 0.2 copy-done.2
  26.8 14.4 %update0.1 = (f32[6,256,512]{2,1,0:T(8,128)}, f32[80,512]{1,0:T(8,128)}, f32[80,512]{1,0:T(8,128)}) custom-call(s32[3,256]{1,0:T(4,128)} %get-tuple-element.19.refs_0_, s32[2,80]{1,0:T(2,128)} %bitcast.4, s32[1]{0:T(128)} %bitcast.1.first.refs_2_, f32[6,256,512]{2,1,0:T(8,128)} %refs_3_.3, f32[3,80,512]{2,1,0:T(8,128)} %copy-done, f32[3,80,512]{2,1,0:T(8,128)} %copy-done.2, ...), custom_call_target="tpu_custom_call" | custom-call | tf_op jit(solution)/shard_map/update0/pallas_call | solution.py:614
  41.3 5.3 %collective-permute-start.6 = (f32[80,512]{1,0:T(8,128)}, f32[80,512]{1,0:T(8,128)S(1)}, u32[]{:S(2)}, u32[]{:S(2)}) collective-permute-start(f32[80,512]{1,0:T(8,128)} %get-tuple-element.24), channel_id=1, source_target_pairs={{0,8},{8,16},{16,24},{1,9},{9,17},{17,25},{2,10},{10,18},{18,26},{... | collective-permute-start | bytes 491528 | tf_op jit(solution)/shard_map/ppermute | solution.py:563
  46.5 1.9 %collective-permute-start.7 = (f32[80,512]{1,0:T(8,128)}, f32[80,512]{1,0:T(8,128)S(1)}, u32[]{:S(2)}, u32[]{:S(2)}) collective-permute-start(f32[80,512]{1,0:T(8,128)} %get-tuple-element.25), channel_id=1, source_target_pairs={{8,0},{16,8},{24,16},{9,1},{17,9},{25,17},{10,2},{18,10},{26,18},{... | collective-permute-start | bytes 491528 | tf_op jit(solution)/shard_map/ppermute | solution.py:563
  48.4 0.6 collective-permute-done.6.refs_4_
  49.1 4.3 %collective-permute-done.7.refs_5_ = f32[80,512]{1,0:T(8,128)S(1)} collective-permute-done((f32[80,512]{1,0:T(8,128)}, f32[80,512]{1,0:T(8,128)S(1)}, u32[]{:S(2)}, u32[]{:S(2)}) %collective-permute-start.7) | collective-permute-done | bytes 163872 | tf_op jit(solution)/shard_map/ppermute | solution.py:563
  53.4 0.7 copy-done.8
  54.0 11.8 %limit0.1 = (f32[6,256,512]{2,1,0:T(8,128)}, f32[48,256]{1,0:T(8,128)}, f32[3,80,512]{2,1,0:T(8,128)}, f32[3,80,512]{2,1,0:T(8,128)}) custom-call(s32[3,256]{1,0:T(4,128)} %get-tuple-element.19.refs_0_, s32[2,80]{1,0:T(2,128)} %bitcast.5, s32[1]{0:T(128)} %bitcast.1.first.refs_2_, f32[6,256,512]{2,1,0:T(8,128)} %get-tuple-element.23.refs_3_, ...), custom_call_target="tpu_custom_call" | custom-call | tf_op jit(solution)/shard_map/limit0/pallas_call | solution.py:639
  65.9 1.9 %collective-permute-start.8 = (f32[3,80,512]{2,1,0:T(8,128)}, f32[3,80,512]{2,1,0:T(8,128)S(1)}, u32[]{:S(2)}, u32[]{:S(2)}) collective-permute-start(f32[3,80,512]{2,1,0:T(8,128)} %get-tuple-element.27), channel_id=1, source_target_pairs={{0,8},{8,16},{16,24},{1,9},{9,17},{17,25},{2,10},{10,18},{18,26},{... | collective-permute-start | bytes 1474568 | tf_op jit(solution)/shard_map/ppermute | solution.py:563
  67.8 2.4 %collective-permute-start.9 = (f32[3,80,512]{2,1,0:T(8,128)}, f32[3,80,512]{2,1,0:T(8,128)S(1)}, u32[]{:S(2)}, u32[]{:S(2)}) collective-permute-start(f32[3,80,512]{2,1,0:T(8,128)} %get-tuple-element.28), channel_id=1, source_target_pairs={{8,0},{16,8},{24,16},{9,1},{17,9},{25,17},{10,2},{18,10},{26,18},{... | collective-permute-start | bytes 1474568 | tf_op jit(solution)/shard_map/ppermute | solution.py:563
  70.2 1.3 %collective-permute-start.10 = (f32[48,256]{1,0:T(8,128)}, f32[48,256]{1,0:T(8,128)S(1)}, u32[]{:S(2)}, u32[]{:S(2)}) collective-permute-start(f32[48,256]{1,0:T(8,128)} %get-tuple-element.29), channel_id=1, source_target_pairs={{0,1},{1,0},{2,3},{3,2},{4,5},{5,4},{6,7},{7,6},{8,9},{9,8},{10,11... | collective-permute-start | bytes 147464 | tf_op jit(solution)/shard_map/ppermute | solution.py:568
  71.5 2.5 %collective-permute-done.10 = f32[48,256]{1,0:T(8,128)S(1)} collective-permute-done((f32[48,256]{1,0:T(8,128)}, f32[48,256]{1,0:T(8,128)S(1)}, u32[]{:S(2)}, u32[]{:S(2)}) %collective-permute-start.10) | collective-permute-done | bytes 49184 | tf_op jit(solution)/shard_map/ppermute | solution.py:568
  74.0 0.8 add.7.refs_7_
  74.8 1.2 %collective-permute-start.13 = (f32[48,256]{1,0:T(8,128)S(1)}, f32[48,256]{1,0:T(8,128)S(1)}, u32[]{:S(2)}, u32[]{:S(2)}) collective-permute-start(f32[48,256]{1,0:T(8,128)S(1)} %add.7.refs_7_), channel_id=1, source_target_pairs={{0,6},{1,7},{2,4},{3,5},{4,2},{5,3},{6,0},{7,1},{8,14},{9,15},{10,... | collective-permute-start | bytes 147464 | tf_op jit(solution)/shard_map/ppermute | solution.py:568
  76.0 0.6 collective-permute-start.12
  76.6 1.7 %collective-permute-start.11 = (f32[48,256]{1,0:T(8,128)S(1)}, f32[48,256]{1,0:T(8,128)S(1)}, u32[]{:S(2)}, u32[]{:S(2)}) collective-permute-start(f32[48,256]{1,0:T(8,128)S(1)} %add.7.refs_7_), channel_id=1, source_target_pairs={{0,2},{1,3},{2,0},{3,1},{4,6},{5,7},{6,4},{7,5},{8,10},{9,11},{10,... | collective-permute-start | bytes 147464 | tf_op jit(solution)/shard_map/ppermute | solution.py:568
  78.4 1.2 %collective-permute-done.13.refs_10_ = f32[48,256]{1,0:T(8,128)S(1)} collective-permute-done((f32[48,256]{1,0:T(8,128)S(1)}, f32[48,256]{1,0:T(8,128)S(1)}, u32[]{:S(2)}, u32[]{:S(2)}) %collective-permute-start.13) | collective-permute-done | bytes 49184 | tf_op jit(solution)/shard_map/ppermute | solution.py:568
  79.6 2.4 %collective-permute-done.12.refs_9_ = f32[48,256]{1,0:T(8,128)S(1)} collective-permute-done((f32[48,256]{1,0:T(8,128)S(1)}, f32[48,256]{1,0:T(8,128)S(1)}, u32[]{:S(2)}, u32[]{:S(2)}) %collective-permute-start.12) | collective-permute-done | bytes 49184 | tf_op jit(solution)/shard_map/ppermute | solution.py:568
  82.0 0.0 copy-start.1
  82.1 0.6 copy-done.13
  82.6 0.0 copy-done.15
  82.6 0.2 copy-done.1
  82.8 0.2 copy-done.3
  83.0 15.6 %update1.1 = (f32[6,256,512]{2,1,0:T(8,128)}, f32[80,512]{1,0:T(8,128)}, f32[80,512]{1,0:T(8,128)}) custom-call(s32[3,256]{1,0:T(4,128)} %get-tuple-element.19.refs_0_, s32[2,80]{1,0:T(2,128)} %bitcast.6, s32[1]{0:T(128)} %bitcast.1.first.refs_2_, f32[6,256,512]{2,1,0:T(8,128)} %refs_3_.3, f32[6,256,512]{2,1,0:T(8,128)} %get-tuple-element.26.refs_4_, ...), custom_call_target="tpu_custom_call" | custom-call | tf_op jit(solution)/shard_map/update1/pallas_call | solution.py:614
  98.6 3.5 %collective-permute-start.14 = (f32[80,512]{1,0:T(8,128)}, f32[80,512]{1,0:T(8,128)S(1)}, u32[]{:S(2)}, u32[]{:S(2)}) collective-permute-start(f32[80,512]{1,0:T(8,128)} %get-tuple-element.31), channel_id=1, source_target_pairs={{0,8},{8,16},{16,24},{1,9},{9,17},{17,25},{2,10},{10,18},{18,26},{... | collective-permute-start | bytes 491528 | tf_op jit(solution)/shard_map/ppermute | solution.py:563
  102.1 1.9 %collective-permute-start.15 = (f32[80,512]{1,0:T(8,128)}, f32[80,512]{1,0:T(8,128)S(1)}, u32[]{:S(2)}, u32[]{:S(2)}) collective-permute-start(f32[80,512]{1,0:T(8,128)} %get-tuple-element.32), channel_id=1, source_target_pairs={{8,0},{16,8},{24,16},{9,1},{17,9},{25,17},{10,2},{18,10},{26,18},{... | collective-permute-start | bytes 491528 | tf_op jit(solution)/shard_map/ppermute | solution.py:563
  104.0 0.6 collective-permute-done.14.refs_4_
  104.7 4.3 %collective-permute-done.15.refs_5_ = f32[80,512]{1,0:T(8,128)S(1)} collective-permute-done((f32[80,512]{1,0:T(8,128)}, f32[80,512]{1,0:T(8,128)S(1)}, u32[]{:S(2)}, u32[]{:S(2)}) %collective-permute-start.15) | collective-permute-done | bytes 163872 | tf_op jit(solution)/shard_map/ppermute | solution.py:563
  108.9 0.7 copy-done.9
  109.6 9.0 %limit1.1 = f32[6,256,512]{2,1,0:T(8,128)} custom-call(s32[3,256]{1,0:T(4,128)} %get-tuple-element.19.refs_0_, s32[2,80]{1,0:T(2,128)} %bitcast.7, s32[1]{0:T(128)} %bitcast.1.first.refs_2_, f32[6,256,512]{2,1,0:T(8,128)} %get-tuple-element.30.refs_3_, f32[80,512]{1,0:T(8,128)} %copy-done.7, f32[80,512]{1,0:T(8,128)} %copy-done.9), custom_call_target="tpu_custom_call" | custom-call | tf_op jit(solution)/shard_map/limit1/pallas_call | solution.py:639
  (27 shorter events, 0.1 us)
Async XLA Ops:
  0.0 21.4 %copy-start.16 = (f32[2,3,256]{2,0,1:T(2,128)S(1)}, f32[2,3,256]{2,0,1:T(2,128)}, u32[]{:S(2)}) copy-start(f32[2,3,256]{2,0,1:T(2,128)} %param.6) | copy-start | bytes 18436
  7.2 18.7 %collective-permute-start = (f32[3,80,512]{2,1,0:T(8,128)}, f32[3,80,512]{2,1,0:T(8,128)S(1)}, u32[]{:S(2)}, u32[]{:S(2)}) collective-permute-start(f32[3,80,512]{2,1,0:T(8,128)} %get-tuple-element.20), channel_id=1, source_target_pairs={{0,8},{8,16},{16,24},{1,9},{9,17},{17,25},{2,10},{10,18},{18,26},{... | collective-permute-start | bytes 1474568 | tf_op jit(solution)/shard_map/ppermute | solution.py:563
  11.7 14.2 %collective-permute-start.1 = (f32[3,80,512]{2,1,0:T(8,128)}, f32[3,80,512]{2,1,0:T(8,128)S(1)}, u32[]{:S(2)}, u32[]{:S(2)}) collective-permute-start(f32[3,80,512]{2,1,0:T(8,128)} %get-tuple-element.21), channel_id=1, source_target_pairs={{8,0},{16,8},{24,16},{9,1},{17,9},{25,17},{10,2},{18,10},{26,18},{... | collective-permute-start | bytes 1474568 | tf_op jit(solution)/shard_map/ppermute | solution.py:563
  13.6 3.2 %collective-permute-start.2 = (f32[48,256]{1,0:T(8,128)}, f32[48,256]{1,0:T(8,128)S(1)}, u32[]{:S(2)}, u32[]{:S(2)}) collective-permute-start(f32[48,256]{1,0:T(8,128)} %get-tuple-element.22), channel_id=1, source_target_pairs={{0,1},{1,0},{2,3},{3,2},{4,5},{5,4},{6,7},{7,6},{8,9},{9,8},{10,11... | collective-permute-start | bytes 147464 | tf_op jit(solution)/shard_map/ppermute | solution.py:568
  17.6 8.2 %copy-start.4 = (f32[48,256]{1,0:T(8,128)}, f32[48,256]{1,0:T(8,128)S(1)}, u32[]{:S(2)}) copy-start(f32[48,256]{1,0:T(8,128)S(1)} %add.6.refs_6_) | copy-start | bytes 147460
  17.6 5.0 %collective-permute-start.5 = (f32[48,256]{1,0:T(8,128)S(1)}, f32[48,256]{1,0:T(8,128)S(1)}, u32[]{:S(2)}, u32[]{:S(2)}) collective-permute-start(f32[48,256]{1,0:T(8,128)S(1)} %add.6.refs_6_), channel_id=1, source_target_pairs={{0,6},{1,7},{2,4},{3,5},{4,2},{5,3},{6,0},{7,1},{8,14},{9,15},{10,... | collective-permute-start | bytes 147464 | tf_op jit(solution)/shard_map/ppermute | solution.py:568
  21.0 4.7 %collective-permute-start.4 = (f32[48,256]{1,0:T(8,128)S(1)}, f32[48,256]{1,0:T(8,128)S(1)}, u32[]{:S(2)}, u32[]{:S(2)}) collective-permute-start(f32[48,256]{1,0:T(8,128)S(1)} %add.6.refs_6_), channel_id=1, source_target_pairs={{0,4},{1,5},{2,6},{3,7},{4,0},{5,1},{6,2},{7,3},{8,12},{9,13},{10,... | collective-permute-start | bytes 147464 | tf_op jit(solution)/shard_map/ppermute | solution.py:568
  21.0 4.8 %collective-permute-start.3 = (f32[48,256]{1,0:T(8,128)S(1)}, f32[48,256]{1,0:T(8,128)S(1)}, u32[]{:S(2)}, u32[]{:S(2)}) collective-permute-start(f32[48,256]{1,0:T(8,128)S(1)} %add.6.refs_6_), channel_id=1, source_target_pairs={{0,2},{1,3},{2,0},{3,1},{4,6},{5,7},{6,4},{7,5},{8,10},{9,11},{10,... | collective-permute-start | bytes 147464 | tf_op jit(solution)/shard_map/ppermute | solution.py:568
  22.6 3.2 %copy-start.10 = (f32[48,256]{1,0:T(8,128)}, f32[48,256]{1,0:T(8,128)S(1)}, u32[]{:S(2)}) copy-start(f32[48,256]{1,0:T(8,128)S(1)} %collective-permute-done.5.refs_9_) | copy-start | bytes 147460
  25.8 0.6 copy-start.12
  25.8 0.6 copy-start.14
  25.8 0.8 copy-start
  25.8 1.0 copy-start.2
  41.3 7.8 %collective-permute-start.6 = (f32[80,512]{1,0:T(8,128)}, f32[80,512]{1,0:T(8,128)S(1)}, u32[]{:S(2)}, u32[]{:S(2)}) collective-permute-start(f32[80,512]{1,0:T(8,128)} %get-tuple-element.24), channel_id=1, source_target_pairs={{0,8},{8,16},{16,24},{1,9},{9,17},{17,25},{2,10},{10,18},{18,26},{... | collective-permute-start | bytes 491528 | tf_op jit(solution)/shard_map/ppermute | solution.py:563
  46.5 6.8 %collective-permute-start.7 = (f32[80,512]{1,0:T(8,128)}, f32[80,512]{1,0:T(8,128)S(1)}, u32[]{:S(2)}, u32[]{:S(2)}) collective-permute-start(f32[80,512]{1,0:T(8,128)} %get-tuple-element.25), channel_id=1, source_target_pairs={{8,0},{16,8},{24,16},{9,1},{17,9},{25,17},{10,2},{18,10},{26,18},{... | collective-permute-start | bytes 491528 | tf_op jit(solution)/shard_map/ppermute | solution.py:563
  49.1 4.3 %copy-start.6 = (f32[80,512]{1,0:T(8,128)}, f32[80,512]{1,0:T(8,128)S(1)}, u32[]{:S(2)}) copy-start(f32[80,512]{1,0:T(8,128)S(1)} %collective-permute-done.6.refs_4_) | copy-start | bytes 491524
  53.4 0.7 copy-start.8
  65.9 16.1 %collective-permute-start.8 = (f32[3,80,512]{2,1,0:T(8,128)}, f32[3,80,512]{2,1,0:T(8,128)S(1)}, u32[]{:S(2)}, u32[]{:S(2)}) collective-permute-start(f32[3,80,512]{2,1,0:T(8,128)} %get-tuple-element.27), channel_id=1, source_target_pairs={{0,8},{8,16},{16,24},{1,9},{9,17},{17,25},{2,10},{10,18},{18,26},{... | collective-permute-start | bytes 1474568 | tf_op jit(solution)/shard_map/ppermute | solution.py:563
  67.8 14.2 %collective-permute-start.9 = (f32[3,80,512]{2,1,0:T(8,128)}, f32[3,80,512]{2,1,0:T(8,128)S(1)}, u32[]{:S(2)}, u32[]{:S(2)}) collective-permute-start(f32[3,80,512]{2,1,0:T(8,128)} %get-tuple-element.28), channel_id=1, source_target_pairs={{8,0},{16,8},{24,16},{9,1},{17,9},{25,17},{10,2},{18,10},{26,18},{... | collective-permute-start | bytes 1474568 | tf_op jit(solution)/shard_map/ppermute | solution.py:563
  70.2 3.7 %collective-permute-start.10 = (f32[48,256]{1,0:T(8,128)}, f32[48,256]{1,0:T(8,128)S(1)}, u32[]{:S(2)}, u32[]{:S(2)}) collective-permute-start(f32[48,256]{1,0:T(8,128)} %get-tuple-element.29), channel_id=1, source_target_pairs={{0,1},{1,0},{2,3},{3,2},{4,5},{5,4},{6,7},{7,6},{8,9},{9,8},{10,11... | collective-permute-start | bytes 147464 | tf_op jit(solution)/shard_map/ppermute | solution.py:568
  74.8 7.3 %copy-start.5 = (f32[48,256]{1,0:T(8,128)}, f32[48,256]{1,0:T(8,128)S(1)}, u32[]{:S(2)}) copy-start(f32[48,256]{1,0:T(8,128)S(1)} %add.7.refs_7_) | copy-start | bytes 147460
  74.8 4.9 %collective-permute-start.13 = (f32[48,256]{1,0:T(8,128)S(1)}, f32[48,256]{1,0:T(8,128)S(1)}, u32[]{:S(2)}, u32[]{:S(2)}) collective-permute-start(f32[48,256]{1,0:T(8,128)S(1)} %add.7.refs_7_), channel_id=1, source_target_pairs={{0,6},{1,7},{2,4},{3,5},{4,2},{5,3},{6,0},{7,1},{8,14},{9,15},{10,... | collective-permute-start | bytes 147464 | tf_op jit(solution)/shard_map/ppermute | solution.py:568
  76.0 6.0 %collective-permute-start.12 = (f32[48,256]{1,0:T(8,128)S(1)}, f32[48,256]{1,0:T(8,128)S(1)}, u32[]{:S(2)}, u32[]{:S(2)}) collective-permute-start(f32[48,256]{1,0:T(8,128)S(1)} %add.7.refs_7_), channel_id=1, source_target_pairs={{0,4},{1,5},{2,6},{3,7},{4,0},{5,1},{6,2},{7,3},{8,12},{9,13},{10,... | collective-permute-start | bytes 147464 | tf_op jit(solution)/shard_map/ppermute | solution.py:568
  76.6 5.4 %collective-permute-start.11 = (f32[48,256]{1,0:T(8,128)S(1)}, f32[48,256]{1,0:T(8,128)S(1)}, u32[]{:S(2)}, u32[]{:S(2)}) collective-permute-start(f32[48,256]{1,0:T(8,128)S(1)} %add.7.refs_7_), channel_id=1, source_target_pairs={{0,2},{1,3},{2,0},{3,1},{4,6},{5,7},{6,4},{7,5},{8,10},{9,11},{10,... | collective-permute-start | bytes 147464 | tf_op jit(solution)/shard_map/ppermute | solution.py:568
  79.6 2.5 %copy-start.11 = (f32[48,256]{1,0:T(8,128)}, f32[48,256]{1,0:T(8,128)S(1)}, u32[]{:S(2)}) copy-start(f32[48,256]{1,0:T(8,128)S(1)} %collective-permute-done.13.refs_10_) | copy-start | bytes 147460
  82.0 0.6 copy-start.13
  82.0 0.6 copy-start.15
  82.0 0.8 copy-start.1
  82.1 0.9 copy-start.3
  98.6 6.1 %collective-permute-start.14 = (f32[80,512]{1,0:T(8,128)}, f32[80,512]{1,0:T(8,128)S(1)}, u32[]{:S(2)}, u32[]{:S(2)}) collective-permute-start(f32[80,512]{1,0:T(8,128)} %get-tuple-element.31), channel_id=1, source_target_pairs={{0,8},{8,16},{16,24},{1,9},{9,17},{17,25},{2,10},{10,18},{18,26},{... | collective-permute-start | bytes 491528 | tf_op jit(solution)/shard_map/ppermute | solution.py:563
  102.1 6.8 %collective-permute-start.15 = (f32[80,512]{1,0:T(8,128)}, f32[80,512]{1,0:T(8,128)S(1)}, u32[]{:S(2)}, u32[]{:S(2)}) collective-permute-start(f32[80,512]{1,0:T(8,128)} %get-tuple-element.32), channel_id=1, source_target_pairs={{8,0},{16,8},{24,16},{9,1},{17,9},{25,17},{10,2},{18,10},{26,18},{... | collective-permute-start | bytes 491528 | tf_op jit(solution)/shard_map/ppermute | solution.py:563
  104.7 4.3 %copy-start.7 = (f32[80,512]{1,0:T(8,128)}, f32[80,512]{1,0:T(8,128)S(1)}, u32[]{:S(2)}) copy-start(f32[80,512]{1,0:T(8,128)S(1)} %collective-permute-done.14.refs_4_) | copy-start | bytes 491524
  108.9 0.7 copy-start.9
where the time goes:
time: 119 us
  Pallas kernels  58 us (49%)
  starting transfers between devices  33.3 us (28%)
  waiting for transfers between devices  21.7 us (18%)
  local copies, waits for them, and re-layouts  3.84 us (3%)
  other arithmetic  1.61 us (1%)
    pallas_call x2, Pallas kernels, update(): pl.pallas_call(lambda *refs: update_kernel(*refs, section=section), out_s...  30 us
    ppermute x8, starting transfers between devices, passed_along(): return lax.ppermute(value, axis, pairs)  23.4 us
    pallas_call x2, Pallas kernels, limit(): pl.pallas_call(lambda *refs: limit_kernel(*refs, section=section), out_sh...  20.8 us
    ppermute x8, waiting for transfers between devices, swapped(): return lax.ppermute(value, 'vel', [(i, i ^ bits) for i in range(peers)])  11.9 us
    ppermute x8, starting transfers between devices, swapped(): return lax.ppermute(value, 'vel', [(i, i ^ bits) for i in range(peers)])  9.89 us
    ppermute x8, waiting for transfers between devices, passed_along(): return lax.ppermute(value, axis, pairs)  9.85 us
    pallas_call x1, Pallas kernels, on_device(): pl.pallas_call(open_kernel, out_shape=(mom, halo, halo, S(neighbour.shape...  7.15 us
    unnamed x35, local copies, waits for them, and re-layouts  3.24 us
  transfers between devices with their start and end apart: 16, of which 11 were waited for; matrix products, arithmetic and copies ran while one was open for 2% of the time, Pallas kernels for 0%

commit v1 on v0

v1 whole, which is shorter than its diff:
```python
import math

import jax
import jax.numpy as jnp
import numpy as np
from jax import lax
from jax.experimental import pallas as pl
from jax.experimental.pallas import tpu as pltpu
from jax.sharding import PartitionSpec as P

VGRID = 64
velocity_limit = 6.0
time_step = 0.012
viscous_conductive_ratio = 2.0 / 3.0
density_floor = 0.1
kelvin_lower_limit = 0.2
skew_multiplier_limit = 0.9
slope_floor = 0.01

LANE = 128
SUB = 8
MODES = 6
TERMS = 32
f32 = jnp.float32
bf16 = jnp.bfloat16


def monomial_integral(power_r, power_s):
    return math.factorial(power_r) * math.factorial(power_s) / math.factorial(power_r + power_s + 2)


def dg_tables():
    powers = [(0, 0), (1, 0), (0, 1), (2, 0), (1, 1), (0, 2)]
    gram = np.array(
        [[monomial_integral(a[0] + b[0], a[1] + b[1]) for b in powers] for a in powers]
    )
    coeffs = np.linalg.inv(np.linalg.cholesky(gram))
    deriv_r = np.zeros((6, 6))
    deriv_s = np.zeros((6, 6))
    for i, a in enumerate(powers):
        for j, b in enumerate(powers):
            if a[0] > 0:
                deriv_r[i, j] = a[0] * monomial_integral(a[0] - 1 + b[0], a[1] + b[1])
            if a[1] > 0:
                deriv_s[i, j] = a[1] * monomial_integral(a[0] + b[0], a[1] - 1 + b[1])
    stiff_r = coeffs @ deriv_r @ coeffs.T
    stiff_s = coeffs @ deriv_s @ coeffs.T

    def evaluate(location):
        return coeffs @ np.array([location[0] ** p[0] * location[1] ** p[1] for p in powers])

    vertices = np.array([[0.0, 0.0], [1.0, 0.0], [0.0, 1.0]])
    offset = math.sqrt(0.15)
    positions = np.array([0.5 - offset, 0.5, 0.5 + offset])
    weights = np.array([5.0, 8.0, 5.0]) / 18.0
    traces = np.zeros((3, 3, 6))
    for m in range(3):
        for q in range(3):
            along = positions[q]
            traces[m, q] = evaluate((1.0 - along) * vertices[m] + along * vertices[(m + 1) % 3])
    legendre = np.stack(
        [
            np.ones(3),
            math.sqrt(3.0) * (2.0 * positions - 1.0),
            math.sqrt(5.0) * (6.0 * positions**2 - 6.0 * positions + 1.0),
        ]
    )
    edge = np.einsum("lq,q,mqj->mlj", legendre, weights, traces)
    node_list = [(0.0, 0.0), (1.0, 0.0), (0.0, 1.0), (0.5, 0.0), (0.5, 0.5), (0.0, 0.5)]
    nodal = np.array([evaluate(np.array(n)) for n in node_list])
    inverse = np.linalg.inv(nodal)
    return stiff_r, stiff_s, traces, edge, nodal, inverse


KR, KS, TR, EDGE, NODAL, INVERSE = dg_tables()


def k(value):
    return float(np.float32(value))


def edge_parts(z):
    z0, z1, z2, z3, z4, z5 = z
    b = EDGE[0]
    a0 = z0 * k(b[0, 0])
    even = (
        a0 + z1 * k(b[0, 1]) + z3 * k(b[0, 3]) + z5 * k(b[0, 5]),
        z1 * k(b[1, 1]) + z3 * k(b[1, 3]) + z5 * k(b[1, 5]),
        z3 * k(b[2, 3]) + z5 * k(b[2, 5]),
    )
    odd = (
        z2 * k(-b[0, 2]) + z4 * k(-b[0, 4]),
        z2 * k(-b[1, 2]) + z4 * k(-b[1, 4]),
        z4 * k(-b[2, 4]),
    )
    c = EDGE[2]
    last = (
        a0 + z1 * k(c[0, 1]) + z3 * k(c[0, 3]),
        z2 * k(c[1, 2]) + z4 * k(c[1, 4]),
        z5 * k(c[2, 5]),
    )
    return even, odd, last


def level0(z):
    z0, z1, z2, z3, z4, z5 = z
    b, c = EDGE[0], EDGE[2]
    a0 = z0 * k(b[0, 0])
    even = a0 + z1 * k(b[0, 1]) + z3 * k(b[0, 3]) + z5 * k(b[0, 5])
    odd = z2 * k(-b[0, 2]) + z4 * k(-b[0, 4])
    return even - odd, even + odd, a0 + z1 * k(c[0, 1]) + z3 * k(c[0, 3])


def table_values(z):
    even, odd, last = edge_parts(z)
    return (
        (even[0] - odd[0], odd[1] - even[1], even[2] - odd[2]),
        (even[0] + odd[0], even[1] + odd[1], even[2] + odd[2]),
        (last[0], -last[1], last[2]),
    )


def at(row, chunk):
    return pl.ds(row, SUB), pl.ds(chunk * LANE, LANE)


def modes_at(ref, row, chunk):
    return [ref[(j, *at(row, chunk))] for j in range(ref.shape[0])]


def over_groups(count, body):
    def step(g, _):
        body(pl.multiple_of(g * SUB, SUB))
        return 0

    lax.fori_loop(0, count // SUB, step, 0)


def copy_rows(source, target, start, to, count):
    for piece in range(0, count, SUB):
        rows = min(SUB, count - piece)
        target[pl.ds(to + piece, rows), :] = source[pl.ds(start + piece, rows), :]


def pipelined_groups(count, stages, fetch, compute):
    last = count - SUB
    fetch(0, stages[0])

    def step(pair, _):
        row = pl.multiple_of(pair * (2 * SUB), 2 * SUB)
        after = pl.multiple_of(row + SUB, SUB)
        fetch(after, stages[1])
        compute(row, stages[0])
        fetch(pl.multiple_of(jnp.minimum(row + 2 * SUB, last), SUB), stages[0])
        compute(after, stages[1])
        return 0

    lax.fori_loop(0, count // (2 * SUB), step, 0)


def grid_rows(first, shape):
    index = first + lax.broadcasted_iota(jnp.int32, shape, len(shape) - 1)
    spacing = 2.0 * velocity_limit / VGRID
    x = -velocity_limit + ((index // VGRID).astype(f32) + 0.5) * spacing
    y = -velocity_limit + ((index % VGRID).astype(f32) + 0.5) * spacing
    return x, y, spacing


def split3(value):
    high = value.astype(bf16).astype(f32)
    rest = value - high
    middle = rest.astype(bf16).astype(f32)
    return high, middle, (rest - middle).astype(bf16).astype(f32)


def weight_rows(first, vel):
    x, y, spacing = grid_rows(first, (SUB, vel))
    row = lax.broadcasted_iota(jnp.int32, (SUB, vel), 0)
    square = x * x + y * y
    weights = jnp.ones_like(x)
    for index, value in enumerate((x, y, x * x, x * y, y * y, x * square, y * square)):
        weights = jnp.where(row == index + 1, value, weights)
    weights = weights * (spacing * spacing)
    return jnp.concatenate([*split3(weights), jnp.zeros_like(x)], axis=0).astype(bf16)


def mode_moments(weights, value):
    high = value.astype(bf16)
    low = (value - high.astype(f32)).astype(bf16)
    dims = (((1,), (1,)), ((), ()))
    total = lax.dot_general(weights, high, dims, preferred_element_type=f32)
    total = total + lax.dot_general(weights, low, dims, preferred_element_type=f32)
    return total[0:8] + total[8:16] + total[16:24]


def first_kernel(info, z_ref, mom):
    weights = weight_rows(info[0], z_ref.shape[2])
    for j in range(MODES):
        mom[pl.ds(j * SUB, SUB), :] = mode_moments(weights, z_ref[j])


def put_index(neigh_ref, rows_ref, lists, src, away, offsets, elems, chunks):
    slots = rows_ref.shape[1]
    faces = 3 * elems
    shape = neigh_ref.shape
    face = lax.broadcasted_iota(jnp.int32, shape, 0) * elems + lax.broadcasted_iota(jnp.int32, shape, 1)

    def mark(slot, found):
        found = jnp.where(face == lists[0, slot], faces + slot, found)
        return jnp.where(face == lists[1, slot], faces + slots + slot, found)

    found = jnp.maximum(lax.fori_loop(0, slots, mark, neigh_ref[...]), 0)
    src[...] = found * chunks
    away[...] = jnp.where(found < faces, found % elems, found - 2 * elems) * chunks
    known = jnp.maximum(rows_ref[...], 0)
    offsets[pl.ds(0, 2), :] = known * chunks
    offsets[pl.ds(2, 2), :] = known % elems * chunks


def put_flows(corner, cols):
    cx = [corner[i, 0:1, :] for i in range(3)]
    cy = [corner[i, 1:2, :] for i in range(3)]
    det = (cx[1] - cx[0]) * (cy[2] - cy[0]) - (cx[2] - cx[0]) * (cy[1] - cy[0])
    step = time_step / det
    rows = [-step * (cy[1] - cy[0]), step * (cx[1] - cx[0]), -step * (cy[0] - cy[2]), step * (cx[0] - cx[2])]
    cols[...] = jnp.concatenate([*rows, jnp.zeros((LANE - 4, cols.shape[0]), f32)], axis=0).T


def sides(info):
    parity = info[1]
    return (1 - parity, parity)


def prepare_kernel(lists, info, neigh_ref, rows_ref, corner, src, away, offsets, basis, cols):
    vel = basis.shape[1] // MODES
    put_index(neigh_ref, rows_ref, lists, src, away, offsets, cols.shape[0], vel // LANE)
    put_flows(corner, cols)
    put_basis(info[0], basis, vel)


def trace_kernel(offsets, info, z_ref, tbl0, tbl12, near, far, stage0, stage12):
    elems, vel = z_ref.shape[1:]
    chunks = vel // LANE
    slots = offsets.shape[1]

    def fill(row):
        for c in range(chunks):
            for m, values in enumerate(table_values(modes_at(z_ref, row, c))):
                start = (m * elems + row) * chunks + c
                tbl0[pl.ds(start, SUB, stride=chunks), :] = values[0]
                for level in (1, 2):
                    start = ((m * elems + row) * 2 + level - 1) * chunks + c
                    tbl12[pl.ds(start, SUB, stride=2 * chunks), :] = values[level]

    over_groups(elems, fill)

    def take(row):
        for place, side in enumerate(sides(info)):
            for i in range(SUB):
                start = offsets[side, row + i]
                to = (place * slots + row + i) * chunks
                copy_rows(tbl0, stage0, start, to, chunks)
                copy_rows(tbl12, stage12, 2 * start, 2 * to, 2 * chunks)

    over_groups(slots, take)

    def pack(row):
        for place, out in enumerate((near, far)):
            for c in range(chunks):
                start = (place * slots + row) * chunks
                out[(0, *at(row, c))] = stage0[pl.ds(start + c, SUB, stride=chunks), :]
                for level in range(2):
                    out[(level + 1, *at(row, c))] = stage12[
                        pl.ds(2 * start + level * chunks + c, SUB, stride=2 * chunks), :
                    ]

    over_groups(slots, pack)


def flow_forms(cols, grid, row):
    col = [jnp.broadcast_to(cols[pl.ds(row, SUB), n : n + 1], (SUB, LANE)) for n in range(4)]
    flows = []
    for x, y in grid:
        g0 = col[0] * x + col[1] * y
        g2 = col[2] * x + col[3] * y
        flows.append((g0, -(g0 + g2), g2))
    return flows


def chunk_grid(first, chunks):
    return [grid_rows(first + c * LANE, (1, LANE))[:2] for c in range(chunks)]


def put_basis(first, basis, vel):
    x, y, _ = grid_rows(first, (1, vel))
    xx = x * x
    yy = y * y
    xx_high = xx.astype(bf16).astype(f32)
    yy_high = yy.astype(bf16).astype(f32)
    monomials = (jnp.ones_like(x), x, y, xx_high, xx - xx_high, yy_high, yy - yy_high)
    row = lax.broadcasted_iota(jnp.int32, (SUB, vel), 0)
    zero = jnp.zeros((SUB, vel), f32)
    for n in range(MODES):
        mine = row == n
        for pair in range(TERMS // 2):
            halves = []
            for term in (2 * pair, 2 * pair + 1):
                which = term // 3
                halves.append(jnp.where(mine, monomials[which], 0.0) if which < len(monomials) else zero)
            basis[pl.ds(pair * 2 * SUB, 2 * SUB), pl.ds(n * vel, vel)] = jnp.concatenate(
                halves, axis=0
            ).astype(bf16)


def node_parameters(mom, rate, elems, scale):
    shape = (SUB, elems)
    row = lax.broadcasted_iota(jnp.int32, shape, 0)

    def column(values):
        out = jnp.full(shape, k(values[0]), f32)
        for n in range(1, MODES):
            out = jnp.where(row == n, k(values[n]), out)
        return out

    columns = [column(NODAL[:, j]) for j in range(MODES)]
    R = []
    for index in range(8):
        total = columns[0] * mom[index : index + 1, :]
        for j in range(1, MODES):
            total = total + columns[j] * mom[j * SUB + index : j * SUB + index + 1, :]
        R.append(total)
    zeroth, mass_x, mass_y, flux_xx, flux_xy, flux_yy, third_x, third_y = R
    density = jnp.maximum(zeroth, density_floor)
    ux = mass_x / density
    uy = mass_y / density
    drift_sq = ux * ux + uy * uy
    drift_mass = ux * mass_x + uy * mass_y
    trace = flux_xx + flux_yy
    kelvin = jnp.maximum(
        (trace - 2.0 * drift_mass + drift_sq * zeroth) / (2.0 * density), kelvin_lower_limit
    )
    qx = 0.5 * (
        third_x
        - 2.0 * (flux_xx * ux + flux_xy * uy)
        + mass_x * drift_sq
        - ux * trace
        + 2.0 * ux * drift_mass
        - ux * drift_sq * zeroth
    )
    qy = 0.5 * (
        third_y
        - 2.0 * (flux_xy * ux + flux_yy * uy)
        + mass_y * drift_sq
        - uy * trace
        + 2.0 * uy * drift_mass
        - uy * drift_sq * zeroth
    )
    nu = scale * rate * density
    over = 1.0 / kelvin
    weight = (1.0 - viscous_conductive_ratio) / (4.0 * density * kelvin * kelvin)
    qx = qx * weight
    qy = qy * weight
    excess = (over * drift_sq - 4.0, -2.0 * over * ux, -2.0 * over * uy, over, over)
    amplitude = jnp.log(nu * density * over * k(1.0 / (2.0 * math.pi)))
    exponent = (
        amplitude - 0.5 * over * drift_sq,
        over * ux,
        over * uy,
        -0.5 * over,
        -0.5 * over,
    )
    skew = (-(qx * ux + qy * uy), qx, qy)
    return nu, (excess, exponent, skew)


def spread(form, elems):
    pieces = []
    for index, value in enumerate(form):
        parts = split3(value)
        pieces += parts
        if index >= 3:
            pieces += parts
    pieces.append(jnp.zeros((TERMS * SUB - SUB * len(pieces), elems), f32))
    return jnp.concatenate(pieces, axis=0).T.astype(bf16)


def relaxed(forms, slot, row, chunk, vel, nu, inside):
    def form(i):
        return forms[i][pl.ds(row, SUB), pl.ds(slot * vel + chunk * LANE, LANE)]

    skewed = jnp.minimum(jnp.maximum(form(2) * form(0), -skew_multiplier_limit), skew_multiplier_limit)
    return jnp.exp(form(1)) * (1.0 + skewed) - nu * inside


def form_kernel(*refs, parts, section):
    mom_refs = refs[:parts]
    rate, basis, spreads, nus, *forms = refs[parts:]
    elems = rate.shape[1]
    half = basis.shape[1] // 2
    scale = time_step if section == 0 else 0.5 * time_step
    moments = mom_refs[0][...]
    for ref in mom_refs[1:]:
        moments = moments + ref[...]
    nu, coefficients = node_parameters(moments, rate[...], elems, scale)
    nus[...] = jnp.concatenate([nu, jnp.zeros((LANE - SUB, elems), f32)], axis=0).T
    for i, form in enumerate(coefficients):
        spreads[i] = spread(form, elems)
        forms[i][...] = jnp.dot(spreads[i], basis[:, pl.ds(half, half)], preferred_element_type=f32)


def mean_kernel(offsets, src, info, _, z_ref, near_in, far_in, cols, nus, *refs, section):
    forms = refs[:3]
    refs = refs[3:]
    base_ref = None
    if section == 1:
        base_ref = refs[0]
        refs = refs[1:]
    tbl, centre, high, near, far, mtbl, stage_a, stage_b, stage = refs
    elems, vel = z_ref.shape[1:]
    chunks = vel // LANE
    slots = offsets.shape[1]
    faces = 3 * elems

    def fill_border(row):
        for side, halo in zip(sides(info), (near_in, far_in)):
            for c in range(chunks):
                start = (faces + side * slots + row) * chunks + c
                tbl[pl.ds(start, SUB, stride=chunks), :] = halo[(0, *at(row, c))]

    over_groups(slots, fill_border)

    N, V = NODAL, INVERSE
    grid = chunk_grid(info[0], chunks)

    def fetch(row, stage):
        for m in range(3):
            for i in range(SUB):
                copy_rows(tbl, stage, src[m, row + i], (m * SUB + i) * chunks, chunks)

    def compute(row, stage):
        flows = flow_forms(cols, grid, row)
        nu_cols = [jnp.broadcast_to(nus[pl.ds(row, SUB), n : n + 1], (SUB, LANE)) for n in range(3, MODES)]
        for c in range(chunks):
            z0, z1, z2, z3, z4, z5 = modes_at(z_ref, row, c)
            own = level0((z0, z1, z2, z3, z4, z5))
            through = None
            for m in range(3):
                g = flows[c][m]
                value = g * jnp.where(
                    g < 0.0, own[m], stage[pl.ds(m * SUB * chunks + c, SUB, stride=chunks), :]
                )
                through = value if through is None else through + value
            moved = z0 + through * k(EDGE[0, 0, 0])
            if section == 1:
                moved = 0.5 * (base_ref[(0, *at(row, c))] + moved)
            a0 = z0 * k(N[0, 0])
            e34 = a0 + z1 * k(N[3, 1]) + z3 * k(N[3, 3]) + z5 * k(N[3, 5])
            o34 = z2 * k(N[4, 2]) + z4 * k(N[4, 4])
            inside = (
                e34 - o34,
                e34 + o34,
                a0 + z1 * k(N[5, 1]) + z3 * k(N[5, 3]) + z5 * k(N[5, 5]),
            )
            H = [relaxed(forms, n, row, c, vel, nu_cols[n], inside[n]) for n in range(3)]
            value = moved + (H[0] + H[1] + H[2]) * k(V[0, 3])
            centre[at(row, c)] = value
            mtbl[pl.ds(row * chunks + c, SUB, stride=chunks), :] = value
            for n in range(3):
                high[(n, *at(row, c))] = H[n]

    pipelined_groups(elems, (stage_a, stage_b), fetch, compute)

    def take(row):
        for place, side in enumerate(sides(info)):
            for i in range(SUB):
                copy_rows(mtbl, stage, offsets[2 + side, row + i], (place * slots + row + i) * chunks, chunks)

    over_groups(slots, take)

    def pack(row):
        for place, out in enumerate((near, far)):
            for c in range(chunks):
                start = (place * slots + row) * chunks + c
                out[at(row, c)] = stage[pl.ds(start, SUB, stride=chunks), :]

    over_groups(slots, pack)


def rest_kernel(src, info, tbl0, _, z_ref, near, far, high, spreads, nus, basis, cols, *refs, section):
    base_ref = None
    if section == 1:
        base_ref = refs[0]
        refs = refs[1:]
    tbl, out, sizes, stage_a, stage_b, *forms = refs
    elems, vel = z_ref.shape[1:]
    chunks = vel // LANE
    pitch = 3 * chunks
    slots = near.shape[1]
    faces = 3 * elems

    def fill_border(row):
        for side, halo in zip(sides(info), (near, far)):
            for level in range(2):
                for c in range(chunks):
                    start = ((faces + side * slots + row) * 2 + level) * chunks + c
                    tbl[pl.ds(start, SUB, stride=2 * chunks), :] = halo[(level + 1, *at(row, c))]

    over_groups(slots, fill_border)

    for i in range(3):
        forms[i][...] = jnp.dot(
            spreads[i], basis[:, pl.ds(0, 3 * vel)], preferred_element_type=f32
        )
    N, V, B0, B2 = NODAL, INVERSE, EDGE[0], EDGE[2]
    grid = chunk_grid(info[0], chunks)

    def fetch(row, stage):
        for m in range(3):
            for i in range(SUB):
                start = src[m, row + i]
                to = (m * SUB + i) * pitch
                copy_rows(tbl0, stage, start, to, chunks)
                copy_rows(tbl, stage, 2 * start, to + chunks, 2 * chunks)

    def compute(row, stage):
        flows = flow_forms(cols, grid, row)
        nu_cols = [jnp.broadcast_to(nus[pl.ds(row, SUB), n : n + 1], (SUB, LANE)) for n in range(3)]
        for c in range(chunks):
            z = modes_at(z_ref, row, c)
            z0, z1, z2, z3, z4, z5 = z

            def beside(m, level):
                return stage[pl.ds(m * SUB * pitch + level * chunks + c, SUB, stride=pitch), :]

            even, odd, last = edge_parts(z)
            gs, g1, gr = flows[c]
            out0 = gs < 0.0
            out1 = g1 < 0.0
            out2 = gr < 0.0
            V0 = [gs * jnp.where(out0, even[i] - odd[i], beside(0, i)) for i in range(3)]
            W0 = [
                g1 * jnp.where(out1, even[0] + odd[0], beside(1, 0)),
                g1 * jnp.where(out1, even[1] + odd[1], -beside(1, 1)),
                g1 * jnp.where(out1, even[2] + odd[2], beside(1, 2)),
            ]
            X = [gr * jnp.where(out2, last[i], beside(2, i)) for i in range(3)]
            S = [a + b for a, b in zip(V0, W0)]
            D = [b - a for a, b in zip(V0, W0)]
            h = gr + 2.0 * gs
            moved = [
                z1 + S[0] * k(B0[0, 1]) + S[1] * k(B0[1, 1]) + X[0] * k(B2[0, 1]) + (gr * z0) * k(KR[1, 0]),
                z2 + D[0] * k(-B0[0, 2]) + D[1] * k(-B0[1, 2]) + X[1] * k(B2[1, 2]) + (h * z0) * k(KR[2, 0]),
                z3
                + S[0] * k(B0[0, 3])
                + S[1] * k(B0[1, 3])
                + S[2] * k(B0[2, 3])
                + X[0] * k(B2[0, 3])
                + gr * (z0 * k(KR[3, 0]) + z1 * k(KR[3, 1])),
                z4
                + D[0] * k(-B0[0, 4])
                + D[1] * k(-B0[1, 4])
                + D[2] * k(-B0[2, 4])
                + X[1] * k(B2[1, 4])
                + h * (z0 * k(KR[4, 0]) + z1 * k(KR[4, 1]))
                + gr * (z2 * k(KR[4, 2])),
                z5
                + S[0] * k(B0[0, 5])
                + S[1] * k(B0[1, 5])
                + S[2] * k(B0[2, 5])
                + X[2] * k(B2[2, 5])
                + gr * (z0 * k(KR[5, 0]) + z1 * k(KR[5, 1]))
                + h * (z2 * k(KR[5, 2])),
            ]
            if section == 1:
                moved = [0.5 * (base_ref[(j + 1, *at(row, c))] + moved[j]) for j in range(5)]
            e02 = last[0] + z5 * k(N[0, 5])
            o02 = z2 * k(N[2, 2]) + z4 * k(N[2, 4])
            inside = (e02 - o02, z0 * k(N[0, 0]) + z1 * k(N[1, 1]) + z3 * k(N[1, 3]), e02 + o02)
            H = [relaxed(forms, n, row, c, vel, nu_cols[n], inside[n]) for n in range(3)]
            H += [high[(n, *at(row, c))] for n in range(3)]
            s02 = H[0] + H[2]
            d20 = H[2] - H[0]
            s34 = H[3] + H[4]
            d43 = H[4] - H[3]
            change = (
                s02 * k(V[1, 0]) + H[1] * k(V[1, 1]) + s34 * k(V[1, 3]) + H[5] * k(V[1, 5]),
                d20 * k(V[2, 2]) + d43 * k(V[2, 4]),
                (s02 + H[5]) * k(V[3, 0]) + (H[1] - s34) * k(V[3, 1]),
                d20 * k(V[4, 2]) + d43 * k(V[4, 4]),
                s02 * k(V[5, 0]) + H[5] * k(V[5, 5]),
            )
            z = [moved[j] + change[j] for j in range(5)]
            for j in range(5):
                out[(j, *at(row, c))] = z[j]
            size1 = jnp.abs(z[0])
            size2 = jnp.abs(z[1])
            size4 = jnp.abs(z[3])
            linear = None
            quadric = None
            for m, q in ((0, 0), (0, 1), (0, 2), (2, 0), (2, 1)):
                t = TR[m, q]
                if q != 1:
                    value = size1 * k(abs(t[1])) + size2 * k(abs(t[2]))
                    linear = value if linear is None else jnp.maximum(linear, value)
                value = jnp.abs(z[2] * k(t[3]) + z[4] * k(t[5]))
                if abs(t[4]) > 1e-9:
                    value = value + size4 * k(abs(t[4]))
                quadric = value if quadric is None else jnp.maximum(quadric, value)
            linear = jnp.maximum(linear, slope_floor)
            quadric = jnp.maximum(quadric, slope_floor)
            over = k(math.sqrt(2.0)) / (linear * quadric)
            sizes[(0, *at(row, c))] = over * quadric
            sizes[(1, *at(row, c))] = over * linear

    pipelined_groups(elems, (stage_a, stage_b), fetch, compute)


def limit_kernel(away, info, centre, rest, sizes, near, far, out, *refs, section):
    if section == 0:
        mom, mtbl, stage_a, stage_b = refs
        target = out
    else:
        mtbl, stage_a, stage_b, target, sems = refs
    elems, vel = centre.shape
    chunks = vel // LANE
    slots = near.shape[0]

    def fill(row):
        for c in range(chunks):
            mtbl[pl.ds(row * chunks + c, SUB, stride=chunks), :] = centre[at(row, c)]

    over_groups(elems, fill)

    def fill_border(row):
        for side, halo in zip(sides(info), (near, far)):
            for c in range(chunks):
                start = (elems + side * slots + row) * chunks + c
                mtbl[pl.ds(start, SUB, stride=chunks), :] = halo[at(row, c)]

    over_groups(slots, fill_border)

    def fetch(row, stage):
        for m in range(3):
            for i in range(SUB):
                copy_rows(mtbl, stage, away[m, row + i], (m * SUB + i) * chunks, chunks)

    def compute(row, stage):
        for c in range(chunks):
            z0 = centre[at(row, c)]
            gaps = [
                jnp.abs(stage[pl.ds(m * SUB * chunks + c, SUB, stride=chunks), :] - z0) for m in range(3)
            ]
            gap = jnp.maximum(jnp.maximum(gaps[0], gaps[1]), gaps[2])
            theta1 = jnp.minimum(1.0, gap * sizes[(0, *at(row, c))])
            theta2 = jnp.minimum(theta1, gap * sizes[(1, *at(row, c))])
            target[(0, *at(row, c))] = z0
            for j in range(1, MODES):
                target[(j, *at(row, c))] = rest[(j - 1, *at(row, c))] * (theta1 if j < 3 else theta2)

    if section == 0:
        pipelined_groups(elems, (stage_a, stage_b), fetch, compute)
        weights = weight_rows(info[0], vel)
        for j in range(MODES):
            mom[pl.ds(j * SUB, SUB), :] = mode_moments(weights, target[j])
    else:
        pieces = sems.shape[0]
        size = elems // pieces
        copies = []
        for piece in range(pieces):
            begin = piece * size

            def fetch_piece(row, stage, begin=begin):
                fetch(row + begin, stage)

            def compute_piece(row, stage, begin=begin):
                compute(pl.multiple_of(row + begin, SUB), stage)

            pipelined_groups(size, (stage_a, stage_b), fetch_piece, compute_piece)
            part = pl.ds(begin, size)
            copy = pltpu.make_async_copy(target.at[:, part, :], out.at[:, part, :], sems.at[piece])
            copy.start()
            copies.append(copy)
        for copy in copies:
            copy.wait()


def traded(value, near):
    peers = lax.axis_size("space")
    pairs = []
    for i in range(0 if near else 1, peers - 1, 2):
        pairs += [(i, i + 1), (i + 1, i)]
    return lax.ppermute(value, "space", pairs)


def swapped(value, bits):
    peers = lax.axis_size("vel")
    return lax.ppermute(value, "vel", [(i, i ^ bits) for i in range(peers)])


def moment_parts(paired):
    peers = lax.axis_size("vel")
    done = 2
    while True:
        width = min(4, peers // done)
        parts = [paired] + [swapped(paired, bits * done) for bits in range(1, width)]
        done *= width
        if done >= peers:
            return parts
        paired = sum(parts[1:], parts[0])


def on_device(distribution, corners, neighbour, boundary_faces, collision_rate):
    modes, elems, vel = distribution.shape
    chunks = vel // LANE
    slots = boundary_faces.shape[2]
    lists = boundary_faces[0]
    info = jnp.stack([lax.axis_index("vel") * vel, lax.axis_index("space") % 2]).astype(jnp.int32)
    faces = 3 * elems
    rows = faces + 2 * slots
    S = jax.ShapeDtypeStruct
    state = S((modes, elems, vel), f32)
    one = S((slots, vel), f32)
    halo = S((3, slots, vel), f32)
    mom = S((modes * SUB, elems), f32)
    columns = S((elems, LANE), f32)
    smem = pl.BlockSpec(memory_space=pltpu.SMEM)
    vmem = pl.BlockSpec(memory_space=pltpu.VMEM)
    hbm = pl.BlockSpec(memory_space=pltpu.HBM)

    def params(mib):
        return pltpu.CompilerParams(vmem_limit_bytes=mib << 20)

    def buffer(count):
        return pltpu.VMEM((count, LANE), f32)

    def evaluated():
        return [pltpu.VMEM((elems, 3 * vel), f32) for _ in range(3)]

    rate = collision_rate.reshape(1, elems)
    index = S(neighbour.shape, jnp.int32)
    src, away, offsets, basis, cols = pl.pallas_call(
        prepare_kernel,
        out_shape=(
            index,
            index,
            S((4, slots), jnp.int32),
            S((TERMS * SUB, modes * vel), bf16),
            columns,
        ),
        in_specs=[smem, smem] + [vmem] * 3,
        out_specs=(vmem,) * 5,
        compiler_params=params(8),
        name="prepare",
    )(lists, info, neighbour, lists, corners.transpose(1, 0, 2))

    current = start = distribution
    partial = pl.pallas_call(
        first_kernel,
        out_shape=mom,
        in_specs=[smem, vmem],
        out_specs=vmem,
        compiler_params=params(8),
        name="first",
    )(info, current)

    for section in range(2):
        opening = section == 0
        paired = partial + swapped(partial, 1)
        tbl0, tbl12, near, far = pl.pallas_call(
            trace_kernel,
            out_shape=(S((rows * chunks, LANE), f32), S((2 * rows * chunks, LANE), f32), halo, halo),
            in_specs=[smem, smem, vmem],
            out_specs=(vmem,) * 4,
            scratch_shapes=[buffer(2 * slots * chunks), buffer(4 * slots * chunks)],
            compiler_params=params(8),
            name="trace",
        )(offsets, info, current)
        near, far, paired = lax.optimization_barrier((near, far, paired))
        far = traded(far, False)
        near = traded(near, True)
        parts = moment_parts(paired)

        base = [] if opening else [start]
        spreads, nus, *forms = pl.pallas_call(
            lambda *refs, section=section: form_kernel(*refs, parts=len(parts), section=section),
            out_shape=(S((3, elems, TERMS * SUB), bf16), columns) + (S((elems, 3 * vel), f32),) * 3,
            in_specs=[vmem] * (len(parts) + 2),
            out_specs=(vmem,) * 5,
            compiler_params=params(16),
            name=f"form{section}",
        )(*parts, rate, basis)

        tbl0, centre, high, near_mean, far_mean = pl.pallas_call(
            lambda *refs, section=section: mean_kernel(*refs, section=section),
            out_shape=(S((rows * chunks, LANE), f32), S((elems, vel), f32), S((3, elems, vel), f32), one, one),
            input_output_aliases={3: 0},
            in_specs=[smem] * 3 + [vmem] * (9 + len(base)),
            out_specs=(vmem,) * 5,
            scratch_shapes=[buffer(elems * chunks)]
            + [buffer(3 * SUB * chunks)] * 2
            + [buffer(2 * slots * chunks)],
            compiler_params=params(16),
            name=f"mean{section}",
        )(offsets, src, info, tbl0, current, near, far, cols, nus, *forms, *base)
        far_mean = traded(far_mean, False)
        near_mean = traded(near_mean, True)

        _, rest, sizes = pl.pallas_call(
            lambda *refs, section=section: rest_kernel(*refs, section=section),
            out_shape=(S((2 * rows * chunks, LANE), f32), S((5, elems, vel), f32), S((2, elems, vel), f32)),
            input_output_aliases={3: 0},
            in_specs=[smem] * 2 + [vmem] * (10 + len(base)),
            out_specs=(vmem,) * 3,
            scratch_shapes=[buffer(9 * SUB * chunks)] * 2 + evaluated(),
            compiler_params=params(20),
            name=f"rest{section}",
        )(src, info, tbl0, tbl12, current, near, far, high, spreads, nus, basis, cols, *base)

        scratch = [buffer((elems + 2 * slots) * chunks)] + [buffer(3 * SUB * chunks)] * 2
        if not opening:
            scratch += [pltpu.VMEM(state.shape, f32), pltpu.SemaphoreType.DMA((4,))]
        made = pl.pallas_call(
            lambda *refs, section=section: limit_kernel(*refs, section=section),
            out_shape=(state, mom) if opening else (state,),
            in_specs=[smem, smem] + [vmem] * 5,
            out_specs=(vmem, vmem) if opening else (hbm,),
            scratch_shapes=scratch,
            compiler_params=params(8),
            name=f"limit{section}",
        )(away, info, centre, rest, sizes, near_mean, far_mean)
        if opening:
            current, partial = made
    return made[0]


def solution(mesh):
    in_specs = (
        P(None, "space", "vel"),
        P(None, None, "space"),
        P(None, "space"),
        P("space", None, None),
        P("space"),
    )
    return jax.shard_map(
        on_device, mesh=mesh, in_specs=in_specs, out_specs=P(None, "space", "vel"), check_vma=False
    )
```

time: 119 us -> 72.7 us (0.61)
  Pallas kernels: 58 us -> 39.1 us
  waiting for transfers between devices: 21.7 us -> 6.72 us
  starting transfers between devices: 33.3 us -> 24.5 us
  local copies, waits for them, and re-layouts: 3.84 us -> 1.91 us
  other arithmetic: 1.61 us -> 0.09 us
    pallas_call x5 -> x12, Pallas kernels: 58 us -> 39.1 us  [the longest x2 14.5 us: on_device(): pl.pallas_call(lambda *refs, section=section: rest_kernel(*refs, section=...]
    ppermute x8, waiting for transfers between devices: 9.85 us -> 0.02 us  [traded(): return lax.ppermute(value, 'space', pairs)]
    ppermute x8, starting transfers between devices: 23.4 us -> 14.7 us  [traded(): return lax.ppermute(value, 'space', pairs)]
    ppermute x8, waiting for transfers between devices: 11.9 us -> 6.7 us  [swapped(): return lax.ppermute(value, 'vel', [(i, i ^ bits) for i in range(peers)])]
    add x2, other arithmetic: 1.61 us -> 0.02 us  [on_device(): paired = partial + swapped(partial, 1)]
    unnamed x35 -> x12, local copies, waits for them, and re-layouts: 3.24 us -> 1.91 us
  transfers between devices with their start and end apart: 16 -> 16, of which waited for: 11 -> 5; matrix products, arithmetic and copies ran while one was open for 2% -> 0% of each run, Pallas kernels for 0% -> 31%
where the time goes in v1:
time: 72.7 us; the launch traced here: 72.5 us
  Pallas kernels  39.1 us (54%)
  starting transfers between devices  24.5 us (34%)
  waiting for transfers between devices  6.72 us (9%)
  local copies, waits for them, and re-layouts  1.91 us (3%)
    ppermute x8, starting transfers between devices, traded(): return lax.ppermute(value, 'space', pairs)  14.7 us
    pallas_call x2, Pallas kernels, on_device(): pl.pallas_call(lambda *refs, section=section: rest_kernel(*refs, section=...  14.5 us
    ppermute x8, starting transfers between devices, swapped(): return lax.ppermute(value, 'vel', [(i, i ^ bits) for i in range(peers)])  9.76 us
    pallas_call x2, Pallas kernels, on_device(): pl.pallas_call(lambda *refs, section=section: mean_kernel(*refs, section=...  8.33 us
    pallas_call x2, Pallas kernels, on_device(): pl.pallas_call(lambda *refs, section=section: limit_kernel(*refs, section...  7.05 us
    ppermute x8, waiting for transfers between devices, swapped(): return lax.ppermute(value, 'vel', [(i, i ^ bits) for i in range(peers)])  6.7 us
    pallas_call x2, Pallas kernels, on_device(): pl.pallas_call(trace_kernel, out_shape=(S((rows * chunks, LANE), f32), S(...  4.6 us
    unnamed x12, local copies, waits for them, and re-layouts  1.91 us
  transfers between devices with their start and end apart: 16, of which 5 were waited for; matrix products, arithmetic and copies ran while one was open for 0% of the time, Pallas kernels for 31%

profile of v1, /device:TPU:1, one launch (start us, length us, event | category | flops | bytes accessed | tf_op | source)
XLA Modules:
  0.0 72.5 jit_solution(6825217703626516991)
XLA Ops:
  0.0 0.1 pad_add_fusion.info.refs_2_.refs_1_
  0.1 1.9 %copy-done = f32[6,256,512]{2,1,0:T(8,128)S(1)} copy-done((f32[6,256,512]{2,1,0:T(8,128)S(1)}, f32[6,256,512]{2,1,0:T(8,128)}, u32[]{:S(2)}) %copy-start) | copy-done | bytes 3145752
  2.0 1.5 %first.1 = f32[48,256]{1,0:T(8,128)S(1)} custom-call(s32[2]{0:T(128)S(1)} %pad_add_fusion.info.refs_2_.refs_1_, f32[6,256,512]{2,1,0:T(8,128)S(1)} %copy-done), custom_call_target="tpu_custom_call" | custom-call | tf_op jit(solution)/shard_map/first/pallas_call | solution.py:757
  3.5 2.1 %collective-permute-start = (f32[48,256]{1,0:T(8,128)S(1)}, f32[48,256]{1,0:T(8,128)S(1)}, u32[]{:S(2)}, u32[]{:S(2)}) collective-permute-start(f32[48,256]{1,0:T(8,128)S(1)} %first.1), channel_id=1, source_target_pairs={{0,1},{1,0},{2,3},{3,2},{4,5},{5,4},{6,7},{7,6},{8,9},{9,8},{10,11... | collective-permute-start | bytes 147464 | tf_op jit(solution)/shard_map/ppermute | solution.py:697
  5.6 0.0 copy-done.5
  5.7 1.4 %prepare.1 = (s32[3,256]{1,0:T(4,128)S(1)}, s32[3,256]{1,0:T(4,128)S(1)}, s32[4,80]{1,0:T(4,128)S(1)}, bf16[256,3072]{1,0:T(8,128)(2,1)S(1)}, f32[256,128]{1,0:T(8,128)S(1)}) custom-call(s32[2,80]{1,0:T(2,128)S(1)} %bitcast.8, s32[2]{0:T(128)S(1)} %pad_add_fusion.info.refs_2_.refs_1_, s32[3,256]{1,0:T(4,128)S(1)} %copy-done.4, s32[2,80]{1,0:T(2,128)S(1)} %bitcast.9, ...), custom_call_target="tpu_custom_call" | custom-call | tf_op jit(solution)/shard_map/prepare/pallas_call | solution.py:741
  7.0 2.3 %trace.2 = (f32[3712,128]{1,0:T(8,128)S(1)}, f32[7424,128]{1,0:T(8,128)S(1)}, f32[3,80,512]{2,1,0:T(8,128)S(1)}, f32[3,80,512]{2,1,0:T(8,128)S(1)}) custom-call(s32[4,80]{1,0:T(4,128)S(1)} %get-tuple-element.51.offsets.refs_0_, s32[2]{0:T(128)S(1)} %pad_add_fusion.info.refs_2_.refs_1_, f32[6,256,512]{2,1,0:T(8,128)S(1)} %copy-done.1), custom_call_target="tpu_custom_call" | custom-call | tf_op jit(solution)/shard_map/trace/pallas_call | solution.py:769
  9.4 0.0 collective-permute-done
  9.4 1.0 %collective-permute-start.1 = (f32[3,80,512]{2,1,0:T(8,128)S(1)}, f32[3,80,512]{2,1,0:T(8,128)S(1)}, u32[]{:S(2)}, u32[]{:S(2)}) collective-permute-start(f32[3,80,512]{2,1,0:T(8,128)S(1)} %get-tuple-element.56), channel_id=1, source_target_pairs={{0,8},{8,0},{16,24},{24,16},{1,9},{9,1},{17,25},{25,17},{2,10},{10... | collective-permute-start | bytes 1474568 | tf_op jit(solution)/shard_map/ppermute | solution.py:692
  10.4 3.0 %collective-permute-start.2 = (f32[3,80,512]{2,1,0:T(8,128)S(1)}, f32[3,80,512]{2,1,0:T(8,128)S(1)}, u32[]{:S(2)}, u32[]{:S(2)}) collective-permute-start(f32[3,80,512]{2,1,0:T(8,128)S(1)} %get-tuple-element.57), channel_id=1, source_target_pairs={{8,16},{16,8},{9,17},{17,9},{10,18},{18,10},{11,19},{19,11},{12,20... | collective-permute-start | bytes 1474568 | tf_op jit(solution)/shard_map/ppermute | solution.py:692
  13.5 3.4 %collective-permute-start.5 = (f32[48,256]{1,0:T(8,128)S(1)}, f32[48,256]{1,0:T(8,128)S(1)}, u32[]{:S(2)}, u32[]{:S(2)}) collective-permute-start(f32[48,256]{1,0:T(8,128)S(1)} %add.11.refs_0_), channel_id=1, source_target_pairs={{0,6},{1,7},{2,4},{3,5},{4,2},{5,3},{6,0},{7,1},{8,14},{9,15},{10,... | collective-permute-start | bytes 147464 | tf_op jit(solution)/shard_map/ppermute | solution.py:697
  16.8 0.0 collective-permute-start.4
  16.9 0.4 collective-permute-start.3
  17.2 1.5 %collective-permute-done.5.refs_3_ = f32[48,256]{1,0:T(8,128)S(1)} collective-permute-done((f32[48,256]{1,0:T(8,128)S(1)}, f32[48,256]{1,0:T(8,128)S(1)}, u32[]{:S(2)}, u32[]{:S(2)}) %collective-permute-start.5) | collective-permute-done | bytes 49184 | tf_op jit(solution)/shard_map/ppermute | solution.py:697
  18.7 2.0 %collective-permute-done.4.refs_2_ = f32[48,256]{1,0:T(8,128)S(1)} collective-permute-done((f32[48,256]{1,0:T(8,128)S(1)}, f32[48,256]{1,0:T(8,128)S(1)}, u32[]{:S(2)}, u32[]{:S(2)}) %collective-permute-start.4) | collective-permute-done | bytes 49184 | tf_op jit(solution)/shard_map/ppermute | solution.py:697
  20.7 0.0 collective-permute-done.3.refs_1_
  20.7 0.0 copy-done.3
  20.7 0.9 %form0.1 = (bf16[3,256,256]{2,1,0:T(8,128)(2,1)S(1)}, f32[256,128]{1,0:T(8,128)S(1)}, f32[256,1536]{1,0:T(8,128)S(1)}, f32[256,1536]{1,0:T(8,128)S(1)}, f32[256,1536]{1,0:T(8,128)S(1)}) custom-call(f32[48,256]{1,0:T(8,128)S(1)} %add.11.refs_0_, f32[48,256]{1,0:T(8,128)S(1)} %collective-permute-done.3.refs_1_, f32[48,256]{1,0:T(8,128)S(1)} %collective-permute-done.4.refs_2_, ...), custom_call_target="tpu_custom_call" | custom-call | tf_op jit(solution)/shard_map/form0/pallas_call | solution.py:784
  21.6 0.0 collective-permute-done.1.refs_5_
  21.6 0.0 collective-permute-done.2.refs_6_
  21.6 4.1 %mean0.1 = (f32[3712,128]{1,0:T(8,128)S(1)}, f32[256,512]{1,0:T(8,128)S(1)}, f32[3,256,512]{2,1,0:T(8,128)S(1)}, f32[80,512]{1,0:T(8,128)S(1)}, f32[80,512]{1,0:T(8,128)S(1)}) custom-call(s32[4,80]{1,0:T(4,128)S(1)} %get-tuple-element.51.offsets.refs_0_, s32[3,256]{1,0:T(4,128)S(1)} %get-tuple-element.52.refs_1_.refs_0_, ...), custom_call_target="tpu_custom_call", output_to_operand_aliasing={{0}: (3, {})} | custom-call | tf_op jit(solution)/shard_map/mean0/pallas_call | solution.py:793
  25.8 0.1 collective-permute-start.6
  25.8 3.9 %collective-permute-start.7 = (f32[80,512]{1,0:T(8,128)S(1)}, f32[80,512]{1,0:T(8,128)S(1)}, u32[]{:S(2)}, u32[]{:S(2)}) collective-permute-start(f32[80,512]{1,0:T(8,128)S(1)} %get-tuple-element.73), channel_id=1, source_target_pairs={{8,16},{16,8},{9,17},{17,9},{10,18},{18,10},{11,19},{19,11},{12,20... | collective-permute-start | bytes 491528 | tf_op jit(solution)/shard_map/ppermute | solution.py:692
  29.8 7.1 %rest0.1 = (f32[7424,128]{1,0:T(8,128)S(1)}, f32[5,256,512]{2,1,0:T(8,128)S(1)}, f32[2,256,512]{2,1,0:T(8,128)S(1)}) custom-call(s32[3,256]{1,0:T(4,128)S(1)} %get-tuple-element.52.refs_1_.refs_0_, s32[2]{0:T(128)S(1)} %pad_add_fusion.info.refs_2_.refs_1_, f32[3712,128]{1,0:T(8,128)S(1)} %get-tuple-element.66.refs_2_, ...), custom_call_target="tpu_custom_call", output_to_operand_aliasing={{0}: (3, {})} | custom-call | tf_op jit(solution)/shard_map/rest0/pallas_call | solution.py:808
  36.9 0.0 collective-permute-done.6.refs_5_
  36.9 0.0 collective-permute-done.7.refs_6_
  36.9 3.5 %limit0.1 = (f32[6,256,512]{2,1,0:T(8,128)S(1)}, f32[48,256]{1,0:T(8,128)S(1)}) custom-call(s32[3,256]{1,0:T(4,128)S(1)} %get-tuple-element.50.refs_0_, s32[2]{0:T(128)S(1)} %pad_add_fusion.info.refs_2_.refs_1_, f32[256,512]{1,0:T(8,128)S(1)} %get-tuple-element.65.refs_2_, f32[5,256,512]{2,1,0:T(8,128)S(1)} %get-tuple-element.70.refs_3_, ...), custom_call_target="tpu_custom_call" | custom-call | tf_op jit(solution)/shard_map/limit0/pallas_call | solution.py:822
  40.5 0.3 collective-permute-start.8
  40.7 2.3 %trace.3 = (f32[3712,128]{1,0:T(8,128)S(1)}, f32[7424,128]{1,0:T(8,128)S(1)}, f32[3,80,512]{2,1,0:T(8,128)S(1)}, f32[3,80,512]{2,1,0:T(8,128)S(1)}) custom-call(s32[4,80]{1,0:T(4,128)S(1)} %get-tuple-element.51.offsets.refs_0_, s32[2]{0:T(128)S(1)} %pad_add_fusion.info.refs_2_.refs_1_, f32[6,256,512]{2,1,0:T(8,128)S(1)} %get-tuple-element.74.z_ref.refs_4_), custom_call_target="tpu_custom_call" | custom-call | tf_op jit(solution)/shard_map/trace/pallas_call | solution.py:769
  43.0 0.4 collective-permute-done.8
  43.4 0.1 collective-permute-start.9
  43.5 3.1 %collective-permute-start.10 = (f32[3,80,512]{2,1,0:T(8,128)S(1)}, f32[3,80,512]{2,1,0:T(8,128)S(1)}, u32[]{:S(2)}, u32[]{:S(2)}) collective-permute-start(f32[3,80,512]{2,1,0:T(8,128)S(1)} %get-tuple-element.80), channel_id=1, source_target_pairs={{8,16},{16,8},{9,17},{17,9},{10,18},{18,10},{11,19},{19,11},{12,20... | collective-permute-start | bytes 1474568 | tf_op jit(solution)/shard_map/ppermute | solution.py:692
  46.6 2.0 %collective-permute-start.13 = (f32[48,256]{1,0:T(8,128)S(1)}, f32[48,256]{1,0:T(8,128)S(1)}, u32[]{:S(2)}, u32[]{:S(2)}) collective-permute-start(f32[48,256]{1,0:T(8,128)S(1)} %add.12.refs_0_), channel_id=1, source_target_pairs={{0,6},{1,7},{2,4},{3,5},{4,2},{5,3},{6,0},{7,1},{8,14},{9,15},{10,... | collective-permute-start | bytes 147464 | tf_op jit(solution)/shard_map/ppermute | solution.py:697
  48.6 0.0 collective-permute-start.12
  48.6 1.6 %collective-permute-start.11 = (f32[48,256]{1,0:T(8,128)S(1)}, f32[48,256]{1,0:T(8,128)S(1)}, u32[]{:S(2)}, u32[]{:S(2)}) collective-permute-start(f32[48,256]{1,0:T(8,128)S(1)} %add.12.refs_0_), channel_id=1, source_target_pairs={{0,2},{1,3},{2,0},{3,1},{4,6},{5,7},{6,4},{7,5},{8,10},{9,11},{10,... | collective-permute-start | bytes 147464 | tf_op jit(solution)/shard_map/ppermute | solution.py:697
  50.2 1.5 %collective-permute-done.13.refs_3_ = f32[48,256]{1,0:T(8,128)S(1)} collective-permute-done((f32[48,256]{1,0:T(8,128)S(1)}, f32[48,256]{1,0:T(8,128)S(1)}, u32[]{:S(2)}, u32[]{:S(2)}) %collective-permute-start.13) | collective-permute-done | bytes 49184 | tf_op jit(solution)/shard_map/ppermute | solution.py:697
  51.8 1.3 %collective-permute-done.12.refs_2_ = f32[48,256]{1,0:T(8,128)S(1)} collective-permute-done((f32[48,256]{1,0:T(8,128)S(1)}, f32[48,256]{1,0:T(8,128)S(1)}, u32[]{:S(2)}, u32[]{:S(2)}) %collective-permute-start.12) | collective-permute-done | bytes 49184 | tf_op jit(solution)/shard_map/ppermute | solution.py:697
  53.0 0.0 collective-permute-done.11.refs_1_
  53.0 0.9 %form1.1 = (bf16[3,256,256]{2,1,0:T(8,128)(2,1)S(1)}, f32[256,128]{1,0:T(8,128)S(1)}, f32[256,1536]{1,0:T(8,128)S(1)}, f32[256,1536]{1,0:T(8,128)S(1)}, f32[256,1536]{1,0:T(8,128)S(1)}) custom-call(f32[48,256]{1,0:T(8,128)S(1)} %add.12.refs_0_, f32[48,256]{1,0:T(8,128)S(1)} %collective-permute-done.11.refs_1_, ...), custom_call_target="tpu_custom_call" | custom-call | tf_op jit(solution)/shard_map/form1/pallas_call | solution.py:784
  53.9 0.0 collective-permute-done.9.refs_5_
  53.9 0.0 collective-permute-done.10.refs_6_
  53.9 4.2 %mean1.1 = (f32[3712,128]{1,0:T(8,128)S(1)}, f32[256,512]{1,0:T(8,128)S(1)}, f32[3,256,512]{2,1,0:T(8,128)S(1)}, f32[80,512]{1,0:T(8,128)S(1)}, f32[80,512]{1,0:T(8,128)S(1)}) custom-call(s32[4,80]{1,0:T(4,128)S(1)} %get-tuple-element.51.offsets.refs_0_, s32[3,256]{1,0:T(4,128)S(1)} %get-tuple-element.52.refs_1_.refs_0_, ...), custom_call_target="tpu_custom_call", output_to_operand_aliasing={{0}: (3, {})} | custom-call | tf_op jit(solution)/shard_map/mean1/pallas_call | solution.py:793
  58.1 0.2 collective-permute-start.14
  58.3 3.4 %collective-permute-start.15 = (f32[80,512]{1,0:T(8,128)S(1)}, f32[80,512]{1,0:T(8,128)S(1)}, u32[]{:S(2)}, u32[]{:S(2)}) collective-permute-start(f32[80,512]{1,0:T(8,128)S(1)} %get-tuple-element.94), channel_id=1, source_target_pairs={{8,16},{16,8},{9,17},{17,9},{10,18},{18,10},{11,19},{19,11},{12,20... | collective-permute-start | bytes 491528 | tf_op jit(solution)/shard_map/ppermute | solution.py:692
  61.7 7.3 %rest1.1 = (f32[7424,128]{1,0:T(8,128)S(1)}, f32[5,256,512]{2,1,0:T(8,128)S(1)}, f32[2,256,512]{2,1,0:T(8,128)S(1)}) custom-call(s32[3,256]{1,0:T(4,128)S(1)} %get-tuple-element.52.refs_1_.refs_0_, s32[2]{0:T(128)S(1)} %pad_add_fusion.info.refs_2_.refs_1_, f32[3712,128]{1,0:T(8,128)S(1)} %get-tuple-element.87.refs_2_, ...), custom_call_target="tpu_custom_call", output_to_operand_aliasing={{0}: (3, {})} | custom-call | tf_op jit(solution)/shard_map/rest1/pallas_call | solution.py:808
  69.0 0.0 collective-permute-done.14.refs_5_
  69.0 0.0 collective-permute-done.15.refs_6_
  69.0 3.5 %limit1.1 = f32[6,256,512]{2,1,0:T(8,128)} custom-call(s32[3,256]{1,0:T(4,128)S(1)} %get-tuple-element.50.refs_0_, s32[2]{0:T(128)S(1)} %pad_add_fusion.info.refs_2_.refs_1_, f32[256,512]{1,0:T(8,128)S(1)} %get-tuple-element.86.refs_2_, f32[5,256,512]{2,1,0:T(8,128)S(1)} %get-tuple-element.91.refs_3_, f32[2,256,512]{2,1,0:T(8,128)S(1)} %get-tuple-element.92.refs_4_, ...), custom_call_target="tpu_custom_call" | custom-call | tf_op jit(solution)/shard_map/limit1/pallas_call | solution.py:822
  (11 shorter events, 0.0 us)
Async XLA Ops:
  0.0 5.6 %copy-start.5 = (s32[1,2,80]{2,1,0:T(2,128)S(1)}, s32[1,2,80]{2,1,0:T(2,128)}, u32[]{:S(2)}) copy-start(s32[1,2,80]{2,1,0:T(2,128)} %param.8) | copy-start | bytes 1924
  0.0 5.6 %copy-start.4 = (s32[3,256]{1,0:T(4,128)S(1)}, s32[3,256]{1,0:T(4,128)}, u32[]{:S(2)}) copy-start(s32[3,256]{1,0:T(4,128)} %neigh_ref.1) | copy-start | bytes 9220
  0.0 5.6 %copy-start.2 = (f32[2,3,256]{2,0,1:T(2,128)S(1)}, f32[2,3,256]{2,0,1:T(2,128)}, u32[]{:S(2)}) copy-start(f32[2,3,256]{2,0,1:T(2,128)} %param.6) | copy-start | bytes 18436
  0.1 1.9 %copy-start = (f32[6,256,512]{2,1,0:T(8,128)S(1)}, f32[6,256,512]{2,1,0:T(8,128)}, u32[]{:S(2)}) copy-start(f32[6,256,512]{2,1,0:T(8,128)} %refs_12_.3) | copy-start | bytes 9437188
  2.0 5.1 %copy-start.1 = (f32[6,256,512]{2,1,0:T(8,128)S(1)}, f32[6,256,512]{2,1,0:T(8,128)}, u32[]{:S(2)}) copy-start(f32[6,256,512]{2,1,0:T(8,128)} %refs_12_.3) | copy-start | bytes 9437188
  3.5 17.2 %copy-start.3 = (f32[256]{0:T(256)S(1)}, f32[256]{0:T(256)}, u32[]{:S(2)}) copy-start(f32[256]{0:T(256)} %param.9) | copy-start | bytes 3076
  3.5 5.8 %collective-permute-start = (f32[48,256]{1,0:T(8,128)S(1)}, f32[48,256]{1,0:T(8,128)S(1)}, u32[]{:S(2)}, u32[]{:S(2)}) collective-permute-start(f32[48,256]{1,0:T(8,128)S(1)} %first.1), channel_id=1, source_target_pairs={{0,1},{1,0},{2,3},{3,2},{4,5},{5,4},{6,7},{7,6},{8,9},{9,8},{10,11... | collective-permute-start | bytes 147464 | tf_op jit(solution)/shard_map/ppermute | solution.py:697
  9.4 12.2 %collective-permute-start.1 = (f32[3,80,512]{2,1,0:T(8,128)S(1)}, f32[3,80,512]{2,1,0:T(8,128)S(1)}, u32[]{:S(2)}, u32[]{:S(2)}) collective-permute-start(f32[3,80,512]{2,1,0:T(8,128)S(1)} %get-tuple-element.56), channel_id=1, source_target_pairs={{0,8},{8,0},{16,24},{24,16},{1,9},{9,1},{17,25},{25,17},{2,10},{10... | collective-permute-start | bytes 1474568 | tf_op jit(solution)/shard_map/ppermute | solution.py:692
  10.4 11.2 %collective-permute-start.2 = (f32[3,80,512]{2,1,0:T(8,128)S(1)}, f32[3,80,512]{2,1,0:T(8,128)S(1)}, u32[]{:S(2)}, u32[]{:S(2)}) collective-permute-start(f32[3,80,512]{2,1,0:T(8,128)S(1)} %get-tuple-element.57), channel_id=1, source_target_pairs={{8,16},{16,8},{9,17},{17,9},{10,18},{18,10},{11,19},{19,11},{12,20... | collective-permute-start | bytes 1474568 | tf_op jit(solution)/shard_map/ppermute | solution.py:692
  13.5 5.2 %collective-permute-start.5 = (f32[48,256]{1,0:T(8,128)S(1)}, f32[48,256]{1,0:T(8,128)S(1)}, u32[]{:S(2)}, u32[]{:S(2)}) collective-permute-start(f32[48,256]{1,0:T(8,128)S(1)} %add.11.refs_0_), channel_id=1, source_target_pairs={{0,6},{1,7},{2,4},{3,5},{4,2},{5,3},{6,0},{7,1},{8,14},{9,15},{10,... | collective-permute-start | bytes 147464 | tf_op jit(solution)/shard_map/ppermute | solution.py:697
  16.8 3.8 %collective-permute-start.4 = (f32[48,256]{1,0:T(8,128)S(1)}, f32[48,256]{1,0:T(8,128)S(1)}, u32[]{:S(2)}, u32[]{:S(2)}) collective-permute-start(f32[48,256]{1,0:T(8,128)S(1)} %add.11.refs_0_), channel_id=1, source_target_pairs={{0,4},{1,5},{2,6},{3,7},{4,0},{5,1},{6,2},{7,3},{8,12},{9,13},{10,... | collective-permute-start | bytes 147464 | tf_op jit(solution)/shard_map/ppermute | solution.py:697
  16.9 3.8 %collective-permute-start.3 = (f32[48,256]{1,0:T(8,128)S(1)}, f32[48,256]{1,0:T(8,128)S(1)}, u32[]{:S(2)}, u32[]{:S(2)}) collective-permute-start(f32[48,256]{1,0:T(8,128)S(1)} %add.11.refs_0_), channel_id=1, source_target_pairs={{0,2},{1,3},{2,0},{3,1},{4,6},{5,7},{6,4},{7,5},{8,10},{9,11},{10,... | collective-permute-start | bytes 147464 | tf_op jit(solution)/shard_map/ppermute | solution.py:697
  25.8 11.1 %collective-permute-start.6 = (f32[80,512]{1,0:T(8,128)S(1)}, f32[80,512]{1,0:T(8,128)S(1)}, u32[]{:S(2)}, u32[]{:S(2)}) collective-permute-start(f32[80,512]{1,0:T(8,128)S(1)} %get-tuple-element.72), channel_id=1, source_target_pairs={{0,8},{8,0},{16,24},{24,16},{1,9},{9,1},{17,25},{25,17},{2,10},{10... | collective-permute-start | bytes 491528 | tf_op jit(solution)/shard_map/ppermute | solution.py:692
  25.8 11.1 %collective-permute-start.7 = (f32[80,512]{1,0:T(8,128)S(1)}, f32[80,512]{1,0:T(8,128)S(1)}, u32[]{:S(2)}, u32[]{:S(2)}) collective-permute-start(f32[80,512]{1,0:T(8,128)S(1)} %get-tuple-element.73), channel_id=1, source_target_pairs={{8,16},{16,8},{9,17},{17,9},{10,18},{18,10},{11,19},{19,11},{12,20... | collective-permute-start | bytes 491528 | tf_op jit(solution)/shard_map/ppermute | solution.py:692
  40.5 3.0 %collective-permute-start.8 = (f32[48,256]{1,0:T(8,128)S(1)}, f32[48,256]{1,0:T(8,128)S(1)}, u32[]{:S(2)}, u32[]{:S(2)}) collective-permute-start(f32[48,256]{1,0:T(8,128)S(1)} %get-tuple-element.78), channel_id=1, source_target_pairs={{0,1},{1,0},{2,3},{3,2},{4,5},{5,4},{6,7},{7,6},{8,9},{9,8},{10,11... | collective-permute-start | bytes 147464 | tf_op jit(solution)/shard_map/ppermute | solution.py:697
  43.4 10.5 %collective-permute-start.9 = (f32[3,80,512]{2,1,0:T(8,128)S(1)}, f32[3,80,512]{2,1,0:T(8,128)S(1)}, u32[]{:S(2)}, u32[]{:S(2)}) collective-permute-start(f32[3,80,512]{2,1,0:T(8,128)S(1)} %get-tuple-element.79), channel_id=1, source_target_pairs={{0,8},{8,0},{16,24},{24,16},{1,9},{9,1},{17,25},{25,17},{2,10},{10... | collective-permute-start | bytes 1474568 | tf_op jit(solution)/shard_map/ppermute | solution.py:692
  43.5 10.4 %collective-permute-start.10 = (f32[3,80,512]{2,1,0:T(8,128)S(1)}, f32[3,80,512]{2,1,0:T(8,128)S(1)}, u32[]{:S(2)}, u32[]{:S(2)}) collective-permute-start(f32[3,80,512]{2,1,0:T(8,128)S(1)} %get-tuple-element.80), channel_id=1, source_target_pairs={{8,16},{16,8},{9,17},{17,9},{10,18},{18,10},{11,19},{19,11},{12,20... | collective-permute-start | bytes 1474568 | tf_op jit(solution)/shard_map/ppermute | solution.py:692
  46.6 5.2 %collective-permute-start.13 = (f32[48,256]{1,0:T(8,128)S(1)}, f32[48,256]{1,0:T(8,128)S(1)}, u32[]{:S(2)}, u32[]{:S(2)}) collective-permute-start(f32[48,256]{1,0:T(8,128)S(1)} %add.12.refs_0_), channel_id=1, source_target_pairs={{0,6},{1,7},{2,4},{3,5},{4,2},{5,3},{6,0},{7,1},{8,14},{9,15},{10,... | collective-permute-start | bytes 147464 | tf_op jit(solution)/shard_map/ppermute | solution.py:697
  48.6 4.4 %collective-permute-start.12 = (f32[48,256]{1,0:T(8,128)S(1)}, f32[48,256]{1,0:T(8,128)S(1)}, u32[]{:S(2)}, u32[]{:S(2)}) collective-permute-start(f32[48,256]{1,0:T(8,128)S(1)} %add.12.refs_0_), channel_id=1, source_target_pairs={{0,4},{1,5},{2,6},{3,7},{4,0},{5,1},{6,2},{7,3},{8,12},{9,13},{10,... | collective-permute-start | bytes 147464 | tf_op jit(solution)/shard_map/ppermute | solution.py:697
  48.6 4.4 %collective-permute-start.11 = (f32[48,256]{1,0:T(8,128)S(1)}, f32[48,256]{1,0:T(8,128)S(1)}, u32[]{:S(2)}, u32[]{:S(2)}) collective-permute-start(f32[48,256]{1,0:T(8,128)S(1)} %add.12.refs_0_), channel_id=1, source_target_pairs={{0,2},{1,3},{2,0},{3,1},{4,6},{5,7},{6,4},{7,5},{8,10},{9,11},{10,... | collective-permute-start | bytes 147464 | tf_op jit(solution)/shard_map/ppermute | solution.py:697
  58.1 10.9 %collective-permute-start.14 = (f32[80,512]{1,0:T(8,128)S(1)}, f32[80,512]{1,0:T(8,128)S(1)}, u32[]{:S(2)}, u32[]{:S(2)}) collective-permute-start(f32[80,512]{1,0:T(8,128)S(1)} %get-tuple-element.93), channel_id=1, source_target_pairs={{0,8},{8,0},{16,24},{24,16},{1,9},{9,1},{17,25},{25,17},{2,10},{10... | collective-permute-start | bytes 491528 | tf_op jit(solution)/shard_map/ppermute | solution.py:692
  58.3 10.7 %collective-permute-start.15 = (f32[80,512]{1,0:T(8,128)S(1)}, f32[80,512]{1,0:T(8,128)S(1)}, u32[]{:S(2)}, u32[]{:S(2)}) collective-permute-start(f32[80,512]{1,0:T(8,128)S(1)} %get-tuple-element.94), channel_id=1, source_target_pairs={{8,16},{16,8},{9,17},{17,9},{10,18},{18,10},{11,19},{19,11},{12,20... | collective-permute-start | bytes 491528 | tf_op jit(solution)/shard_map/ppermute | solution.py:692

commit v2 on v1

--- a/solution.py
+++ b/solution.py
@@ -102,15 +102,6 @@
     return even, odd, last
 
 
-def level0(z):
-    z0, z1, z2, z3, z4, z5 = z
-    b, c = EDGE[0], EDGE[2]
-    a0 = z0 * k(b[0, 0])
-    even = a0 + z1 * k(b[0, 1]) + z3 * k(b[0, 3]) + z5 * k(b[0, 5])
-    odd = z2 * k(-b[0, 2]) + z4 * k(-b[0, 4])
-    return even - odd, even + odd, a0 + z1 * k(c[0, 1]) + z3 * k(c[0, 3])
-
-
 def table_values(z):
     even, odd, last = edge_parts(z)
     return (
@@ -128,12 +119,13 @@
     return [ref[(j, *at(row, chunk))] for j in range(ref.shape[0])]
 
 
-def over_groups(count, body):
+def over_groups(count, body, together=1):
     def step(g, _):
-        body(pl.multiple_of(g * SUB, SUB))
+        for i in range(together):
+            body(pl.multiple_of(g * (SUB * together) + i * SUB, SUB))
         return 0
 
-    lax.fori_loop(0, count // SUB, step, 0)
+    lax.fori_loop(0, count // (SUB * together), step, 0)
 
 
 def copy_rows(source, target, start, to, count):
@@ -217,13 +209,20 @@
     offsets[pl.ds(2, 2), :] = known % elems * chunks
 
 
+def put_columns(rows, out):
+    elems = out.shape[1]
+    turned = jnp.concatenate([*rows, jnp.zeros((LANE - out.shape[0], elems), f32)], axis=0).T
+    for n in range(out.shape[0]):
+        out[n] = jnp.broadcast_to(turned[:, n : n + 1], (elems, LANE))
+
+
 def put_flows(corner, cols):
     cx = [corner[i, 0:1, :] for i in range(3)]
     cy = [corner[i, 1:2, :] for i in range(3)]
     det = (cx[1] - cx[0]) * (cy[2] - cy[0]) - (cx[2] - cx[0]) * (cy[1] - cy[0])
     step = time_step / det
     rows = [-step * (cy[1] - cy[0]), step * (cx[1] - cx[0]), -step * (cy[0] - cy[2]), step * (cx[0] - cx[2])]
-    cols[...] = jnp.concatenate([*rows, jnp.zeros((LANE - 4, cols.shape[0]), f32)], axis=0).T
+    put_columns(rows, cols)
 
 
 def sides(info):
@@ -233,7 +232,7 @@
 
 def prepare_kernel(lists, info, neigh_ref, rows_ref, corner, src, away, offsets, basis, cols):
     vel = basis.shape[1] // MODES
-    put_index(neigh_ref, rows_ref, lists, src, away, offsets, cols.shape[0], vel // LANE)
+    put_index(neigh_ref, rows_ref, lists, src, away, offsets, cols.shape[1], vel // LANE)
     put_flows(corner, cols)
     put_basis(info[0], basis, vel)
 
@@ -277,8 +276,10 @@
     over_groups(slots, pack)
 
 
-def flow_forms(cols, grid, row):
-    col = [jnp.broadcast_to(cols[pl.ds(row, SUB), n : n + 1], (SUB, LANE)) for n in range(4)]
+def flow_forms(cols, grid, row, half=False):
+    col = [cols[n, pl.ds(row, SUB), :] for n in range(4)]
+    if half:
+        col = [0.5 * value for value in col]
     flows = []
     for x, y in grid:
         g0 = col[0] * x + col[1] * y
@@ -402,20 +403,71 @@
     for ref in mom_refs[1:]:
         moments = moments + ref[...]
     nu, coefficients = node_parameters(moments, rate[...], elems, scale)
-    nus[...] = jnp.concatenate([nu, jnp.zeros((LANE - SUB, elems), f32)], axis=0).T
+    put_columns([nu[n : n + 1, :] for n in range(MODES)], nus)
     for i, form in enumerate(coefficients):
         spreads[i] = spread(form, elems)
         forms[i][...] = jnp.dot(spreads[i], basis[:, pl.ds(half, half)], preferred_element_type=f32)
 
 
-def mean_kernel(offsets, src, info, _, z_ref, near_in, far_in, cols, nus, *refs, section):
+def lifted(V, W, X):
+    B0, B2 = EDGE[0], EDGE[2]
+    S = [a + b for a, b in zip(V, W)]
+    D = [b - a for a, b in zip(V, W)]
+    return (
+        (S[0] + X[0]) * k(B0[0, 0]),
+        S[0] * k(B0[0, 1]) + S[1] * k(B0[1, 1]) + X[0] * k(B2[0, 1]),
+        D[0] * k(-B0[0, 2]) + D[1] * k(-B0[1, 2]) + X[1] * k(B2[1, 2]),
+        S[0] * k(B0[0, 3]) + S[1] * k(B0[1, 3]) + S[2] * k(B0[2, 3]) + X[0] * k(B2[0, 3]),
+        D[0] * k(-B0[0, 4]) + D[1] * k(-B0[1, 4]) + D[2] * k(-B0[2, 4]) + X[1] * k(B2[1, 4]),
+        S[0] * k(B0[0, 5]) + S[1] * k(B0[1, 5]) + S[2] * k(B0[2, 5]) + X[2] * k(B2[2, 5]),
+    )
+
+
+def own_kernel(info, z_ref, cols, *refs, section):
+    if section == 1:
+        base_ref, out = refs
+    else:
+        (out,) = refs
+    elems, vel = z_ref.shape[1:]
+    chunks = vel // LANE
+    grid = chunk_grid(info[0], chunks)
+
+    def compute(row):
+        flows = flow_forms(cols, grid, row)
+        for c in range(chunks):
+            z = modes_at(z_ref, row, c)
+            z0, z1, z2, z3, z4, z5 = z
+            even, odd, last = edge_parts(z)
+            gs, g1, gr = flows[c]
+            out0, out1, out2 = [jnp.minimum(g, 0.0) for g in flows[c]]
+            V = [out0 * (even[i] - odd[i]) for i in range(3)]
+            W = [out1 * (even[i] + odd[i]) for i in range(3)]
+            X = [out2 * last[i] for i in range(3)]
+            h = gr + 2.0 * gs
+            volume = (
+                None,
+                (gr * z0) * k(KR[1, 0]),
+                (h * z0) * k(KR[2, 0]),
+                gr * (z0 * k(KR[3, 0]) + z1 * k(KR[3, 1])),
+                h * (z0 * k(KR[4, 0]) + z1 * k(KR[4, 1])) + gr * (z2 * k(KR[4, 2])),
+                gr * (z0 * k(KR[5, 0]) + z1 * k(KR[5, 1])) + h * (z2 * k(KR[5, 2])),
+            )
+            surface = lifted(V, W, X)
+            for j in range(MODES):
+                value = z[j] + surface[j]
+                if j:
+                    value = value + volume[j]
+                if section == 1:
+                    value = 0.5 * (base_ref[(j, *at(row, c))] + value)
+                out[(j, *at(row, c))] = value
+
+    over_groups(elems, compute, 2)
+
+
+def mean_kernel(offsets, src, info, _, z_ref, own, near_in, far_in, cols, nus, *refs, section):
     forms = refs[:3]
     refs = refs[3:]
-    base_ref = None
-    if section == 1:
-        base_ref = refs[0]
-        refs = refs[1:]
-    tbl, centre, high, near, far, mtbl, stage_a, stage_b, stage = refs
+    tbl, mtbl, centre, high, near, far, stage_a, stage_b, stage = refs
     elems, vel = z_ref.shape[1:]
     chunks = vel // LANE
     slots = offsets.shape[1]
@@ -438,21 +490,17 @@
                 copy_rows(tbl, stage, src[m, row + i], (m * SUB + i) * chunks, chunks)
 
     def compute(row, stage):
-        flows = flow_forms(cols, grid, row)
-        nu_cols = [jnp.broadcast_to(nus[pl.ds(row, SUB), n : n + 1], (SUB, LANE)) for n in range(3, MODES)]
+        flows = flow_forms(cols, grid, row, section == 1)
+        nu_cols = [nus[n, pl.ds(row, SUB), :] for n in range(3, MODES)]
         for c in range(chunks):
             z0, z1, z2, z3, z4, z5 = modes_at(z_ref, row, c)
-            own = level0((z0, z1, z2, z3, z4, z5))
             through = None
             for m in range(3):
-                g = flows[c][m]
-                value = g * jnp.where(
-                    g < 0.0, own[m], stage[pl.ds(m * SUB * chunks + c, SUB, stride=chunks), :]
-                )
+                value = jnp.maximum(flows[c][m], 0.0) * stage[
+                    pl.ds(m * SUB * chunks + c, SUB, stride=chunks), :
+                ]
                 through = value if through is None else through + value
-            moved = z0 + through * k(EDGE[0, 0, 0])
-            if section == 1:
-                moved = 0.5 * (base_ref[(0, *at(row, c))] + moved)
+            moved = own[(0, *at(row, c))] + through * k(EDGE[0, 0, 0])
             a0 = z0 * k(N[0, 0])
             e34 = a0 + z1 * k(N[3, 1]) + z3 * k(N[3, 3]) + z5 * k(N[3, 5])
             o34 = z2 * k(N[4, 2]) + z4 * k(N[4, 4])
@@ -486,11 +534,7 @@
     over_groups(slots, pack)
 
 
-def rest_kernel(src, info, tbl0, _, z_ref, near, far, high, spreads, nus, basis, cols, *refs, section):
-    base_ref = None
-    if section == 1:
-        base_ref = refs[0]
-        refs = refs[1:]
+def rest_kernel(src, info, tbl0, _, z_ref, own, near, far, high, spreads, nus, basis, cols, *refs, section):
     tbl, out, sizes, stage_a, stage_b, *forms = refs
     elems, vel = z_ref.shape[1:]
     chunks = vel // LANE
@@ -511,7 +555,7 @@
         forms[i][...] = jnp.dot(
             spreads[i], basis[:, pl.ds(0, 3 * vel)], preferred_element_type=f32
         )
-    N, V, B0, B2 = NODAL, INVERSE, EDGE[0], EDGE[2]
+    N, V = NODAL, INVERSE
     grid = chunk_grid(info[0], chunks)
 
     def fetch(row, stage):
@@ -523,8 +567,8 @@
                 copy_rows(tbl, stage, 2 * start, to + chunks, 2 * chunks)
 
     def compute(row, stage):
-        flows = flow_forms(cols, grid, row)
-        nu_cols = [jnp.broadcast_to(nus[pl.ds(row, SUB), n : n + 1], (SUB, LANE)) for n in range(3)]
+        flows = flow_forms(cols, grid, row, section == 1)
+        nu_cols = [nus[n, pl.ds(row, SUB), :] for n in range(3)]
         for c in range(chunks):
             z = modes_at(z_ref, row, c)
             z0, z1, z2, z3, z4, z5 = z
@@ -532,50 +576,16 @@
             def beside(m, level):
                 return stage[pl.ds(m * SUB * pitch + level * chunks + c, SUB, stride=pitch), :]
 
-            even, odd, last = edge_parts(z)
-            gs, g1, gr = flows[c]
-            out0 = gs < 0.0
-            out1 = g1 < 0.0
-            out2 = gr < 0.0
-            V0 = [gs * jnp.where(out0, even[i] - odd[i], beside(0, i)) for i in range(3)]
-            W0 = [
-                g1 * jnp.where(out1, even[0] + odd[0], beside(1, 0)),
-                g1 * jnp.where(out1, even[1] + odd[1], -beside(1, 1)),
-                g1 * jnp.where(out1, even[2] + odd[2], beside(1, 2)),
-            ]
-            X = [gr * jnp.where(out2, last[i], beside(2, i)) for i in range(3)]
-            S = [a + b for a, b in zip(V0, W0)]
-            D = [b - a for a, b in zip(V0, W0)]
-            h = gr + 2.0 * gs
-            moved = [
-                z1 + S[0] * k(B0[0, 1]) + S[1] * k(B0[1, 1]) + X[0] * k(B2[0, 1]) + (gr * z0) * k(KR[1, 0]),
-                z2 + D[0] * k(-B0[0, 2]) + D[1] * k(-B0[1, 2]) + X[1] * k(B2[1, 2]) + (h * z0) * k(KR[2, 0]),
-                z3
-                + S[0] * k(B0[0, 3])
-                + S[1] * k(B0[1, 3])
-                + S[2] * k(B0[2, 3])
-                + X[0] * k(B2[0, 3])
-                + gr * (z0 * k(KR[3, 0]) + z1 * k(KR[3, 1])),
-                z4
-                + D[0] * k(-B0[0, 4])
-                + D[1] * k(-B0[1, 4])
-                + D[2] * k(-B0[2, 4])
-                + X[1] * k(B2[1, 4])
-                + h * (z0 * k(KR[4, 0]) + z1 * k(KR[4, 1]))
-                + gr * (z2 * k(KR[4, 2])),
-                z5
-                + S[0] * k(B0[0, 5])
-                + S[1] * k(B0[1, 5])
-                + S[2] * k(B0[2, 5])
-                + X[2] * k(B2[2, 5])
-                + gr * (z0 * k(KR[5, 0]) + z1 * k(KR[5, 1]))
-                + h * (z2 * k(KR[5, 2])),
-            ]
-            if section == 1:
-                moved = [0.5 * (base_ref[(j + 1, *at(row, c))] + moved[j]) for j in range(5)]
-            e02 = last[0] + z5 * k(N[0, 5])
+            in0, in1, in2 = [jnp.maximum(g, 0.0) for g in flows[c]]
+            V_in = [in0 * beside(0, i) for i in range(3)]
+            W_in = [in1 * beside(1, 0), -(in1 * beside(1, 1)), in1 * beside(1, 2)]
+            X_in = [in2 * beside(2, i) for i in range(3)]
+            surface = lifted(V_in, W_in, X_in)
+            moved = [own[(j + 1, *at(row, c))] + surface[j + 1] for j in range(5)]
+            a0 = z0 * k(N[0, 0])
+            e02 = a0 + z1 * k(N[0, 1]) + z3 * k(N[0, 3]) + z5 * k(N[0, 5])
             o02 = z2 * k(N[2, 2]) + z4 * k(N[2, 4])
-            inside = (e02 - o02, z0 * k(N[0, 0]) + z1 * k(N[1, 1]) + z3 * k(N[1, 3]), e02 + o02)
+            inside = (e02 - o02, a0 + z1 * k(N[1, 1]) + z3 * k(N[1, 3]), e02 + o02)
             H = [relaxed(forms, n, row, c, vel, nu_cols[n], inside[n]) for n in range(3)]
             H += [high[(n, *at(row, c))] for n in range(3)]
             s02 = H[0] + H[2]
@@ -615,21 +625,15 @@
     pipelined_groups(elems, (stage_a, stage_b), fetch, compute)
 
 
-def limit_kernel(away, info, centre, rest, sizes, near, far, out, *refs, section):
+def limit_kernel(away, info, _, centre, rest, sizes, near, far, mtbl, out, *refs, section):
     if section == 0:
-        mom, mtbl, stage_a, stage_b = refs
+        mom, stage_a, stage_b = refs
         target = out
     else:
-        mtbl, stage_a, stage_b, target, sems = refs
+        stage_a, stage_b, target, sems = refs
     elems, vel = centre.shape
     chunks = vel // LANE
     slots = near.shape[0]
-
-    def fill(row):
-        for c in range(chunks):
-            mtbl[pl.ds(row * chunks + c, SUB, stride=chunks), :] = centre[at(row, c)]
-
-    over_groups(elems, fill)
 
     def fill_border(row):
         for side, halo in zip(sides(info), (near, far)):
@@ -722,7 +726,6 @@
     one = S((slots, vel), f32)
     halo = S((3, slots, vel), f32)
     mom = S((modes * SUB, elems), f32)
-    columns = S((elems, LANE), f32)
     smem = pl.BlockSpec(memory_space=pltpu.SMEM)
     vmem = pl.BlockSpec(memory_space=pltpu.VMEM)
     hbm = pl.BlockSpec(memory_space=pltpu.HBM)
@@ -745,7 +748,7 @@
             index,
             S((4, slots), jnp.int32),
             S((TERMS * SUB, modes * vel), bf16),
-            columns,
+            S((4, elems, LANE), f32),
         ),
         in_specs=[smem, smem] + [vmem] * 3,
         out_specs=(vmem,) * 5,
@@ -776,61 +779,75 @@
             name="trace",
         )(offsets, info, current)
         near, far, paired = lax.optimization_barrier((near, far, paired))
+        near = traded(near, True)
         far = traded(far, False)
-        near = traded(near, True)
         parts = moment_parts(paired)
 
         base = [] if opening else [start]
+        own = pl.pallas_call(
+            lambda *refs, section=section: own_kernel(*refs, section=section),
+            out_shape=state,
+            in_specs=[smem] + [vmem] * (2 + len(base)),
+            out_specs=vmem,
+            compiler_params=params(4),
+            name=f"own{section}",
+        )(info, current, cols, *base)
         spreads, nus, *forms = pl.pallas_call(
             lambda *refs, section=section: form_kernel(*refs, parts=len(parts), section=section),
-            out_shape=(S((3, elems, TERMS * SUB), bf16), columns) + (S((elems, 3 * vel), f32),) * 3,
+            out_shape=(S((3, elems, TERMS * SUB), bf16), S((modes, elems, LANE), f32)) + (S((elems, 3 * vel), f32),) * 3,
             in_specs=[vmem] * (len(parts) + 2),
             out_specs=(vmem,) * 5,
             compiler_params=params(16),
             name=f"form{section}",
         )(*parts, rate, basis)
 
-        tbl0, centre, high, near_mean, far_mean = pl.pallas_call(
+        tbl0, mean_table, centre, high, near_mean, far_mean = pl.pallas_call(
             lambda *refs, section=section: mean_kernel(*refs, section=section),
-            out_shape=(S((rows * chunks, LANE), f32), S((elems, vel), f32), S((3, elems, vel), f32), one, one),
+            out_shape=(
+                S((rows * chunks, LANE), f32),
+                S(((elems + 2 * slots) * chunks, LANE), f32),
+                S((elems, vel), f32),
+                S((3, elems, vel), f32),
+                one,
+                one,
+            ),
             input_output_aliases={3: 0},
-            in_specs=[smem] * 3 + [vmem] * (9 + len(base)),
-            out_specs=(vmem,) * 5,
-            scratch_shapes=[buffer(elems * chunks)]
-            + [buffer(3 * SUB * chunks)] * 2
-            + [buffer(2 * slots * chunks)],
+            in_specs=[smem] * 3 + [vmem] * 10,
+            out_specs=(vmem,) * 6,
+            scratch_shapes=[buffer(3 * SUB * chunks)] * 2 + [buffer(2 * slots * chunks)],
             compiler_params=params(16),
             name=f"mean{section}",
-        )(offsets, src, info, tbl0, current, near, far, cols, nus, *forms, *base)
+        )(offsets, src, info, tbl0, current, own, near, far, cols, nus, *forms)
+        near_mean = traded(near_mean, True)
         far_mean = traded(far_mean, False)
-        near_mean = traded(near_mean, True)
 
         _, rest, sizes = pl.pallas_call(
             lambda *refs, section=section: rest_kernel(*refs, section=section),
             out_shape=(S((2 * rows * chunks, LANE), f32), S((5, elems, vel), f32), S((2, elems, vel), f32)),
             input_output_aliases={3: 0},
-            in_specs=[smem] * 2 + [vmem] * (10 + len(base)),
+            in_specs=[smem] * 2 + [vmem] * 11,
             out_specs=(vmem,) * 3,
             scratch_shapes=[buffer(9 * SUB * chunks)] * 2 + evaluated(),
             compiler_params=params(20),
             name=f"rest{section}",
-        )(src, info, tbl0, tbl12, current, near, far, high, spreads, nus, basis, cols, *base)
-
-        scratch = [buffer((elems + 2 * slots) * chunks)] + [buffer(3 * SUB * chunks)] * 2
+        )(src, info, tbl0, tbl12, current, own, near, far, high, spreads, nus, basis, cols)
+
+        scratch = [buffer(3 * SUB * chunks)] * 2
         if not opening:
             scratch += [pltpu.VMEM(state.shape, f32), pltpu.SemaphoreType.DMA((4,))]
         made = pl.pallas_call(
             lambda *refs, section=section: limit_kernel(*refs, section=section),
-            out_shape=(state, mom) if opening else (state,),
-            in_specs=[smem, smem] + [vmem] * 5,
-            out_specs=(vmem, vmem) if opening else (hbm,),
+            out_shape=(S(mean_table.shape, f32), state) + ((mom,) if opening else ()),
+            in_specs=[smem, smem] + [vmem] * 6,
+            out_specs=(vmem,) * 3 if opening else (vmem, hbm),
+            input_output_aliases={2: 0},
             scratch_shapes=scratch,
             compiler_params=params(8),
             name=f"limit{section}",
-        )(away, info, centre, rest, sizes, near_mean, far_mean)
+        )(away, info, mean_table, centre, rest, sizes, near_mean, far_mean)
         if opening:
-            current, partial = made
-    return made[0]
+            _, current, partial = made
+    return made[1]
 
 
 def solution(mesh):

time: 72.7 us -> 68.3 us (0.939)
  waiting for transfers between devices: 6.72 us -> 0.9 us
  Pallas kernels: 39.1 us -> 40.6 us
    pallas_call x0 -> x2, Pallas kernels: none -> 6.15 us  [on_device(): pl.pallas_call(lambda *refs, section=section: own_kernel(*refs, section=s...]
    ppermute x8, waiting for transfers between devices: 6.7 us -> 0.87 us  [swapped(): return lax.ppermute(value, 'vel', [(i, i ^ bits) for i in range(peers)])]
    pallas_call x2, Pallas kernels: 14.5 us -> 11.6 us  [on_device(): pl.pallas_call(lambda *refs, section=section: rest_kernel(*refs, section=...]
    pallas_call x2, Pallas kernels: 8.33 us -> 6.42 us  [on_device(): pl.pallas_call(lambda *refs, section=section: mean_kernel(*refs, section=...]
  transfers between devices with their start and end apart: 16 -> 16, of which waited for: 5 -> 2; matrix products, arithmetic and copies ran while one was open for 0% -> 0% of each run, Pallas kernels for 31% -> 38%
where the time goes in v2:
time: 68.3 us; the launch traced here: 68 us
  Pallas kernels  40.6 us (59%)
  starting transfers between devices  24.3 us (36%)
  local copies, waits for them, and re-layouts  1.91 us (3%)
  waiting for transfers between devices  0.9 us (1%)
    ppermute x8, starting transfers between devices, traded(): return lax.ppermute(value, 'space', pairs)  14.6 us
    pallas_call x2, Pallas kernels, on_device(): pl.pallas_call(lambda *refs, section=section: rest_kernel(*refs, section=...  11.6 us
    ppermute x8, starting transfers between devices, swapped(): return lax.ppermute(value, 'vel', [(i, i ^ bits) for i in range(peers)])  9.72 us
    pallas_call x2, Pallas kernels, on_device(): pl.pallas_call(lambda *refs, section=section: limit_kernel(*refs, section...  6.75 us
    pallas_call x2, Pallas kernels, on_device(): pl.pallas_call(lambda *refs, section=section: mean_kernel(*refs, section=...  6.42 us
    pallas_call x2, Pallas kernels, on_device(): pl.pallas_call(lambda *refs, section=section: own_kernel(*refs, section=s...  6.15 us
    pallas_call x2, Pallas kernels, on_device(): pl.pallas_call(trace_kernel, out_shape=(S((rows * chunks, LANE), f32), S(...  4.6 us
    unnamed x12, local copies, waits for them, and re-layouts  1.91 us
  transfers between devices with their start and end apart: 16, of which 2 were waited for; matrix products, arithmetic and copies ran while one was open for 0% of the time, Pallas kernels for 38%

profile of v2, /device:TPU:1, one launch (start us, length us, event | category | flops | bytes accessed | tf_op | source)
XLA Modules:
  0.0 68.0 jit_solution(9953164359589282251)
XLA Ops:
  0.0 0.1 pad_add_fusion.info.refs_0_.refs_2_.refs_1_
  0.1 1.9 %copy-done = f32[6,256,512]{2,1,0:T(8,128)S(1)} copy-done((f32[6,256,512]{2,1,0:T(8,128)S(1)}, f32[6,256,512]{2,1,0:T(8,128)}, u32[]{:S(2)}) %copy-start) | copy-done | bytes 3145752
  2.0 1.5 %first.1 = f32[48,256]{1,0:T(8,128)S(1)} custom-call(s32[2]{0:T(128)S(1)} %pad_add_fusion.info.refs_0_.refs_2_.refs_1_, f32[6,256,512]{2,1,0:T(8,128)S(1)} %copy-done), custom_call_target="tpu_custom_call" | custom-call | tf_op jit(solution)/shard_map/first/pallas_call | solution.py:760
  3.5 2.1 %collective-permute-start = (f32[48,256]{1,0:T(8,128)S(1)}, f32[48,256]{1,0:T(8,128)S(1)}, u32[]{:S(2)}, u32[]{:S(2)}) collective-permute-start(f32[48,256]{1,0:T(8,128)S(1)} %first.1), channel_id=1, source_target_pairs={{0,1},{1,0},{2,3},{3,2},{4,5},{5,4},{6,7},{7,6},{8,9},{9,8},{10,11... | collective-permute-start | bytes 147464 | tf_op jit(solution)/shard_map/ppermute | solution.py:701
  5.6 1.6 %prepare.1 = (s32[3,256]{1,0:T(4,128)S(1)}, s32[3,256]{1,0:T(4,128)S(1)}, s32[4,80]{1,0:T(4,128)S(1)}, bf16[256,3072]{1,0:T(8,128)(2,1)S(1)}, f32[4,256,128]{2,1,0:T(8,128)S(1)}) custom-call(s32[2,80]{1,0:T(2,128)S(1)} %bitcast.8, s32[2]{0:T(128)S(1)} %pad_add_fusion.info.refs_0_.refs_2_.refs_1_, s32[3,256]{1,0:T(4,128)S(1)} %copy-done.4, ...), custom_call_target="tpu_custom_call" | custom-call | tf_op jit(solution)/shard_map/prepare/pallas_call | solution.py:744
  7.2 2.3 %trace.2 = (f32[3712,128]{1,0:T(8,128)S(1)}, f32[7424,128]{1,0:T(8,128)S(1)}, f32[3,80,512]{2,1,0:T(8,128)S(1)}, f32[3,80,512]{2,1,0:T(8,128)S(1)}) custom-call(s32[4,80]{1,0:T(4,128)S(1)} %get-tuple-element.54.offsets.refs_0_, s32[2]{0:T(128)S(1)} %pad_add_fusion.info.refs_0_.refs_2_.refs_1_, f32[6,256,512]{2,1,0:T(8,128)S(1)} %copy-done.1), custom_call_target="tpu_custom_call" | custom-call | tf_op jit(solution)/shard_map/trace/pallas_call | solution.py:772
  9.5 0.0 collective-permute-done
  9.6 1.0 %collective-permute-start.1 = (f32[3,80,512]{2,1,0:T(8,128)S(1)}, f32[3,80,512]{2,1,0:T(8,128)S(1)}, u32[]{:S(2)}, u32[]{:S(2)}) collective-permute-start(f32[3,80,512]{2,1,0:T(8,128)S(1)} %get-tuple-element.60), channel_id=1, source_target_pairs={{0,8},{8,0},{16,24},{24,16},{1,9},{9,1},{17,25},{25,17},{2,10},{10... | collective-permute-start | bytes 1474568 | tf_op jit(solution)/shard_map/ppermute | solution.py:696
  10.6 3.0 %collective-permute-start.2 = (f32[3,80,512]{2,1,0:T(8,128)S(1)}, f32[3,80,512]{2,1,0:T(8,128)S(1)}, u32[]{:S(2)}, u32[]{:S(2)}) collective-permute-start(f32[3,80,512]{2,1,0:T(8,128)S(1)} %get-tuple-element.61), channel_id=1, source_target_pairs={{8,16},{16,8},{9,17},{17,9},{10,18},{18,10},{11,19},{19,11},{12,20... | collective-permute-start | bytes 1474568 | tf_op jit(solution)/shard_map/ppermute | solution.py:696
  13.6 3.4 %collective-permute-start.5 = (f32[48,256]{1,0:T(8,128)S(1)}, f32[48,256]{1,0:T(8,128)S(1)}, u32[]{:S(2)}, u32[]{:S(2)}) collective-permute-start(f32[48,256]{1,0:T(8,128)S(1)} %add.11.refs_0_), channel_id=1, source_target_pairs={{0,6},{1,7},{2,4},{3,5},{4,2},{5,3},{6,0},{7,1},{8,14},{9,15},{10,... | collective-permute-start | bytes 147464 | tf_op jit(solution)/shard_map/ppermute | solution.py:701
  17.0 0.0 collective-permute-start.4
  17.0 0.4 collective-permute-start.3
  17.4 3.0 %own0.1.refs_5_ = f32[6,256,512]{2,1,0:T(8,128)S(1)} custom-call(s32[2]{0:T(128)S(1)} %pad_add_fusion.info.refs_0_.refs_2_.refs_1_, f32[6,256,512]{2,1,0:T(8,128)S(1)} %copy-done.1, f32[4,256,128]{2,1,0:T(8,128)S(1)} %get-tuple-element.57.refs_2_.refs_8_.refs_12_), custom_call_target="tpu_custom_call" | custom-call | tf_op jit(solution)/shard_map/own0/pallas_call | solution.py:787
  20.4 0.0 collective-permute-done.5.refs_3_
  20.4 0.5 collective-permute-done.4.refs_2_
  20.9 0.0 collective-permute-done.3.refs_1_
  20.9 0.9 %form0.1 = (bf16[3,256,256]{2,1,0:T(8,128)(2,1)S(1)}, f32[6,256,128]{2,1,0:T(8,128)S(1)}, f32[256,1536]{1,0:T(8,128)S(1)}, f32[256,1536]{1,0:T(8,128)S(1)}, f32[256,1536]{1,0:T(8,128)S(1)}) custom-call(f32[48,256]{1,0:T(8,128)S(1)} %add.11.refs_0_, f32[48,256]{1,0:T(8,128)S(1)} %collective-permute-done.3.refs_1_, ...), custom_call_target="tpu_custom_call" | custom-call | tf_op jit(solution)/shard_map/form0/pallas_call | solution.py:795
  21.8 0.0 collective-permute-done.1.refs_6_
  21.8 0.0 collective-permute-done.2.refs_7_
  21.8 3.2 %mean0.1 = (f32[3712,128]{1,0:T(8,128)S(1)}, f32[1664,128]{1,0:T(8,128)S(1)}, f32[256,512]{1,0:T(8,128)S(1)}, f32[3,256,512]{2,1,0:T(8,128)S(1)}, f32[80,512]{1,0:T(8,128)S(1)}, /*index=5*/f32[80,512]{1,0:T(8,128)S(1)}) custom-call(s32[4,80]{1,0:T(4,128)S(1)} %get-tuple-element.54.offsets.refs_0_, ...), custom_call_target="tpu_custom_call", output_to_operand_aliasing={{0}: (3, {})} | custom-call | tf_op jit(solution)/shard_map/mean0/pallas_call | solution.py:804
  25.1 0.1 collective-permute-start.6
  25.1 3.9 %collective-permute-start.7 = (f32[80,512]{1,0:T(8,128)S(1)}, f32[80,512]{1,0:T(8,128)S(1)}, u32[]{:S(2)}, u32[]{:S(2)}) collective-permute-start(f32[80,512]{1,0:T(8,128)S(1)} %get-tuple-element.77), channel_id=1, source_target_pairs={{8,16},{16,8},{9,17},{17,9},{10,18},{18,10},{11,19},{19,11},{12,20... | collective-permute-start | bytes 491528 | tf_op jit(solution)/shard_map/ppermute | solution.py:696
  29.1 5.8 %rest0.1 = (f32[7424,128]{1,0:T(8,128)S(1)}, f32[5,256,512]{2,1,0:T(8,128)S(1)}, f32[2,256,512]{2,1,0:T(8,128)S(1)}) custom-call(s32[3,256]{1,0:T(4,128)S(1)} %get-tuple-element.55.refs_1_.refs_0_, s32[2]{0:T(128)S(1)} %pad_add_fusion.info.refs_0_.refs_2_.refs_1_, f32[3712,128]{1,0:T(8,128)S(1)} %get-tuple-element.70.refs_2_, ...), custom_call_target="tpu_custom_call", output_to_operand_aliasing={{0}: (3, {})} | custom-call | tf_op jit(solution)/shard_map/rest0/pallas_call | solution.py:824
  34.9 0.0 collective-permute-done.6.refs_6_
  34.9 0.0 collective-permute-done.7.refs_7_
  34.9 3.4 %limit0.1 = (f32[1664,128]{1,0:T(8,128)S(1)}, f32[6,256,512]{2,1,0:T(8,128)S(1)}, f32[48,256]{1,0:T(8,128)S(1)}) custom-call(s32[3,256]{1,0:T(4,128)S(1)} %get-tuple-element.53.refs_0_, s32[2]{0:T(128)S(1)} %pad_add_fusion.info.refs_0_.refs_2_.refs_1_, f32[1664,128]{1,0:T(8,128)S(1)} %get-tuple-element.68.refs_2_, ...), custom_call_target="tpu_custom_call", output_to_operand_aliasing={{0}: (2, {})} | custom-call | tf_op jit(solution)/shard_map/limit0/pallas_call | solution.py:838
  38.3 0.3 collective-permute-start.8
  38.6 2.3 %trace.3 = (f32[3712,128]{1,0:T(8,128)S(1)}, f32[7424,128]{1,0:T(8,128)S(1)}, f32[3,80,512]{2,1,0:T(8,128)S(1)}, f32[3,80,512]{2,1,0:T(8,128)S(1)}) custom-call(s32[4,80]{1,0:T(4,128)S(1)} %get-tuple-element.54.offsets.refs_0_, s32[2]{0:T(128)S(1)} %pad_add_fusion.info.refs_0_.refs_2_.refs_1_, f32[6,256,512]{2,1,0:T(8,128)S(1)} %get-tuple-element.78.z_ref.refs_1_.refs_4_), custom_call_target="tpu_custom_call" | custom-call | tf_op jit(solution)/shard_map/trace/pallas_call | solution.py:772
  40.9 0.4 collective-permute-done.8
  41.3 0.1 collective-permute-start.9
  41.3 3.1 %collective-permute-start.10 = (f32[3,80,512]{2,1,0:T(8,128)S(1)}, f32[3,80,512]{2,1,0:T(8,128)S(1)}, u32[]{:S(2)}, u32[]{:S(2)}) collective-permute-start(f32[3,80,512]{2,1,0:T(8,128)S(1)} %get-tuple-element.84), channel_id=1, source_target_pairs={{8,16},{16,8},{9,17},{17,9},{10,18},{18,10},{11,19},{19,11},{12,20... | collective-permute-start | bytes 1474568 | tf_op jit(solution)/shard_map/ppermute | solution.py:696
  44.4 2.5 %collective-permute-start.13 = (f32[48,256]{1,0:T(8,128)S(1)}, f32[48,256]{1,0:T(8,128)S(1)}, u32[]{:S(2)}, u32[]{:S(2)}) collective-permute-start(f32[48,256]{1,0:T(8,128)S(1)} %add.12.refs_0_), channel_id=1, source_target_pairs={{0,6},{1,7},{2,4},{3,5},{4,2},{5,3},{6,0},{7,1},{8,14},{9,15},{10,... | collective-permute-start | bytes 147464 | tf_op jit(solution)/shard_map/ppermute | solution.py:701
  46.9 0.0 collective-permute-start.12
  47.0 1.1 %collective-permute-start.11 = (f32[48,256]{1,0:T(8,128)S(1)}, f32[48,256]{1,0:T(8,128)S(1)}, u32[]{:S(2)}, u32[]{:S(2)}) collective-permute-start(f32[48,256]{1,0:T(8,128)S(1)} %add.12.refs_0_), channel_id=1, source_target_pairs={{0,2},{1,3},{2,0},{3,1},{4,6},{5,7},{6,4},{7,5},{8,10},{9,11},{10,... | collective-permute-start | bytes 147464 | tf_op jit(solution)/shard_map/ppermute | solution.py:701
  48.1 3.2 %own1.1.refs_5_ = f32[6,256,512]{2,1,0:T(8,128)S(1)} custom-call(s32[2]{0:T(128)S(1)} %pad_add_fusion.info.refs_0_.refs_2_.refs_1_, f32[6,256,512]{2,1,0:T(8,128)S(1)} %get-tuple-element.78.z_ref.refs_1_.refs_4_, f32[4,256,128]{2,1,0:T(8,128)S(1)} %get-tuple-element.57.refs_2_.refs_8_.refs_12_, f32[6,256,512]{2,1,0:T(8,128)S(1)} %copy-done.1), custom_call_target="tpu_custom_call" | custom-call | tf_op jit(solution)/shard_map/own1/pallas_call | solution.py:787
  51.2 0.0 collective-permute-done.13.refs_3_
  51.2 0.0 collective-permute-done.12.refs_2_
  51.2 0.0 collective-permute-done.11.refs_1_
  51.3 0.9 %form1.1 = (bf16[3,256,256]{2,1,0:T(8,128)(2,1)S(1)}, f32[6,256,128]{2,1,0:T(8,128)S(1)}, f32[256,1536]{1,0:T(8,128)S(1)}, f32[256,1536]{1,0:T(8,128)S(1)}, f32[256,1536]{1,0:T(8,128)S(1)}) custom-call(f32[48,256]{1,0:T(8,128)S(1)} %add.12.refs_0_, f32[48,256]{1,0:T(8,128)S(1)} %collective-permute-done.11.refs_1_, ...), custom_call_target="tpu_custom_call" | custom-call | tf_op jit(solution)/shard_map/form1/pallas_call | solution.py:795
  52.2 0.0 collective-permute-done.9.refs_6_
  52.2 0.0 collective-permute-done.10.refs_7_
  52.2 3.2 %mean1.1 = (f32[3712,128]{1,0:T(8,128)S(1)}, f32[1664,128]{1,0:T(8,128)S(1)}, f32[256,512]{1,0:T(8,128)S(1)}, f32[3,256,512]{2,1,0:T(8,128)S(1)}, f32[80,512]{1,0:T(8,128)S(1)}, /*index=5*/f32[80,512]{1,0:T(8,128)S(1)}) custom-call(s32[4,80]{1,0:T(4,128)S(1)} %get-tuple-element.54.offsets.refs_0_, ...), custom_call_target="tpu_custom_call", output_to_operand_aliasing={{0}: (3, {})} | custom-call | tf_op jit(solution)/shard_map/mean1/pallas_call | solution.py:804
  55.4 0.2 collective-permute-start.14
  55.6 3.2 %collective-permute-start.15 = (f32[80,512]{1,0:T(8,128)S(1)}, f32[80,512]{1,0:T(8,128)S(1)}, u32[]{:S(2)}, u32[]{:S(2)}) collective-permute-start(f32[80,512]{1,0:T(8,128)S(1)} %get-tuple-element.99), channel_id=1, source_target_pairs={{8,16},{16,8},{9,17},{17,9},{10,18},{18,10},{11,19},{19,11},{12,20... | collective-permute-start | bytes 491528 | tf_op jit(solution)/shard_map/ppermute | solution.py:696
  58.8 5.9 %rest1.1 = (f32[7424,128]{1,0:T(8,128)S(1)}, f32[5,256,512]{2,1,0:T(8,128)S(1)}, f32[2,256,512]{2,1,0:T(8,128)S(1)}) custom-call(s32[3,256]{1,0:T(4,128)S(1)} %get-tuple-element.55.refs_1_.refs_0_, s32[2]{0:T(128)S(1)} %pad_add_fusion.info.refs_0_.refs_2_.refs_1_, f32[3712,128]{1,0:T(8,128)S(1)} %get-tuple-element.92.refs_2_, ...), custom_call_target="tpu_custom_call", output_to_operand_aliasing={{0}: (3, {})} | custom-call | tf_op jit(solution)/shard_map/rest1/pallas_call | solution.py:824
  64.7 0.0 collective-permute-done.14.refs_6_
  64.7 0.0 collective-permute-done.15.refs_7_
  64.7 3.3 %limit1.1 = (f32[1664,128]{1,0:T(8,128)S(1)}, f32[6,256,512]{2,1,0:T(8,128)}) custom-call(s32[3,256]{1,0:T(4,128)S(1)} %get-tuple-element.53.refs_0_, s32[2]{0:T(128)S(1)} %pad_add_fusion.info.refs_0_.refs_2_.refs_1_, f32[1664,128]{1,0:T(8,128)S(1)} %get-tuple-element.90.refs_2_, ...), custom_call_target="tpu_custom_call", output_to_operand_aliasing={{0}: (2, {})} | custom-call | tf_op jit(solution)/shard_map/limit1/pallas_call | solution.py:838
  (13 shorter events, 0.0 us)
Async XLA Ops:
  0.0 5.6 %copy-start.5 = (s32[1,2,80]{2,1,0:T(2,128)S(1)}, s32[1,2,80]{2,1,0:T(2,128)}, u32[]{:S(2)}) copy-start(s32[1,2,80]{2,1,0:T(2,128)} %param.8) | copy-start | bytes 1924
  0.0 5.6 %copy-start.4 = (s32[3,256]{1,0:T(4,128)S(1)}, s32[3,256]{1,0:T(4,128)}, u32[]{:S(2)}) copy-start(s32[3,256]{1,0:T(4,128)} %neigh_ref.1) | copy-start | bytes 9220
  0.0 5.6 %copy-start.2 = (f32[2,3,256]{2,0,1:T(2,128)S(1)}, f32[2,3,256]{2,0,1:T(2,128)}, u32[]{:S(2)}) copy-start(f32[2,3,256]{2,0,1:T(2,128)} %param.6) | copy-start | bytes 18436
  0.1 1.9 %copy-start = (f32[6,256,512]{2,1,0:T(8,128)S(1)}, f32[6,256,512]{2,1,0:T(8,128)}, u32[]{:S(2)}) copy-start(f32[6,256,512]{2,1,0:T(8,128)} %refs_3_.1) | copy-start | bytes 9437188
  2.0 5.2 %copy-start.1 = (f32[6,256,512]{2,1,0:T(8,128)S(1)}, f32[6,256,512]{2,1,0:T(8,128)}, u32[]{:S(2)}) copy-start(f32[6,256,512]{2,1,0:T(8,128)} %refs_3_.1) | copy-start | bytes 9437188
  3.5 6.0 %collective-permute-start = (f32[48,256]{1,0:T(8,128)S(1)}, f32[48,256]{1,0:T(8,128)S(1)}, u32[]{:S(2)}, u32[]{:S(2)}) collective-permute-start(f32[48,256]{1,0:T(8,128)S(1)} %first.1), channel_id=1, source_target_pairs={{0,1},{1,0},{2,3},{3,2},{4,5},{5,4},{6,7},{7,6},{8,9},{9,8},{10,11... | collective-permute-start | bytes 147464 | tf_op jit(solution)/shard_map/ppermute | solution.py:701
  9.6 12.2 %collective-permute-start.1 = (f32[3,80,512]{2,1,0:T(8,128)S(1)}, f32[3,80,512]{2,1,0:T(8,128)S(1)}, u32[]{:S(2)}, u32[]{:S(2)}) collective-permute-start(f32[3,80,512]{2,1,0:T(8,128)S(1)} %get-tuple-element.60), channel_id=1, source_target_pairs={{0,8},{8,0},{16,24},{24,16},{1,9},{9,1},{17,25},{25,17},{2,10},{10... | collective-permute-start | bytes 1474568 | tf_op jit(solution)/shard_map/ppermute | solution.py:696
  10.6 11.2 %collective-permute-start.2 = (f32[3,80,512]{2,1,0:T(8,128)S(1)}, f32[3,80,512]{2,1,0:T(8,128)S(1)}, u32[]{:S(2)}, u32[]{:S(2)}) collective-permute-start(f32[3,80,512]{2,1,0:T(8,128)S(1)} %get-tuple-element.61), channel_id=1, source_target_pairs={{8,16},{16,8},{9,17},{17,9},{10,18},{18,10},{11,19},{19,11},{12,20... | collective-permute-start | bytes 1474568 | tf_op jit(solution)/shard_map/ppermute | solution.py:696
  13.6 6.7 %collective-permute-start.5 = (f32[48,256]{1,0:T(8,128)S(1)}, f32[48,256]{1,0:T(8,128)S(1)}, u32[]{:S(2)}, u32[]{:S(2)}) collective-permute-start(f32[48,256]{1,0:T(8,128)S(1)} %add.11.refs_0_), channel_id=1, source_target_pairs={{0,6},{1,7},{2,4},{3,5},{4,2},{5,3},{6,0},{7,1},{8,14},{9,15},{10,... | collective-permute-start | bytes 147464 | tf_op jit(solution)/shard_map/ppermute | solution.py:701
  17.0 3.8 %collective-permute-start.4 = (f32[48,256]{1,0:T(8,128)S(1)}, f32[48,256]{1,0:T(8,128)S(1)}, u32[]{:S(2)}, u32[]{:S(2)}) collective-permute-start(f32[48,256]{1,0:T(8,128)S(1)} %add.11.refs_0_), channel_id=1, source_target_pairs={{0,4},{1,5},{2,6},{3,7},{4,0},{5,1},{6,2},{7,3},{8,12},{9,13},{10,... | collective-permute-start | bytes 147464 | tf_op jit(solution)/shard_map/ppermute | solution.py:701
  17.0 3.8 %collective-permute-start.3 = (f32[48,256]{1,0:T(8,128)S(1)}, f32[48,256]{1,0:T(8,128)S(1)}, u32[]{:S(2)}, u32[]{:S(2)}) collective-permute-start(f32[48,256]{1,0:T(8,128)S(1)} %add.11.refs_0_), channel_id=1, source_target_pairs={{0,2},{1,3},{2,0},{3,1},{4,6},{5,7},{6,4},{7,5},{8,10},{9,11},{10,... | collective-permute-start | bytes 147464 | tf_op jit(solution)/shard_map/ppermute | solution.py:701
  17.4 3.5 %copy-start.3 = (f32[256]{0:T(256)S(1)}, f32[256]{0:T(256)}, u32[]{:S(2)}) copy-start(f32[256]{0:T(256)} %param.9) | copy-start | bytes 3076
  25.1 9.8 %collective-permute-start.6 = (f32[80,512]{1,0:T(8,128)S(1)}, f32[80,512]{1,0:T(8,128)S(1)}, u32[]{:S(2)}, u32[]{:S(2)}) collective-permute-start(f32[80,512]{1,0:T(8,128)S(1)} %get-tuple-element.76), channel_id=1, source_target_pairs={{0,8},{8,0},{16,24},{24,16},{1,9},{9,1},{17,25},{25,17},{2,10},{10... | collective-permute-start | bytes 491528 | tf_op jit(solution)/shard_map/ppermute | solution.py:696
  25.1 9.7 %collective-permute-start.7 = (f32[80,512]{1,0:T(8,128)S(1)}, f32[80,512]{1,0:T(8,128)S(1)}, u32[]{:S(2)}, u32[]{:S(2)}) collective-permute-start(f32[80,512]{1,0:T(8,128)S(1)} %get-tuple-element.77), channel_id=1, source_target_pairs={{8,16},{16,8},{9,17},{17,9},{10,18},{18,10},{11,19},{19,11},{12,20... | collective-permute-start | bytes 491528 | tf_op jit(solution)/shard_map/ppermute | solution.py:696
  38.3 3.0 %collective-permute-start.8 = (f32[48,256]{1,0:T(8,128)S(1)}, f32[48,256]{1,0:T(8,128)S(1)}, u32[]{:S(2)}, u32[]{:S(2)}) collective-permute-start(f32[48,256]{1,0:T(8,128)S(1)} %get-tuple-element.82), channel_id=1, source_target_pairs={{0,1},{1,0},{2,3},{3,2},{4,5},{5,4},{6,7},{7,6},{8,9},{9,8},{10,11... | collective-permute-start | bytes 147464 | tf_op jit(solution)/shard_map/ppermute | solution.py:701
  41.3 10.9 %collective-permute-start.9 = (f32[3,80,512]{2,1,0:T(8,128)S(1)}, f32[3,80,512]{2,1,0:T(8,128)S(1)}, u32[]{:S(2)}, u32[]{:S(2)}) collective-permute-start(f32[3,80,512]{2,1,0:T(8,128)S(1)} %get-tuple-element.83), channel_id=1, source_target_pairs={{0,8},{8,0},{16,24},{24,16},{1,9},{9,1},{17,25},{25,17},{2,10},{10... | collective-permute-start | bytes 1474568 | tf_op jit(solution)/shard_map/ppermute | solution.py:696
  41.3 10.9 %collective-permute-start.10 = (f32[3,80,512]{2,1,0:T(8,128)S(1)}, f32[3,80,512]{2,1,0:T(8,128)S(1)}, u32[]{:S(2)}, u32[]{:S(2)}) collective-permute-start(f32[3,80,512]{2,1,0:T(8,128)S(1)} %get-tuple-element.84), channel_id=1, source_target_pairs={{8,16},{16,8},{9,17},{17,9},{10,18},{18,10},{11,19},{19,11},{12,20... | collective-permute-start | bytes 1474568 | tf_op jit(solution)/shard_map/ppermute | solution.py:696
  44.4 6.8 %collective-permute-start.13 = (f32[48,256]{1,0:T(8,128)S(1)}, f32[48,256]{1,0:T(8,128)S(1)}, u32[]{:S(2)}, u32[]{:S(2)}) collective-permute-start(f32[48,256]{1,0:T(8,128)S(1)} %add.12.refs_0_), channel_id=1, source_target_pairs={{0,6},{1,7},{2,4},{3,5},{4,2},{5,3},{6,0},{7,1},{8,14},{9,15},{10,... | collective-permute-start | bytes 147464 | tf_op jit(solution)/shard_map/ppermute | solution.py:701
  46.9 4.3 %collective-permute-start.12 = (f32[48,256]{1,0:T(8,128)S(1)}, f32[48,256]{1,0:T(8,128)S(1)}, u32[]{:S(2)}, u32[]{:S(2)}) collective-permute-start(f32[48,256]{1,0:T(8,128)S(1)} %add.12.refs_0_), channel_id=1, source_target_pairs={{0,4},{1,5},{2,6},{3,7},{4,0},{5,1},{6,2},{7,3},{8,12},{9,13},{10,... | collective-permute-start | bytes 147464 | tf_op jit(solution)/shard_map/ppermute | solution.py:701
  47.0 4.3 %collective-permute-start.11 = (f32[48,256]{1,0:T(8,128)S(1)}, f32[48,256]{1,0:T(8,128)S(1)}, u32[]{:S(2)}, u32[]{:S(2)}) collective-permute-start(f32[48,256]{1,0:T(8,128)S(1)} %add.12.refs_0_), channel_id=1, source_target_pairs={{0,2},{1,3},{2,0},{3,1},{4,6},{5,7},{6,4},{7,5},{8,10},{9,11},{10,... | collective-permute-start | bytes 147464 | tf_op jit(solution)/shard_map/ppermute | solution.py:701
  55.4 9.3 %collective-permute-start.14 = (f32[80,512]{1,0:T(8,128)S(1)}, f32[80,512]{1,0:T(8,128)S(1)}, u32[]{:S(2)}, u32[]{:S(2)}) collective-permute-start(f32[80,512]{1,0:T(8,128)S(1)} %get-tuple-element.98), channel_id=1, source_target_pairs={{0,8},{8,0},{16,24},{24,16},{1,9},{9,1},{17,25},{25,17},{2,10},{10... | collective-permute-start | bytes 491528 | tf_op jit(solution)/shard_map/ppermute | solution.py:696
  55.6 9.1 %collective-permute-start.15 = (f32[80,512]{1,0:T(8,128)S(1)}, f32[80,512]{1,0:T(8,128)S(1)}, u32[]{:S(2)}, u32[]{:S(2)}) collective-permute-start(f32[80,512]{1,0:T(8,128)S(1)} %get-tuple-element.99), channel_id=1, source_target_pairs={{8,16},{16,8},{9,17},{17,9},{10,18},{18,10},{11,19},{19,11},{12,20... | collective-permute-start | bytes 491528 | tf_op jit(solution)/shard_map/ppermute | solution.py:696

commit v3 on v2

--- a/solution.py
+++ b/solution.py
@@ -119,7 +119,10 @@
     return [ref[(j, *at(row, chunk))] for j in range(ref.shape[0])]
 
 
-def over_groups(count, body, together=1):
+def over_groups(count, body, together=5):
+    while count // SUB % together:
+        together -= 1
+
     def step(g, _):
         for i in range(together):
             body(pl.multiple_of(g * (SUB * together) + i * SUB, SUB))
@@ -134,20 +137,23 @@
         target[pl.ds(to + piece, rows), :] = source[pl.ds(start + piece, rows), :]
 
 
-def pipelined_groups(count, stages, fetch, compute):
+def pipelined_groups(count, stages, fetch, compute, pairs=4):
     last = count - SUB
+    span = 2 * SUB * pairs
     fetch(0, stages[0])
 
-    def step(pair, _):
-        row = pl.multiple_of(pair * (2 * SUB), 2 * SUB)
-        after = pl.multiple_of(row + SUB, SUB)
-        fetch(after, stages[1])
-        compute(row, stages[0])
-        fetch(pl.multiple_of(jnp.minimum(row + 2 * SUB, last), SUB), stages[0])
-        compute(after, stages[1])
+    def step(g, _):
+        start = pl.multiple_of(g * span, span)
+        for i in range(2 * pairs):
+            row = pl.multiple_of(start + i * SUB, SUB)
+            after = row + SUB
+            if i + 1 == 2 * pairs:
+                after = jnp.minimum(after, last)
+            fetch(pl.multiple_of(after, SUB), stages[(i + 1) % 2])
+            compute(row, stages[i % 2])
         return 0
 
-    lax.fori_loop(0, count // (2 * SUB), step, 0)
+    lax.fori_loop(0, count // span, step, 0)
 
 
 def grid_rows(first, shape):
@@ -251,7 +257,7 @@
                     start = ((m * elems + row) * 2 + level - 1) * chunks + c
                     tbl12[pl.ds(start, SUB, stride=2 * chunks), :] = values[level]
 
-    over_groups(elems, fill)
+    over_groups(elems, fill, 2)
 
     def take(row):
         for place, side in enumerate(sides(info)):
@@ -679,7 +685,7 @@
             def compute_piece(row, stage, begin=begin):
                 compute(pl.multiple_of(row + begin, SUB), stage)
 
-            pipelined_groups(size, (stage_a, stage_b), fetch_piece, compute_piece)
+            pipelined_groups(size, (stage_a, stage_b), fetch_piece, compute_piece, 2)
             part = pl.ds(begin, size)
             copy = pltpu.make_async_copy(target.at[:, part, :], out.at[:, part, :], sems.at[piece])
             copy.start()

time: 68.3 us -> 65.8 us (0.963)
  Pallas kernels: 40.6 us -> 37.7 us
    pallas_call x2, Pallas kernels: 6.42 us -> 5.43 us  [on_device(): pl.pallas_call(lambda *refs, section=section: mean_kernel(*refs, section=...]
    pallas_call x2, Pallas kernels: 11.6 us -> 10.7 us  [on_device(): pl.pallas_call(lambda *refs, section=section: rest_kernel(*refs, section=...]
    pallas_call x2, Pallas kernels: 6.75 us -> 6 us  [on_device(): pl.pallas_call(lambda *refs, section=section: limit_kernel(*refs, section...]
where the time goes in v3:
time: 65.8 us; the launch traced here: 65.6 us
  Pallas kernels  37.7 us (57%)
  starting transfers between devices  24.5 us (37%)
  local copies, waits for them, and re-layouts  1.91 us (3%)
  waiting for transfers between devices  0.99 us (2%)
    ppermute x8, starting transfers between devices, traded(): return lax.ppermute(value, 'space', pairs)  14.8 us
    pallas_call x2, Pallas kernels, on_device(): pl.pallas_call(lambda *refs, section=section: rest_kernel(*refs, section=...  10.7 us
    ppermute x8, starting transfers between devices, swapped(): return lax.ppermute(value, 'vel', [(i, i ^ bits) for i in range(peers)])  9.72 us
    pallas_call x2, Pallas kernels, on_device(): pl.pallas_call(lambda *refs, section=section: own_kernel(*refs, section=s...  6.15 us
    pallas_call x2, Pallas kernels, on_device(): pl.pallas_call(lambda *refs, section=section: limit_kernel(*refs, section...  6 us
    pallas_call x2, Pallas kernels, on_device(): pl.pallas_call(lambda *refs, section=section: mean_kernel(*refs, section=...  5.43 us
    pallas_call x2, Pallas kernels, on_device(): pl.pallas_call(trace_kernel, out_shape=(S((rows * chunks, LANE), f32), S(...  4.41 us
    unnamed x12, local copies, waits for them, and re-layouts  1.91 us
  transfers between devices with their start and end apart: 16, of which 2 were waited for; matrix products, arithmetic and copies ran while one was open for 0% of the time, Pallas kernels for 38%

profile of v3, /device:TPU:1, one launch (start us, length us, event | category | flops | bytes accessed | tf_op | source)
XLA Modules:
  0.0 65.6 jit_solution(7022271100909590740)
XLA Ops:
  0.0 0.1 pad_add_fusion.info.refs_0_.refs_2_.refs_1_
  0.1 1.9 %copy-done = f32[6,256,512]{2,1,0:T(8,128)S(1)} copy-done((f32[6,256,512]{2,1,0:T(8,128)S(1)}, f32[6,256,512]{2,1,0:T(8,128)}, u32[]{:S(2)}) %copy-start) | copy-done | bytes 3145752
  2.0 1.5 %first.1 = f32[48,256]{1,0:T(8,128)S(1)} custom-call(s32[2]{0:T(128)S(1)} %pad_add_fusion.info.refs_0_.refs_2_.refs_1_, f32[6,256,512]{2,1,0:T(8,128)S(1)} %copy-done), custom_call_target="tpu_custom_call" | custom-call | tf_op jit(solution)/shard_map/first/pallas_call | solution.py:766
  3.5 2.1 %collective-permute-start = (f32[48,256]{1,0:T(8,128)S(1)}, f32[48,256]{1,0:T(8,128)S(1)}, u32[]{:S(2)}, u32[]{:S(2)}) collective-permute-start(f32[48,256]{1,0:T(8,128)S(1)} %first.1), channel_id=1, source_target_pairs={{0,1},{1,0},{2,3},{3,2},{4,5},{5,4},{6,7},{7,6},{8,9},{9,8},{10,11... | collective-permute-start | bytes 147464 | tf_op jit(solution)/shard_map/ppermute | solution.py:707
  5.6 1.6 %prepare.1 = (s32[3,256]{1,0:T(4,128)S(1)}, s32[3,256]{1,0:T(4,128)S(1)}, s32[4,80]{1,0:T(4,128)S(1)}, bf16[256,3072]{1,0:T(8,128)(2,1)S(1)}, f32[4,256,128]{2,1,0:T(8,128)S(1)}) custom-call(s32[2,80]{1,0:T(2,128)S(1)} %bitcast.8, s32[2]{0:T(128)S(1)} %pad_add_fusion.info.refs_0_.refs_2_.refs_1_, s32[3,256]{1,0:T(4,128)S(1)} %copy-done.4, ...), custom_call_target="tpu_custom_call" | custom-call | tf_op jit(solution)/shard_map/prepare/pallas_call | solution.py:750
  7.2 2.2 %trace.2 = (f32[3712,128]{1,0:T(8,128)S(1)}, f32[7424,128]{1,0:T(8,128)S(1)}, f32[3,80,512]{2,1,0:T(8,128)S(1)}, f32[3,80,512]{2,1,0:T(8,128)S(1)}) custom-call(s32[4,80]{1,0:T(4,128)S(1)} %get-tuple-element.54.offsets.refs_0_, s32[2]{0:T(128)S(1)} %pad_add_fusion.info.refs_0_.refs_2_.refs_1_, f32[6,256,512]{2,1,0:T(8,128)S(1)} %copy-done.1), custom_call_target="tpu_custom_call" | custom-call | tf_op jit(solution)/shard_map/trace/pallas_call | solution.py:778
  9.4 0.0 collective-permute-done
  9.5 1.0 %collective-permute-start.1 = (f32[3,80,512]{2,1,0:T(8,128)S(1)}, f32[3,80,512]{2,1,0:T(8,128)S(1)}, u32[]{:S(2)}, u32[]{:S(2)}) collective-permute-start(f32[3,80,512]{2,1,0:T(8,128)S(1)} %get-tuple-element.60), channel_id=1, source_target_pairs={{0,8},{8,0},{16,24},{24,16},{1,9},{9,1},{17,25},{25,17},{2,10},{10... | collective-permute-start | bytes 1474568 | tf_op jit(solution)/shard_map/ppermute | solution.py:702
  10.5 3.0 %collective-permute-start.2 = (f32[3,80,512]{2,1,0:T(8,128)S(1)}, f32[3,80,512]{2,1,0:T(8,128)S(1)}, u32[]{:S(2)}, u32[]{:S(2)}) collective-permute-start(f32[3,80,512]{2,1,0:T(8,128)S(1)} %get-tuple-element.61), channel_id=1, source_target_pairs={{8,16},{16,8},{9,17},{17,9},{10,18},{18,10},{11,19},{19,11},{12,20... | collective-permute-start | bytes 1474568 | tf_op jit(solution)/shard_map/ppermute | solution.py:702
  13.5 3.4 %collective-permute-start.5 = (f32[48,256]{1,0:T(8,128)S(1)}, f32[48,256]{1,0:T(8,128)S(1)}, u32[]{:S(2)}, u32[]{:S(2)}) collective-permute-start(f32[48,256]{1,0:T(8,128)S(1)} %add.11.refs_0_), channel_id=1, source_target_pairs={{0,6},{1,7},{2,4},{3,5},{4,2},{5,3},{6,0},{7,1},{8,14},{9,15},{10,... | collective-permute-start | bytes 147464 | tf_op jit(solution)/shard_map/ppermute | solution.py:707
  16.9 0.0 collective-permute-start.4
  16.9 0.4 collective-permute-start.3
  17.3 3.0 %own0.1.refs_5_ = f32[6,256,512]{2,1,0:T(8,128)S(1)} custom-call(s32[2]{0:T(128)S(1)} %pad_add_fusion.info.refs_0_.refs_2_.refs_1_, f32[6,256,512]{2,1,0:T(8,128)S(1)} %copy-done.1, f32[4,256,128]{2,1,0:T(8,128)S(1)} %get-tuple-element.57.refs_2_.refs_8_.refs_12_), custom_call_target="tpu_custom_call" | custom-call | tf_op jit(solution)/shard_map/own0/pallas_call | solution.py:793
  20.3 0.0 collective-permute-done.5.refs_3_
  20.3 0.5 collective-permute-done.4.refs_2_
  20.8 0.0 collective-permute-done.3.refs_1_
  20.8 0.9 %form0.1 = (bf16[3,256,256]{2,1,0:T(8,128)(2,1)S(1)}, f32[6,256,128]{2,1,0:T(8,128)S(1)}, f32[256,1536]{1,0:T(8,128)S(1)}, f32[256,1536]{1,0:T(8,128)S(1)}, f32[256,1536]{1,0:T(8,128)S(1)}) custom-call(f32[48,256]{1,0:T(8,128)S(1)} %add.11.refs_0_, f32[48,256]{1,0:T(8,128)S(1)} %collective-permute-done.3.refs_1_, ...), custom_call_target="tpu_custom_call" | custom-call | tf_op jit(solution)/shard_map/form0/pallas_call | solution.py:801
  21.7 0.0 collective-permute-done.1.refs_6_
  21.7 0.0 collective-permute-done.2.refs_7_
  21.7 2.7 %mean0.1 = (f32[3712,128]{1,0:T(8,128)S(1)}, f32[1664,128]{1,0:T(8,128)S(1)}, f32[256,512]{1,0:T(8,128)S(1)}, f32[3,256,512]{2,1,0:T(8,128)S(1)}, f32[80,512]{1,0:T(8,128)S(1)}, /*index=5*/f32[80,512]{1,0:T(8,128)S(1)}) custom-call(s32[4,80]{1,0:T(4,128)S(1)} %get-tuple-element.54.offsets.refs_0_, ...), custom_call_target="tpu_custom_call", output_to_operand_aliasing={{0}: (3, {})} | custom-call | tf_op jit(solution)/shard_map/mean0/pallas_call | solution.py:810
  24.5 0.1 collective-permute-start.6
  24.5 3.9 %collective-permute-start.7 = (f32[80,512]{1,0:T(8,128)S(1)}, f32[80,512]{1,0:T(8,128)S(1)}, u32[]{:S(2)}, u32[]{:S(2)}) collective-permute-start(f32[80,512]{1,0:T(8,128)S(1)} %get-tuple-element.77), channel_id=1, source_target_pairs={{8,16},{16,8},{9,17},{17,9},{10,18},{18,10},{11,19},{19,11},{12,20... | collective-permute-start | bytes 491528 | tf_op jit(solution)/shard_map/ppermute | solution.py:702
  28.5 5.3 %rest0.1 = (f32[7424,128]{1,0:T(8,128)S(1)}, f32[5,256,512]{2,1,0:T(8,128)S(1)}, f32[2,256,512]{2,1,0:T(8,128)S(1)}) custom-call(s32[3,256]{1,0:T(4,128)S(1)} %get-tuple-element.55.refs_1_.refs_0_, s32[2]{0:T(128)S(1)} %pad_add_fusion.info.refs_0_.refs_2_.refs_1_, f32[3712,128]{1,0:T(8,128)S(1)} %get-tuple-element.70.refs_2_, ...), custom_call_target="tpu_custom_call", output_to_operand_aliasing={{0}: (3, {})} | custom-call | tf_op jit(solution)/shard_map/rest0/pallas_call | solution.py:830
  33.8 0.0 collective-permute-done.6.refs_6_
  33.8 0.0 collective-permute-done.7.refs_7_
  33.8 3.0 %limit0.1 = (f32[1664,128]{1,0:T(8,128)S(1)}, f32[6,256,512]{2,1,0:T(8,128)S(1)}, f32[48,256]{1,0:T(8,128)S(1)}) custom-call(s32[3,256]{1,0:T(4,128)S(1)} %get-tuple-element.53.refs_0_, s32[2]{0:T(128)S(1)} %pad_add_fusion.info.refs_0_.refs_2_.refs_1_, f32[1664,128]{1,0:T(8,128)S(1)} %get-tuple-element.68.refs_2_, ...), custom_call_target="tpu_custom_call", output_to_operand_aliasing={{0}: (2, {})} | custom-call | tf_op jit(solution)/shard_map/limit0/pallas_call | solution.py:844
  36.8 0.3 collective-permute-start.8
  37.1 2.2 %trace.3 = (f32[3712,128]{1,0:T(8,128)S(1)}, f32[7424,128]{1,0:T(8,128)S(1)}, f32[3,80,512]{2,1,0:T(8,128)S(1)}, f32[3,80,512]{2,1,0:T(8,128)S(1)}) custom-call(s32[4,80]{1,0:T(4,128)S(1)} %get-tuple-element.54.offsets.refs_0_, s32[2]{0:T(128)S(1)} %pad_add_fusion.info.refs_0_.refs_2_.refs_1_, f32[6,256,512]{2,1,0:T(8,128)S(1)} %get-tuple-element.78.z_ref.refs_1_.refs_4_), custom_call_target="tpu_custom_call" | custom-call | tf_op jit(solution)/shard_map/trace/pallas_call | solution.py:778
  39.3 0.5 collective-permute-done.8
  39.8 0.1 collective-permute-start.9
  39.9 3.1 %collective-permute-start.10 = (f32[3,80,512]{2,1,0:T(8,128)S(1)}, f32[3,80,512]{2,1,0:T(8,128)S(1)}, u32[]{:S(2)}, u32[]{:S(2)}) collective-permute-start(f32[3,80,512]{2,1,0:T(8,128)S(1)} %get-tuple-element.84), channel_id=1, source_target_pairs={{8,16},{16,8},{9,17},{17,9},{10,18},{18,10},{11,19},{19,11},{12,20... | collective-permute-start | bytes 1474568 | tf_op jit(solution)/shard_map/ppermute | solution.py:702
  43.0 2.5 %collective-permute-start.13 = (f32[48,256]{1,0:T(8,128)S(1)}, f32[48,256]{1,0:T(8,128)S(1)}, u32[]{:S(2)}, u32[]{:S(2)}) collective-permute-start(f32[48,256]{1,0:T(8,128)S(1)} %add.12.refs_0_), channel_id=1, source_target_pairs={{0,6},{1,7},{2,4},{3,5},{4,2},{5,3},{6,0},{7,1},{8,14},{9,15},{10,... | collective-permute-start | bytes 147464 | tf_op jit(solution)/shard_map/ppermute | solution.py:707
  45.5 0.0 collective-permute-start.12
  45.5 1.1 %collective-permute-start.11 = (f32[48,256]{1,0:T(8,128)S(1)}, f32[48,256]{1,0:T(8,128)S(1)}, u32[]{:S(2)}, u32[]{:S(2)}) collective-permute-start(f32[48,256]{1,0:T(8,128)S(1)} %add.12.refs_0_), channel_id=1, source_target_pairs={{0,2},{1,3},{2,0},{3,1},{4,6},{5,7},{6,4},{7,5},{8,10},{9,11},{10,... | collective-permute-start | bytes 147464 | tf_op jit(solution)/shard_map/ppermute | solution.py:707
  46.6 3.2 %own1.1.refs_5_ = f32[6,256,512]{2,1,0:T(8,128)S(1)} custom-call(s32[2]{0:T(128)S(1)} %pad_add_fusion.info.refs_0_.refs_2_.refs_1_, f32[6,256,512]{2,1,0:T(8,128)S(1)} %get-tuple-element.78.z_ref.refs_1_.refs_4_, f32[4,256,128]{2,1,0:T(8,128)S(1)} %get-tuple-element.57.refs_2_.refs_8_.refs_12_, f32[6,256,512]{2,1,0:T(8,128)S(1)} %copy-done.1), custom_call_target="tpu_custom_call" | custom-call | tf_op jit(solution)/shard_map/own1/pallas_call | solution.py:793
  49.7 0.0 collective-permute-done.13.refs_3_
  49.8 0.0 collective-permute-done.12.refs_2_
  49.8 0.0 collective-permute-done.11.refs_1_
  49.8 0.9 %form1.1 = (bf16[3,256,256]{2,1,0:T(8,128)(2,1)S(1)}, f32[6,256,128]{2,1,0:T(8,128)S(1)}, f32[256,1536]{1,0:T(8,128)S(1)}, f32[256,1536]{1,0:T(8,128)S(1)}, f32[256,1536]{1,0:T(8,128)S(1)}) custom-call(f32[48,256]{1,0:T(8,128)S(1)} %add.12.refs_0_, f32[48,256]{1,0:T(8,128)S(1)} %collective-permute-done.11.refs_1_, ...), custom_call_target="tpu_custom_call" | custom-call | tf_op jit(solution)/shard_map/form1/pallas_call | solution.py:801
  50.7 0.0 collective-permute-done.9.refs_6_
  50.7 0.0 collective-permute-done.10.refs_7_
  50.7 2.7 %mean1.1 = (f32[3712,128]{1,0:T(8,128)S(1)}, f32[1664,128]{1,0:T(8,128)S(1)}, f32[256,512]{1,0:T(8,128)S(1)}, f32[3,256,512]{2,1,0:T(8,128)S(1)}, f32[80,512]{1,0:T(8,128)S(1)}, /*index=5*/f32[80,512]{1,0:T(8,128)S(1)}) custom-call(s32[4,80]{1,0:T(4,128)S(1)} %get-tuple-element.54.offsets.refs_0_, ...), custom_call_target="tpu_custom_call", output_to_operand_aliasing={{0}: (3, {})} | custom-call | tf_op jit(solution)/shard_map/mean1/pallas_call | solution.py:810
  53.5 0.2 collective-permute-start.14
  53.7 3.3 %collective-permute-start.15 = (f32[80,512]{1,0:T(8,128)S(1)}, f32[80,512]{1,0:T(8,128)S(1)}, u32[]{:S(2)}, u32[]{:S(2)}) collective-permute-start(f32[80,512]{1,0:T(8,128)S(1)} %get-tuple-element.99), channel_id=1, source_target_pairs={{8,16},{16,8},{9,17},{17,9},{10,18},{18,10},{11,19},{19,11},{12,20... | collective-permute-start | bytes 491528 | tf_op jit(solution)/shard_map/ppermute | solution.py:702
  57.0 5.3 %rest1.1 = (f32[7424,128]{1,0:T(8,128)S(1)}, f32[5,256,512]{2,1,0:T(8,128)S(1)}, f32[2,256,512]{2,1,0:T(8,128)S(1)}) custom-call(s32[3,256]{1,0:T(4,128)S(1)} %get-tuple-element.55.refs_1_.refs_0_, s32[2]{0:T(128)S(1)} %pad_add_fusion.info.refs_0_.refs_2_.refs_1_, f32[3712,128]{1,0:T(8,128)S(1)} %get-tuple-element.92.refs_2_, ...), custom_call_target="tpu_custom_call", output_to_operand_aliasing={{0}: (3, {})} | custom-call | tf_op jit(solution)/shard_map/rest1/pallas_call | solution.py:830
  62.4 0.0 collective-permute-done.14.refs_6_
  62.4 0.0 collective-permute-done.15.refs_7_
  62.4 3.0 %limit1.1 = (f32[1664,128]{1,0:T(8,128)S(1)}, f32[6,256,512]{2,1,0:T(8,128)}) custom-call(s32[3,256]{1,0:T(4,128)S(1)} %get-tuple-element.53.refs_0_, s32[2]{0:T(128)S(1)} %pad_add_fusion.info.refs_0_.refs_2_.refs_1_, f32[1664,128]{1,0:T(8,128)S(1)} %get-tuple-element.90.refs_2_, ...), custom_call_target="tpu_custom_call", output_to_operand_aliasing={{0}: (2, {})} | custom-call | tf_op jit(solution)/shard_map/limit1/pallas_call | solution.py:844
  (13 shorter events, 0.0 us)
Async XLA Ops:
  0.0 5.6 %copy-start.5 = (s32[1,2,80]{2,1,0:T(2,128)S(1)}, s32[1,2,80]{2,1,0:T(2,128)}, u32[]{:S(2)}) copy-start(s32[1,2,80]{2,1,0:T(2,128)} %param.8) | copy-start | bytes 1924
  0.0 5.6 %copy-start.4 = (s32[3,256]{1,0:T(4,128)S(1)}, s32[3,256]{1,0:T(4,128)}, u32[]{:S(2)}) copy-start(s32[3,256]{1,0:T(4,128)} %neigh_ref.1) | copy-start | bytes 9220
  0.0 5.6 %copy-start.2 = (f32[2,3,256]{2,0,1:T(2,128)S(1)}, f32[2,3,256]{2,0,1:T(2,128)}, u32[]{:S(2)}) copy-start(f32[2,3,256]{2,0,1:T(2,128)} %param.6) | copy-start | bytes 18436
  0.1 1.9 %copy-start = (f32[6,256,512]{2,1,0:T(8,128)S(1)}, f32[6,256,512]{2,1,0:T(8,128)}, u32[]{:S(2)}) copy-start(f32[6,256,512]{2,1,0:T(8,128)} %refs_3_.1) | copy-start | bytes 9437188
  2.0 5.2 %copy-start.1 = (f32[6,256,512]{2,1,0:T(8,128)S(1)}, f32[6,256,512]{2,1,0:T(8,128)}, u32[]{:S(2)}) copy-start(f32[6,256,512]{2,1,0:T(8,128)} %refs_3_.1) | copy-start | bytes 9437188
  3.5 5.9 %collective-permute-start = (f32[48,256]{1,0:T(8,128)S(1)}, f32[48,256]{1,0:T(8,128)S(1)}, u32[]{:S(2)}, u32[]{:S(2)}) collective-permute-start(f32[48,256]{1,0:T(8,128)S(1)} %first.1), channel_id=1, source_target_pairs={{0,1},{1,0},{2,3},{3,2},{4,5},{5,4},{6,7},{7,6},{8,9},{9,8},{10,11... | collective-permute-start | bytes 147464 | tf_op jit(solution)/shard_map/ppermute | solution.py:707
  9.5 12.2 %collective-permute-start.1 = (f32[3,80,512]{2,1,0:T(8,128)S(1)}, f32[3,80,512]{2,1,0:T(8,128)S(1)}, u32[]{:S(2)}, u32[]{:S(2)}) collective-permute-start(f32[3,80,512]{2,1,0:T(8,128)S(1)} %get-tuple-element.60), channel_id=1, source_target_pairs={{0,8},{8,0},{16,24},{24,16},{1,9},{9,1},{17,25},{25,17},{2,10},{10... | collective-permute-start | bytes 1474568 | tf_op jit(solution)/shard_map/ppermute | solution.py:702
  10.5 11.2 %collective-permute-start.2 = (f32[3,80,512]{2,1,0:T(8,128)S(1)}, f32[3,80,512]{2,1,0:T(8,128)S(1)}, u32[]{:S(2)}, u32[]{:S(2)}) collective-permute-start(f32[3,80,512]{2,1,0:T(8,128)S(1)} %get-tuple-element.61), channel_id=1, source_target_pairs={{8,16},{16,8},{9,17},{17,9},{10,18},{18,10},{11,19},{19,11},{12,20... | collective-permute-start | bytes 1474568 | tf_op jit(solution)/shard_map/ppermute | solution.py:702
  13.5 6.7 %collective-permute-start.5 = (f32[48,256]{1,0:T(8,128)S(1)}, f32[48,256]{1,0:T(8,128)S(1)}, u32[]{:S(2)}, u32[]{:S(2)}) collective-permute-start(f32[48,256]{1,0:T(8,128)S(1)} %add.11.refs_0_), channel_id=1, source_target_pairs={{0,6},{1,7},{2,4},{3,5},{4,2},{5,3},{6,0},{7,1},{8,14},{9,15},{10,... | collective-permute-start | bytes 147464 | tf_op jit(solution)/shard_map/ppermute | solution.py:707
  16.9 3.8 %collective-permute-start.4 = (f32[48,256]{1,0:T(8,128)S(1)}, f32[48,256]{1,0:T(8,128)S(1)}, u32[]{:S(2)}, u32[]{:S(2)}) collective-permute-start(f32[48,256]{1,0:T(8,128)S(1)} %add.11.refs_0_), channel_id=1, source_target_pairs={{0,4},{1,5},{2,6},{3,7},{4,0},{5,1},{6,2},{7,3},{8,12},{9,13},{10,... | collective-permute-start | bytes 147464 | tf_op jit(solution)/shard_map/ppermute | solution.py:707
  16.9 3.8 %collective-permute-start.3 = (f32[48,256]{1,0:T(8,128)S(1)}, f32[48,256]{1,0:T(8,128)S(1)}, u32[]{:S(2)}, u32[]{:S(2)}) collective-permute-start(f32[48,256]{1,0:T(8,128)S(1)} %add.11.refs_0_), channel_id=1, source_target_pairs={{0,2},{1,3},{2,0},{3,1},{4,6},{5,7},{6,4},{7,5},{8,10},{9,11},{10,... | collective-permute-start | bytes 147464 | tf_op jit(solution)/shard_map/ppermute | solution.py:707
  17.3 3.5 %copy-start.3 = (f32[256]{0:T(256)S(1)}, f32[256]{0:T(256)}, u32[]{:S(2)}) copy-start(f32[256]{0:T(256)} %param.9) | copy-start | bytes 3076
  24.5 9.4 %collective-permute-start.6 = (f32[80,512]{1,0:T(8,128)S(1)}, f32[80,512]{1,0:T(8,128)S(1)}, u32[]{:S(2)}, u32[]{:S(2)}) collective-permute-start(f32[80,512]{1,0:T(8,128)S(1)} %get-tuple-element.76), channel_id=1, source_target_pairs={{0,8},{8,0},{16,24},{24,16},{1,9},{9,1},{17,25},{25,17},{2,10},{10... | collective-permute-start | bytes 491528 | tf_op jit(solution)/shard_map/ppermute | solution.py:702
  24.5 9.3 %collective-permute-start.7 = (f32[80,512]{1,0:T(8,128)S(1)}, f32[80,512]{1,0:T(8,128)S(1)}, u32[]{:S(2)}, u32[]{:S(2)}) collective-permute-start(f32[80,512]{1,0:T(8,128)S(1)} %get-tuple-element.77), channel_id=1, source_target_pairs={{8,16},{16,8},{9,17},{17,9},{10,18},{18,10},{11,19},{19,11},{12,20... | collective-permute-start | bytes 491528 | tf_op jit(solution)/shard_map/ppermute | solution.py:702
  36.8 3.0 %collective-permute-start.8 = (f32[48,256]{1,0:T(8,128)S(1)}, f32[48,256]{1,0:T(8,128)S(1)}, u32[]{:S(2)}, u32[]{:S(2)}) collective-permute-start(f32[48,256]{1,0:T(8,128)S(1)} %get-tuple-element.82), channel_id=1, source_target_pairs={{0,1},{1,0},{2,3},{3,2},{4,5},{5,4},{6,7},{7,6},{8,9},{9,8},{10,11... | collective-permute-start | bytes 147464 | tf_op jit(solution)/shard_map/ppermute | solution.py:707
  39.8 10.9 %collective-permute-start.9 = (f32[3,80,512]{2,1,0:T(8,128)S(1)}, f32[3,80,512]{2,1,0:T(8,128)S(1)}, u32[]{:S(2)}, u32[]{:S(2)}) collective-permute-start(f32[3,80,512]{2,1,0:T(8,128)S(1)} %get-tuple-element.83), channel_id=1, source_target_pairs={{0,8},{8,0},{16,24},{24,16},{1,9},{9,1},{17,25},{25,17},{2,10},{10... | collective-permute-start | bytes 1474568 | tf_op jit(solution)/shard_map/ppermute | solution.py:702
  39.9 10.8 %collective-permute-start.10 = (f32[3,80,512]{2,1,0:T(8,128)S(1)}, f32[3,80,512]{2,1,0:T(8,128)S(1)}, u32[]{:S(2)}, u32[]{:S(2)}) collective-permute-start(f32[3,80,512]{2,1,0:T(8,128)S(1)} %get-tuple-element.84), channel_id=1, source_target_pairs={{8,16},{16,8},{9,17},{17,9},{10,18},{18,10},{11,19},{19,11},{12,20... | collective-permute-start | bytes 1474568 | tf_op jit(solution)/shard_map/ppermute | solution.py:702
  43.0 6.8 %collective-permute-start.13 = (f32[48,256]{1,0:T(8,128)S(1)}, f32[48,256]{1,0:T(8,128)S(1)}, u32[]{:S(2)}, u32[]{:S(2)}) collective-permute-start(f32[48,256]{1,0:T(8,128)S(1)} %add.12.refs_0_), channel_id=1, source_target_pairs={{0,6},{1,7},{2,4},{3,5},{4,2},{5,3},{6,0},{7,1},{8,14},{9,15},{10,... | collective-permute-start | bytes 147464 | tf_op jit(solution)/shard_map/ppermute | solution.py:707
  45.5 4.3 %collective-permute-start.12 = (f32[48,256]{1,0:T(8,128)S(1)}, f32[48,256]{1,0:T(8,128)S(1)}, u32[]{:S(2)}, u32[]{:S(2)}) collective-permute-start(f32[48,256]{1,0:T(8,128)S(1)} %add.12.refs_0_), channel_id=1, source_target_pairs={{0,4},{1,5},{2,6},{3,7},{4,0},{5,1},{6,2},{7,3},{8,12},{9,13},{10,... | collective-permute-start | bytes 147464 | tf_op jit(solution)/shard_map/ppermute | solution.py:707
  45.5 4.3 %collective-permute-start.11 = (f32[48,256]{1,0:T(8,128)S(1)}, f32[48,256]{1,0:T(8,128)S(1)}, u32[]{:S(2)}, u32[]{:S(2)}) collective-permute-start(f32[48,256]{1,0:T(8,128)S(1)} %add.12.refs_0_), channel_id=1, source_target_pairs={{0,2},{1,3},{2,0},{3,1},{4,6},{5,7},{6,4},{7,5},{8,10},{9,11},{10,... | collective-permute-start | bytes 147464 | tf_op jit(solution)/shard_map/ppermute | solution.py:707
  53.5 8.9 %collective-permute-start.14 = (f32[80,512]{1,0:T(8,128)S(1)}, f32[80,512]{1,0:T(8,128)S(1)}, u32[]{:S(2)}, u32[]{:S(2)}) collective-permute-start(f32[80,512]{1,0:T(8,128)S(1)} %get-tuple-element.98), channel_id=1, source_target_pairs={{0,8},{8,0},{16,24},{24,16},{1,9},{9,1},{17,25},{25,17},{2,10},{10... | collective-permute-start | bytes 491528 | tf_op jit(solution)/shard_map/ppermute | solution.py:702
  53.7 8.7 %collective-permute-start.15 = (f32[80,512]{1,0:T(8,128)S(1)}, f32[80,512]{1,0:T(8,128)S(1)}, u32[]{:S(2)}, u32[]{:S(2)}) collective-permute-start(f32[80,512]{1,0:T(8,128)S(1)} %get-tuple-element.99), channel_id=1, source_target_pairs={{8,16},{16,8},{9,17},{17,9},{10,18},{18,10},{11,19},{19,11},{12,20... | collective-permute-start | bytes 491528 | tf_op jit(solution)/shard_map/ppermute | solution.py:702

commit v4 on v3

--- a/solution.py
+++ b/solution.py
@@ -191,8 +191,9 @@
     return total[0:8] + total[8:16] + total[16:24]
 
 
-def first_kernel(info, z_ref, mom):
-    weights = weight_rows(info[0], z_ref.shape[2])
+def first_kernel(z_ref, mom):
+    vel = z_ref.shape[2]
+    weights = weight_rows(lax.axis_index("vel") * vel, vel)
     for j in range(MODES):
         mom[pl.ds(j * SUB, SUB), :] = mode_moments(weights, z_ref[j])
 
@@ -203,11 +204,14 @@
     shape = neigh_ref.shape
     face = lax.broadcasted_iota(jnp.int32, shape, 0) * elems + lax.broadcasted_iota(jnp.int32, shape, 1)
 
-    def mark(slot, found):
-        found = jnp.where(face == lists[0, slot], faces + slot, found)
-        return jnp.where(face == lists[1, slot], faces + slots + slot, found)
-
-    found = jnp.maximum(lax.fori_loop(0, slots, mark, neigh_ref[...]), 0)
+    def mark(group, found):
+        for i in range(SUB):
+            slot = group * SUB + i
+            found = jnp.where(face == lists[0, slot], faces + slot, found)
+            found = jnp.where(face == lists[1, slot], faces + slots + slot, found)
+        return found
+
+    found = jnp.maximum(lax.fori_loop(0, slots // SUB, mark, neigh_ref[...]), 0)
     src[...] = found * chunks
     away[...] = jnp.where(found < faces, found % elems, found - 2 * elems) * chunks
     known = jnp.maximum(rows_ref[...], 0)
@@ -231,22 +235,24 @@
     put_columns(rows, cols)
 
 
-def sides(info):
-    parity = info[1]
+def sides():
+    parity = lax.rem(lax.axis_index("space"), 2)
     return (1 - parity, parity)
 
 
-def prepare_kernel(lists, info, neigh_ref, rows_ref, corner, src, away, offsets, basis, cols):
+def prepare_kernel(lists, neigh_ref, rows_ref, corner, src, away, offsets, basis, cols, weights):
     vel = basis.shape[1] // MODES
     put_index(neigh_ref, rows_ref, lists, src, away, offsets, cols.shape[1], vel // LANE)
     put_flows(corner, cols)
-    put_basis(info[0], basis, vel)
-
-
-def trace_kernel(offsets, info, z_ref, tbl0, tbl12, near, far, stage0, stage12):
+    first = lax.axis_index("vel") * vel
+    put_basis(first, basis, vel)
+    weights[...] = weight_rows(first, vel)
+
+
+def trace_kernel(offsets, z_ref, tbl0, tbl12, near, far, stage0, stage12):
     elems, vel = z_ref.shape[1:]
     chunks = vel // LANE
-    slots = offsets.shape[1]
+    slots = near.shape[1]
 
     def fill(row):
         for c in range(chunks):
@@ -260,7 +266,7 @@
     over_groups(elems, fill, 2)
 
     def take(row):
-        for place, side in enumerate(sides(info)):
+        for place, side in enumerate(sides()):
             for i in range(SUB):
                 start = offsets[side, row + i]
                 to = (place * slots + row + i) * chunks
@@ -429,14 +435,14 @@
     )
 
 
-def own_kernel(info, z_ref, cols, *refs, section):
+def own_kernel(z_ref, cols, *refs, section):
     if section == 1:
         base_ref, out = refs
     else:
         (out,) = refs
     elems, vel = z_ref.shape[1:]
     chunks = vel // LANE
-    grid = chunk_grid(info[0], chunks)
+    grid = chunk_grid(lax.axis_index("vel") * vel, chunks)
 
     def compute(row):
         flows = flow_forms(cols, grid, row)
@@ -470,17 +476,17 @@
     over_groups(elems, compute, 2)
 
 
-def mean_kernel(offsets, src, info, _, z_ref, own, near_in, far_in, cols, nus, *refs, section):
+def mean_kernel(offsets, src, _, z_ref, own, near_in, far_in, cols, nus, *refs, section):
     forms = refs[:3]
     refs = refs[3:]
     tbl, mtbl, centre, high, near, far, stage_a, stage_b, stage = refs
     elems, vel = z_ref.shape[1:]
     chunks = vel // LANE
-    slots = offsets.shape[1]
+    slots = near.shape[0]
     faces = 3 * elems
 
     def fill_border(row):
-        for side, halo in zip(sides(info), (near_in, far_in)):
+        for side, halo in zip(sides(), (near_in, far_in)):
             for c in range(chunks):
                 start = (faces + side * slots + row) * chunks + c
                 tbl[pl.ds(start, SUB, stride=chunks), :] = halo[(0, *at(row, c))]
@@ -488,7 +494,7 @@
     over_groups(slots, fill_border)
 
     N, V = NODAL, INVERSE
-    grid = chunk_grid(info[0], chunks)
+    grid = chunk_grid(lax.axis_index("vel") * vel, chunks)
 
     def fetch(row, stage):
         for m in range(3):
@@ -525,7 +531,7 @@
     pipelined_groups(elems, (stage_a, stage_b), fetch, compute)
 
     def take(row):
-        for place, side in enumerate(sides(info)):
+        for place, side in enumerate(sides()):
             for i in range(SUB):
                 copy_rows(mtbl, stage, offsets[2 + side, row + i], (place * slots + row + i) * chunks, chunks)
 
@@ -540,7 +546,7 @@
     over_groups(slots, pack)
 
 
-def rest_kernel(src, info, tbl0, _, z_ref, own, near, far, high, spreads, nus, basis, cols, *refs, section):
+def rest_kernel(src, tbl0, _, z_ref, own, near, far, high, spreads, nus, basis, cols, *refs, section):
     tbl, out, sizes, stage_a, stage_b, *forms = refs
     elems, vel = z_ref.shape[1:]
     chunks = vel // LANE
@@ -549,7 +555,7 @@
     faces = 3 * elems
 
     def fill_border(row):
-        for side, halo in zip(sides(info), (near, far)):
+        for side, halo in zip(sides(), (near, far)):
             for level in range(2):
                 for c in range(chunks):
                     start = ((faces + side * slots + row) * 2 + level) * chunks + c
@@ -562,7 +568,7 @@
             spreads[i], basis[:, pl.ds(0, 3 * vel)], preferred_element_type=f32
         )
     N, V = NODAL, INVERSE
-    grid = chunk_grid(info[0], chunks)
+    grid = chunk_grid(lax.axis_index("vel") * vel, chunks)
 
     def fetch(row, stage):
         for m in range(3):
@@ -631,7 +637,7 @@
     pipelined_groups(elems, (stage_a, stage_b), fetch, compute)
 
 
-def limit_kernel(away, info, _, centre, rest, sizes, near, far, mtbl, out, *refs, section):
+def limit_kernel(away, _, centre, rest, sizes, near, far, weights, mtbl, out, *refs, section):
     if section == 0:
         mom, stage_a, stage_b = refs
         target = out
@@ -642,7 +648,7 @@
     slots = near.shape[0]
 
     def fill_border(row):
-        for side, halo in zip(sides(info), (near, far)):
+        for side, halo in zip(sides(), (near, far)):
             for c in range(chunks):
                 start = (elems + side * slots + row) * chunks + c
                 mtbl[pl.ds(start, SUB, stride=chunks), :] = halo[at(row, c)]
@@ -669,9 +675,8 @@
 
     if section == 0:
         pipelined_groups(elems, (stage_a, stage_b), fetch, compute)
-        weights = weight_rows(info[0], vel)
         for j in range(MODES):
-            mom[pl.ds(j * SUB, SUB), :] = mode_moments(weights, target[j])
+            mom[pl.ds(j * SUB, SUB), :] = mode_moments(weights[...], target[j])
     else:
         pieces = sems.shape[0]
         size = elems // pieces
@@ -724,7 +729,6 @@
     chunks = vel // LANE
     slots = boundary_faces.shape[2]
     lists = boundary_faces[0]
-    info = jnp.stack([lax.axis_index("vel") * vel, lax.axis_index("space") % 2]).astype(jnp.int32)
     faces = 3 * elems
     rows = faces + 2 * slots
     S = jax.ShapeDtypeStruct
@@ -747,7 +751,7 @@
 
     rate = collision_rate.reshape(1, elems)
     index = S(neighbour.shape, jnp.int32)
-    src, away, offsets, basis, cols = pl.pallas_call(
+    src, away, offsets, basis, cols, weights = pl.pallas_call(
         prepare_kernel,
         out_shape=(
             index,
@@ -755,22 +759,23 @@
             S((4, slots), jnp.int32),
             S((TERMS * SUB, modes * vel), bf16),
             S((4, elems, LANE), f32),
+            S((4 * SUB, vel), bf16),
         ),
-        in_specs=[smem, smem] + [vmem] * 3,
-        out_specs=(vmem,) * 5,
+        in_specs=[smem] + [vmem] * 3,
+        out_specs=(vmem,) * 6,
         compiler_params=params(8),
         name="prepare",
-    )(lists, info, neighbour, lists, corners.transpose(1, 0, 2))
+    )(lists, neighbour, lists, corners.transpose(1, 0, 2))
 
     current = start = distribution
     partial = pl.pallas_call(
         first_kernel,
         out_shape=mom,
-        in_specs=[smem, vmem],
+        in_specs=[vmem],
         out_specs=vmem,
         compiler_params=params(8),
         name="first",
-    )(info, current)
+    )(current)
 
     for section in range(2):
         opening = section == 0
@@ -778,12 +783,12 @@
         tbl0, tbl12, near, far = pl.pallas_call(
             trace_kernel,
             out_shape=(S((rows * chunks, LANE), f32), S((2 * rows * chunks, LANE), f32), halo, halo),
-            in_specs=[smem, smem, vmem],
+            in_specs=[smem, vmem],
             out_specs=(vmem,) * 4,
             scratch_shapes=[buffer(2 * slots * chunks), buffer(4 * slots * chunks)],
             compiler_params=params(8),
             name="trace",
-        )(offsets, info, current)
+        )(offsets, current)
         near, far, paired = lax.optimization_barrier((near, far, paired))
         near = traded(near, True)
         far = traded(far, False)
@@ -793,11 +798,11 @@
         own = pl.pallas_call(
             lambda *refs, section=section: own_kernel(*refs, section=section),
             out_shape=state,
-            in_specs=[smem] + [vmem] * (2 + len(base)),
+            in_specs=[vmem] * (2 + len(base)),
             out_specs=vmem,
             compiler_params=params(4),
             name=f"own{section}",
-        )(info, current, cols, *base)
+        )(current, cols, *base)
         spreads, nus, *forms = pl.pallas_call(
             lambda *refs, section=section: form_kernel(*refs, parts=len(parts), section=section),
             out_shape=(S((3, elems, TERMS * SUB), bf16), S((modes, elems, LANE), f32)) + (S((elems, 3 * vel), f32),) * 3,
@@ -817,26 +822,26 @@
                 one,
                 one,
             ),
-            input_output_aliases={3: 0},
-            in_specs=[smem] * 3 + [vmem] * 10,
+            input_output_aliases={2: 0},
+            in_specs=[smem] * 2 + [vmem] * 10,
             out_specs=(vmem,) * 6,
             scratch_shapes=[buffer(3 * SUB * chunks)] * 2 + [buffer(2 * slots * chunks)],
             compiler_params=params(16),
             name=f"mean{section}",
-        )(offsets, src, info, tbl0, current, own, near, far, cols, nus, *forms)
+        )(offsets, src, tbl0, current, own, near, far, cols, nus, *forms)
         near_mean = traded(near_mean, True)
         far_mean = traded(far_mean, False)
 
         _, rest, sizes = pl.pallas_call(
             lambda *refs, section=section: rest_kernel(*refs, section=section),
             out_shape=(S((2 * rows * chunks, LANE), f32), S((5, elems, vel), f32), S((2, elems, vel), f32)),
-            input_output_aliases={3: 0},
-            in_specs=[smem] * 2 + [vmem] * 11,
+            input_output_aliases={2: 0},
+            in_specs=[smem] + [vmem] * 11,
             out_specs=(vmem,) * 3,
             scratch_shapes=[buffer(9 * SUB * chunks)] * 2 + evaluated(),
             compiler_params=params(20),
             name=f"rest{section}",
-        )(src, info, tbl0, tbl12, current, own, near, far, high, spreads, nus, basis, cols)
+        )(src, tbl0, tbl12, current, own, near, far, high, spreads, nus, basis, cols)
 
         scratch = [buffer(3 * SUB * chunks)] * 2
         if not opening:
@@ -844,13 +849,13 @@
         made = pl.pallas_call(
             lambda *refs, section=section: limit_kernel(*refs, section=section),
             out_shape=(S(mean_table.shape, f32), state) + ((mom,) if opening else ()),
-            in_specs=[smem, smem] + [vmem] * 6,
+            in_specs=[smem] + [vmem] * 7,
             out_specs=(vmem,) * 3 if opening else (vmem, hbm),
-            input_output_aliases={2: 0},
+            input_output_aliases={1: 0},
             scratch_shapes=scratch,
             compiler_params=params(8),
             name=f"limit{section}",
-        )(away, info, mean_table, centre, rest, sizes, near_mean, far_mean)
+        )(away, mean_table, centre, rest, sizes, near_mean, far_mean, weights)
         if opening:
             _, current, partial = made
     return made[1]

time: 65.8 us -> 64.7 us (0.983)
  Pallas kernels: 37.7 us -> 35.7 us
  waiting for transfers between devices: 0.99 us -> 1.72 us
    pallas_call x2, Pallas kernels: 6.15 us -> 5.01 us  [on_device(): pl.pallas_call(lambda *refs, section=section: own_kernel(*refs, section=s...]
    ppermute x8, waiting for transfers between devices: 0.97 us -> 1.69 us  [swapped(): return lax.ppermute(value, 'vel', [(i, i ^ bits) for i in range(peers)])]
  transfers between devices with their start and end apart: 16 -> 16, of which waited for: 2 -> 3; matrix products, arithmetic and copies ran while one was open for 0% -> 0% of each run, Pallas kernels for 38% -> 36%
where the time goes in v4:
time: 64.7 us; the launch traced here: 64.5 us
  Pallas kernels  35.7 us (55%)
  starting transfers between devices  24.8 us (38%)
  local copies, waits for them, and re-layouts  1.91 us (3%)
  waiting for transfers between devices  1.72 us (3%)
    ppermute x8, starting transfers between devices, traded(): return lax.ppermute(value, 'space', pairs)  15 us
    pallas_call x2, Pallas kernels, on_device(): pl.pallas_call(lambda *refs, section=section: rest_kernel(*refs, section=...  10.7 us
    ppermute x8, starting transfers between devices, swapped(): return lax.ppermute(value, 'vel', [(i, i ^ bits) for i in range(peers)])  9.82 us
    pallas_call x2, Pallas kernels, on_device(): pl.pallas_call(lambda *refs, section=section: limit_kernel(*refs, section...  6.06 us
    pallas_call x2, Pallas kernels, on_device(): pl.pallas_call(lambda *refs, section=section: mean_kernel(*refs, section=...  5.47 us
    pallas_call x2, Pallas kernels, on_device(): pl.pallas_call(lambda *refs, section=section: own_kernel(*refs, section=s...  5.01 us
    pallas_call x2, Pallas kernels, on_device(): pl.pallas_call(trace_kernel, out_shape=(S((rows * chunks, LANE), f32), S(...  4.43 us
    unnamed x12, local copies, waits for them, and re-layouts  1.91 us
  transfers between devices with their start and end apart: 16, of which 3 were waited for; matrix products, arithmetic and copies ran while one was open for 0% of the time, Pallas kernels for 36%

profile of v4, /device:TPU:1, one launch (start us, length us, event | category | flops | bytes accessed | tf_op | source)
XLA Modules:
  0.0 64.5 jit_solution(11852002407429834660)
XLA Ops:
  0.0 1.9 %copy-done = f32[6,256,512]{2,1,0:T(8,128)S(1)} copy-done((f32[6,256,512]{2,1,0:T(8,128)S(1)}, f32[6,256,512]{2,1,0:T(8,128)}, u32[]{:S(2)}) %copy-start) | copy-done | bytes 3145752
  1.9 1.0 %first.1 = f32[48,256]{1,0:T(8,128)S(1)} custom-call(f32[6,256,512]{2,1,0:T(8,128)S(1)} %copy-done), custom_call_target="tpu_custom_call" | custom-call | tf_op jit(solution)/shard_map/first/pallas_call | solution.py:771
  2.9 2.1 %collective-permute-start = (f32[48,256]{1,0:T(8,128)S(1)}, f32[48,256]{1,0:T(8,128)S(1)}, u32[]{:S(2)}, u32[]{:S(2)}) collective-permute-start(f32[48,256]{1,0:T(8,128)S(1)} %first.1), channel_id=1, source_target_pairs={{0,1},{1,0},{2,3},{3,2},{4,5},{5,4},{6,7},{7,6},{8,9},{9,8},{10,11... | collective-permute-start | bytes 147464 | tf_op jit(solution)/shard_map/ppermute | solution.py:712
  5.0 1.2 %prepare.1 = (s32[3,256]{1,0:T(4,128)S(1)}, s32[3,256]{1,0:T(4,128)S(1)}, s32[4,80]{1,0:T(4,128)S(1)}, bf16[256,3072]{1,0:T(8,128)(2,1)S(1)}, f32[4,256,128]{2,1,0:T(8,128)S(1)}, /*index=5*/bf16[32,512]{1,0:T(8,128)(2,1)S(1)}) custom-call(s32[2,80]{1,0:T(2,128)S(1)} %bitcast.6, s32[3,256]{1,0:T(4,128)S(1)} %copy-done.4, s32[2,80]{1,0:T(2,128)S(1)} %bitcast.7, ...), custom_call_target="tpu_custom_call" | custom-call | tf_op jit(solution)/shard_map/prepare/pallas_call | solution.py:754
  6.2 0.0 copy-done.1
  6.2 2.2 %trace.2 = (f32[3712,128]{1,0:T(8,128)S(1)}, f32[7424,128]{1,0:T(8,128)S(1)}, f32[3,80,512]{2,1,0:T(8,128)S(1)}, f32[3,80,512]{2,1,0:T(8,128)S(1)}) custom-call(s32[4,80]{1,0:T(4,128)S(1)} %get-tuple-element.55.offsets.refs_0_, f32[6,256,512]{2,1,0:T(8,128)S(1)} %copy-done.1), custom_call_target="tpu_custom_call" | custom-call | tf_op jit(solution)/shard_map/trace/pallas_call | solution.py:783
  8.4 0.0 collective-permute-done
  8.5 1.0 %collective-permute-start.1 = (f32[3,80,512]{2,1,0:T(8,128)S(1)}, f32[3,80,512]{2,1,0:T(8,128)S(1)}, u32[]{:S(2)}, u32[]{:S(2)}) collective-permute-start(f32[3,80,512]{2,1,0:T(8,128)S(1)} %get-tuple-element.61), channel_id=1, source_target_pairs={{0,8},{8,0},{16,24},{24,16},{1,9},{9,1},{17,25},{25,17},{2,10},{10... | collective-permute-start | bytes 1474568 | tf_op jit(solution)/shard_map/ppermute | solution.py:707
  9.5 3.0 %collective-permute-start.2 = (f32[3,80,512]{2,1,0:T(8,128)S(1)}, f32[3,80,512]{2,1,0:T(8,128)S(1)}, u32[]{:S(2)}, u32[]{:S(2)}) collective-permute-start(f32[3,80,512]{2,1,0:T(8,128)S(1)} %get-tuple-element.62), channel_id=1, source_target_pairs={{8,16},{16,8},{9,17},{17,9},{10,18},{18,10},{11,19},{19,11},{12,20... | collective-permute-start | bytes 1474568 | tf_op jit(solution)/shard_map/ppermute | solution.py:707
  12.5 3.4 %collective-permute-start.5 = (f32[48,256]{1,0:T(8,128)S(1)}, f32[48,256]{1,0:T(8,128)S(1)}, u32[]{:S(2)}, u32[]{:S(2)}) collective-permute-start(f32[48,256]{1,0:T(8,128)S(1)} %add.6.refs_0_), channel_id=1, source_target_pairs={{0,6},{1,7},{2,4},{3,5},{4,2},{5,3},{6,0},{7,1},{8,14},{9,15},{10,... | collective-permute-start | bytes 147464 | tf_op jit(solution)/shard_map/ppermute | solution.py:712
  15.9 0.0 collective-permute-start.4
  15.9 0.4 collective-permute-start.3
  16.3 2.4 %own0.1.refs_4_ = f32[6,256,512]{2,1,0:T(8,128)S(1)} custom-call(f32[6,256,512]{2,1,0:T(8,128)S(1)} %copy-done.1, f32[4,256,128]{2,1,0:T(8,128)S(1)} %get-tuple-element.58.refs_1_.refs_7_.refs_11_), custom_call_target="tpu_custom_call" | custom-call | tf_op jit(solution)/shard_map/own0/pallas_call | solution.py:798
  18.7 0.0 collective-permute-done.5.refs_3_
  18.7 1.1 %collective-permute-done.4.refs_2_ = f32[48,256]{1,0:T(8,128)S(1)} collective-permute-done((f32[48,256]{1,0:T(8,128)S(1)}, f32[48,256]{1,0:T(8,128)S(1)}, u32[]{:S(2)}, u32[]{:S(2)}) %collective-permute-start.4) | collective-permute-done | bytes 49184 | tf_op jit(solution)/shard_map/ppermute | solution.py:712
  19.8 0.0 collective-permute-done.3.refs_1_
  19.8 0.9 %form0.1 = (bf16[3,256,256]{2,1,0:T(8,128)(2,1)S(1)}, f32[6,256,128]{2,1,0:T(8,128)S(1)}, f32[256,1536]{1,0:T(8,128)S(1)}, f32[256,1536]{1,0:T(8,128)S(1)}, f32[256,1536]{1,0:T(8,128)S(1)}) custom-call(f32[48,256]{1,0:T(8,128)S(1)} %add.6.refs_0_, f32[48,256]{1,0:T(8,128)S(1)} %collective-permute-done.3.refs_1_, ...), custom_call_target="tpu_custom_call" | custom-call | tf_op jit(solution)/shard_map/form0/pallas_call | solution.py:806
  20.7 0.0 collective-permute-done.1.refs_5_
  20.7 0.0 collective-permute-done.2.refs_6_
  20.7 2.7 %mean0.1 = (f32[3712,128]{1,0:T(8,128)S(1)}, f32[1664,128]{1,0:T(8,128)S(1)}, f32[256,512]{1,0:T(8,128)S(1)}, f32[3,256,512]{2,1,0:T(8,128)S(1)}, f32[80,512]{1,0:T(8,128)S(1)}, /*index=5*/f32[80,512]{1,0:T(8,128)S(1)}) custom-call(s32[4,80]{1,0:T(4,128)S(1)} %get-tuple-element.55.offsets.refs_0_, ...), custom_call_target="tpu_custom_call", output_to_operand_aliasing={{0}: (2, {})} | custom-call | tf_op jit(solution)/shard_map/mean0/pallas_call | solution.py:815
  23.5 0.1 collective-permute-start.6
  23.6 3.9 %collective-permute-start.7 = (f32[80,512]{1,0:T(8,128)S(1)}, f32[80,512]{1,0:T(8,128)S(1)}, u32[]{:S(2)}, u32[]{:S(2)}) collective-permute-start(f32[80,512]{1,0:T(8,128)S(1)} %get-tuple-element.78), channel_id=1, source_target_pairs={{8,16},{16,8},{9,17},{17,9},{10,18},{18,10},{11,19},{19,11},{12,20... | collective-permute-start | bytes 491528 | tf_op jit(solution)/shard_map/ppermute | solution.py:707
  27.5 5.3 %rest0.1 = (f32[7424,128]{1,0:T(8,128)S(1)}, f32[5,256,512]{2,1,0:T(8,128)S(1)}, f32[2,256,512]{2,1,0:T(8,128)S(1)}) custom-call(s32[3,256]{1,0:T(4,128)S(1)} %get-tuple-element.56.refs_1_.refs_0_, f32[3712,128]{1,0:T(8,128)S(1)} %get-tuple-element.71.refs_1_, f32[7424,128]{1,0:T(8,128)S(1)} %get-tuple-element.72.refs_2_, ...), custom_call_target="tpu_custom_call", output_to_operand_aliasing={{0}: (2, {})} | custom-call | tf_op jit(solution)/shard_map/rest0/pallas_call | solution.py:835
  32.8 0.0 collective-permute-done.6.refs_5_
  32.9 0.0 collective-permute-done.7.refs_6_
  32.9 3.0 %limit0.1 = (f32[1664,128]{1,0:T(8,128)S(1)}, f32[6,256,512]{2,1,0:T(8,128)S(1)}, f32[48,256]{1,0:T(8,128)S(1)}) custom-call(s32[3,256]{1,0:T(4,128)S(1)} %get-tuple-element.54.refs_0_, f32[1664,128]{1,0:T(8,128)S(1)} %get-tuple-element.69.refs_1_, f32[256,512]{1,0:T(8,128)S(1)} %get-tuple-element.70.refs_2_, ...), custom_call_target="tpu_custom_call", output_to_operand_aliasing={{0}: (1, {})} | custom-call | tf_op jit(solution)/shard_map/limit0/pallas_call | solution.py:849
  35.9 0.4 collective-permute-start.8
  36.3 2.2 %trace.3 = (f32[3712,128]{1,0:T(8,128)S(1)}, f32[7424,128]{1,0:T(8,128)S(1)}, f32[3,80,512]{2,1,0:T(8,128)S(1)}, f32[3,80,512]{2,1,0:T(8,128)S(1)}) custom-call(s32[4,80]{1,0:T(4,128)S(1)} %get-tuple-element.55.offsets.refs_0_, f32[6,256,512]{2,1,0:T(8,128)S(1)} %get-tuple-element.80.z_ref.refs_0_.refs_3_), custom_call_target="tpu_custom_call" | custom-call | tf_op jit(solution)/shard_map/trace/pallas_call | solution.py:783
  38.5 0.4 collective-permute-done.8
  38.9 0.1 collective-permute-start.9
  39.0 3.1 %collective-permute-start.10 = (f32[3,80,512]{2,1,0:T(8,128)S(1)}, f32[3,80,512]{2,1,0:T(8,128)S(1)}, u32[]{:S(2)}, u32[]{:S(2)}) collective-permute-start(f32[3,80,512]{2,1,0:T(8,128)S(1)} %get-tuple-element.86), channel_id=1, source_target_pairs={{8,16},{16,8},{9,17},{17,9},{10,18},{18,10},{11,19},{19,11},{12,20... | collective-permute-start | bytes 1474568 | tf_op jit(solution)/shard_map/ppermute | solution.py:707
  42.1 2.0 %collective-permute-start.13 = (f32[48,256]{1,0:T(8,128)S(1)}, f32[48,256]{1,0:T(8,128)S(1)}, u32[]{:S(2)}, u32[]{:S(2)}) collective-permute-start(f32[48,256]{1,0:T(8,128)S(1)} %add.7.refs_0_), channel_id=1, source_target_pairs={{0,6},{1,7},{2,4},{3,5},{4,2},{5,3},{6,0},{7,1},{8,14},{9,15},{10,... | collective-permute-start | bytes 147464 | tf_op jit(solution)/shard_map/ppermute | solution.py:712
  44.0 0.0 collective-permute-start.12
  44.0 1.6 %collective-permute-start.11 = (f32[48,256]{1,0:T(8,128)S(1)}, f32[48,256]{1,0:T(8,128)S(1)}, u32[]{:S(2)}, u32[]{:S(2)}) collective-permute-start(f32[48,256]{1,0:T(8,128)S(1)} %add.7.refs_0_), channel_id=1, source_target_pairs={{0,2},{1,3},{2,0},{3,1},{4,6},{5,7},{6,4},{7,5},{8,10},{9,11},{10,... | collective-permute-start | bytes 147464 | tf_op jit(solution)/shard_map/ppermute | solution.py:712
  45.7 2.6 %own1.1.refs_4_ = f32[6,256,512]{2,1,0:T(8,128)S(1)} custom-call(f32[6,256,512]{2,1,0:T(8,128)S(1)} %get-tuple-element.80.z_ref.refs_0_.refs_3_, f32[4,256,128]{2,1,0:T(8,128)S(1)} %get-tuple-element.58.refs_1_.refs_7_.refs_11_, f32[6,256,512]{2,1,0:T(8,128)S(1)} %copy-done.1), custom_call_target="tpu_custom_call" | custom-call | tf_op jit(solution)/shard_map/own1/pallas_call | solution.py:798
  48.3 0.0 collective-permute-done.13.refs_3_
  48.3 0.2 collective-permute-done.12.refs_2_
  48.5 0.0 collective-permute-done.11.refs_1_
  48.5 0.9 %form1.1 = (bf16[3,256,256]{2,1,0:T(8,128)(2,1)S(1)}, f32[6,256,128]{2,1,0:T(8,128)S(1)}, f32[256,1536]{1,0:T(8,128)S(1)}, f32[256,1536]{1,0:T(8,128)S(1)}, f32[256,1536]{1,0:T(8,128)S(1)}) custom-call(f32[48,256]{1,0:T(8,128)S(1)} %add.7.refs_0_, f32[48,256]{1,0:T(8,128)S(1)} %collective-permute-done.11.refs_1_, ...), custom_call_target="tpu_custom_call" | custom-call | tf_op jit(solution)/shard_map/form1/pallas_call | solution.py:806
  49.5 0.0 collective-permute-done.9.refs_5_
  49.5 0.0 collective-permute-done.10.refs_6_
  49.5 2.7 %mean1.1 = (f32[3712,128]{1,0:T(8,128)S(1)}, f32[1664,128]{1,0:T(8,128)S(1)}, f32[256,512]{1,0:T(8,128)S(1)}, f32[3,256,512]{2,1,0:T(8,128)S(1)}, f32[80,512]{1,0:T(8,128)S(1)}, /*index=5*/f32[80,512]{1,0:T(8,128)S(1)}) custom-call(s32[4,80]{1,0:T(4,128)S(1)} %get-tuple-element.55.offsets.refs_0_, ...), custom_call_target="tpu_custom_call", output_to_operand_aliasing={{0}: (2, {})} | custom-call | tf_op jit(solution)/shard_map/mean1/pallas_call | solution.py:815
  52.2 0.5 collective-permute-start.14
  52.7 3.3 %collective-permute-start.15 = (f32[80,512]{1,0:T(8,128)S(1)}, f32[80,512]{1,0:T(8,128)S(1)}, u32[]{:S(2)}, u32[]{:S(2)}) collective-permute-start(f32[80,512]{1,0:T(8,128)S(1)} %get-tuple-element.101), channel_id=1, source_target_pairs={{8,16},{16,8},{9,17},{17,9},{10,18},{18,10},{11,19},{19,11},{12,20... | collective-permute-start | bytes 491528 | tf_op jit(solution)/shard_map/ppermute | solution.py:707
  56.0 5.3 %rest1.1 = (f32[7424,128]{1,0:T(8,128)S(1)}, f32[5,256,512]{2,1,0:T(8,128)S(1)}, f32[2,256,512]{2,1,0:T(8,128)S(1)}) custom-call(s32[3,256]{1,0:T(4,128)S(1)} %get-tuple-element.56.refs_1_.refs_0_, f32[3712,128]{1,0:T(8,128)S(1)} %get-tuple-element.94.refs_1_, f32[7424,128]{1,0:T(8,128)S(1)} %get-tuple-element.95.refs_2_, ...), custom_call_target="tpu_custom_call", output_to_operand_aliasing={{0}: (2, {})} | custom-call | tf_op jit(solution)/shard_map/rest1/pallas_call | solution.py:835
  61.3 0.0 collective-permute-done.14.refs_5_
  61.3 0.0 collective-permute-done.15.refs_6_
  61.3 3.0 %limit1.1 = (f32[1664,128]{1,0:T(8,128)S(1)}, f32[6,256,512]{2,1,0:T(8,128)}) custom-call(s32[3,256]{1,0:T(4,128)S(1)} %get-tuple-element.54.refs_0_, f32[1664,128]{1,0:T(8,128)S(1)} %get-tuple-element.92.refs_1_, f32[256,512]{1,0:T(8,128)S(1)} %get-tuple-element.93.refs_2_, ...), custom_call_target="tpu_custom_call", output_to_operand_aliasing={{0}: (1, {})} | custom-call | tf_op jit(solution)/shard_map/limit1/pallas_call | solution.py:849
  (12 shorter events, 0.0 us)
Async XLA Ops:
  0.0 1.9 %copy-start = (f32[6,256,512]{2,1,0:T(8,128)S(1)}, f32[6,256,512]{2,1,0:T(8,128)}, u32[]{:S(2)}) copy-start(f32[6,256,512]{2,1,0:T(8,128)} %refs_2_.1) | copy-start | bytes 9437188
  1.9 3.1 %copy-start.2 = (f32[2,3,256]{2,0,1:T(2,128)S(1)}, f32[2,3,256]{2,0,1:T(2,128)}, u32[]{:S(2)}) copy-start(f32[2,3,256]{2,0,1:T(2,128)} %param.6) | copy-start | bytes 18436
  1.9 3.1 %copy-start.4 = (s32[3,256]{1,0:T(4,128)S(1)}, s32[3,256]{1,0:T(4,128)}, u32[]{:S(2)}) copy-start(s32[3,256]{1,0:T(4,128)} %neigh_ref.1) | copy-start | bytes 9220
  1.9 3.1 %copy-start.5 = (s32[1,2,80]{2,1,0:T(2,128)S(1)}, s32[1,2,80]{2,1,0:T(2,128)}, u32[]{:S(2)}) copy-start(s32[1,2,80]{2,1,0:T(2,128)} %param.8) | copy-start | bytes 1924
  1.9 4.3 %copy-start.1 = (f32[6,256,512]{2,1,0:T(8,128)S(1)}, f32[6,256,512]{2,1,0:T(8,128)}, u32[]{:S(2)}) copy-start(f32[6,256,512]{2,1,0:T(8,128)} %refs_2_.1) | copy-start | bytes 9437188
  2.9 5.5 %collective-permute-start = (f32[48,256]{1,0:T(8,128)S(1)}, f32[48,256]{1,0:T(8,128)S(1)}, u32[]{:S(2)}, u32[]{:S(2)}) collective-permute-start(f32[48,256]{1,0:T(8,128)S(1)} %first.1), channel_id=1, source_target_pairs={{0,1},{1,0},{2,3},{3,2},{4,5},{5,4},{6,7},{7,6},{8,9},{9,8},{10,11... | collective-permute-start | bytes 147464 | tf_op jit(solution)/shard_map/ppermute | solution.py:712
  8.5 12.2 %collective-permute-start.1 = (f32[3,80,512]{2,1,0:T(8,128)S(1)}, f32[3,80,512]{2,1,0:T(8,128)S(1)}, u32[]{:S(2)}, u32[]{:S(2)}) collective-permute-start(f32[3,80,512]{2,1,0:T(8,128)S(1)} %get-tuple-element.61), channel_id=1, source_target_pairs={{0,8},{8,0},{16,24},{24,16},{1,9},{9,1},{17,25},{25,17},{2,10},{10... | collective-permute-start | bytes 1474568 | tf_op jit(solution)/shard_map/ppermute | solution.py:707
  9.5 11.2 %collective-permute-start.2 = (f32[3,80,512]{2,1,0:T(8,128)S(1)}, f32[3,80,512]{2,1,0:T(8,128)S(1)}, u32[]{:S(2)}, u32[]{:S(2)}) collective-permute-start(f32[3,80,512]{2,1,0:T(8,128)S(1)} %get-tuple-element.62), channel_id=1, source_target_pairs={{8,16},{16,8},{9,17},{17,9},{10,18},{18,10},{11,19},{19,11},{12,20... | collective-permute-start | bytes 1474568 | tf_op jit(solution)/shard_map/ppermute | solution.py:707
  12.5 6.2 %collective-permute-start.5 = (f32[48,256]{1,0:T(8,128)S(1)}, f32[48,256]{1,0:T(8,128)S(1)}, u32[]{:S(2)}, u32[]{:S(2)}) collective-permute-start(f32[48,256]{1,0:T(8,128)S(1)} %add.6.refs_0_), channel_id=1, source_target_pairs={{0,6},{1,7},{2,4},{3,5},{4,2},{5,3},{6,0},{7,1},{8,14},{9,15},{10,... | collective-permute-start | bytes 147464 | tf_op jit(solution)/shard_map/ppermute | solution.py:712
  15.9 3.8 %collective-permute-start.4 = (f32[48,256]{1,0:T(8,128)S(1)}, f32[48,256]{1,0:T(8,128)S(1)}, u32[]{:S(2)}, u32[]{:S(2)}) collective-permute-start(f32[48,256]{1,0:T(8,128)S(1)} %add.6.refs_0_), channel_id=1, source_target_pairs={{0,4},{1,5},{2,6},{3,7},{4,0},{5,1},{6,2},{7,3},{8,12},{9,13},{10,... | collective-permute-start | bytes 147464 | tf_op jit(solution)/shard_map/ppermute | solution.py:712
  15.9 3.8 %collective-permute-start.3 = (f32[48,256]{1,0:T(8,128)S(1)}, f32[48,256]{1,0:T(8,128)S(1)}, u32[]{:S(2)}, u32[]{:S(2)}) collective-permute-start(f32[48,256]{1,0:T(8,128)S(1)} %add.6.refs_0_), channel_id=1, source_target_pairs={{0,2},{1,3},{2,0},{3,1},{4,6},{5,7},{6,4},{7,5},{8,10},{9,11},{10,... | collective-permute-start | bytes 147464 | tf_op jit(solution)/shard_map/ppermute | solution.py:712
  16.3 3.5 %copy-start.3 = (f32[256]{0:T(256)S(1)}, f32[256]{0:T(256)}, u32[]{:S(2)}) copy-start(f32[256]{0:T(256)} %param.9) | copy-start | bytes 3076
  23.5 9.4 %collective-permute-start.6 = (f32[80,512]{1,0:T(8,128)S(1)}, f32[80,512]{1,0:T(8,128)S(1)}, u32[]{:S(2)}, u32[]{:S(2)}) collective-permute-start(f32[80,512]{1,0:T(8,128)S(1)} %get-tuple-element.77), channel_id=1, source_target_pairs={{0,8},{8,0},{16,24},{24,16},{1,9},{9,1},{17,25},{25,17},{2,10},{10... | collective-permute-start | bytes 491528 | tf_op jit(solution)/shard_map/ppermute | solution.py:707
  23.6 9.3 %collective-permute-start.7 = (f32[80,512]{1,0:T(8,128)S(1)}, f32[80,512]{1,0:T(8,128)S(1)}, u32[]{:S(2)}, u32[]{:S(2)}) collective-permute-start(f32[80,512]{1,0:T(8,128)S(1)} %get-tuple-element.78), channel_id=1, source_target_pairs={{8,16},{16,8},{9,17},{17,9},{10,18},{18,10},{11,19},{19,11},{12,20... | collective-permute-start | bytes 491528 | tf_op jit(solution)/shard_map/ppermute | solution.py:707
  35.9 3.0 %collective-permute-start.8 = (f32[48,256]{1,0:T(8,128)S(1)}, f32[48,256]{1,0:T(8,128)S(1)}, u32[]{:S(2)}, u32[]{:S(2)}) collective-permute-start(f32[48,256]{1,0:T(8,128)S(1)} %get-tuple-element.84), channel_id=1, source_target_pairs={{0,1},{1,0},{2,3},{3,2},{4,5},{5,4},{6,7},{7,6},{8,9},{9,8},{10,11... | collective-permute-start | bytes 147464 | tf_op jit(solution)/shard_map/ppermute | solution.py:712
  38.9 10.6 %collective-permute-start.9 = (f32[3,80,512]{2,1,0:T(8,128)S(1)}, f32[3,80,512]{2,1,0:T(8,128)S(1)}, u32[]{:S(2)}, u32[]{:S(2)}) collective-permute-start(f32[3,80,512]{2,1,0:T(8,128)S(1)} %get-tuple-element.85), channel_id=1, source_target_pairs={{0,8},{8,0},{16,24},{24,16},{1,9},{9,1},{17,25},{25,17},{2,10},{10... | collective-permute-start | bytes 1474568 | tf_op jit(solution)/shard_map/ppermute | solution.py:707
  39.0 10.5 %collective-permute-start.10 = (f32[3,80,512]{2,1,0:T(8,128)S(1)}, f32[3,80,512]{2,1,0:T(8,128)S(1)}, u32[]{:S(2)}, u32[]{:S(2)}) collective-permute-start(f32[3,80,512]{2,1,0:T(8,128)S(1)} %get-tuple-element.86), channel_id=1, source_target_pairs={{8,16},{16,8},{9,17},{17,9},{10,18},{18,10},{11,19},{19,11},{12,20... | collective-permute-start | bytes 1474568 | tf_op jit(solution)/shard_map/ppermute | solution.py:707
  42.1 6.2 %collective-permute-start.13 = (f32[48,256]{1,0:T(8,128)S(1)}, f32[48,256]{1,0:T(8,128)S(1)}, u32[]{:S(2)}, u32[]{:S(2)}) collective-permute-start(f32[48,256]{1,0:T(8,128)S(1)} %add.7.refs_0_), channel_id=1, source_target_pairs={{0,6},{1,7},{2,4},{3,5},{4,2},{5,3},{6,0},{7,1},{8,14},{9,15},{10,... | collective-permute-start | bytes 147464 | tf_op jit(solution)/shard_map/ppermute | solution.py:712
  44.0 4.5 %collective-permute-start.12 = (f32[48,256]{1,0:T(8,128)S(1)}, f32[48,256]{1,0:T(8,128)S(1)}, u32[]{:S(2)}, u32[]{:S(2)}) collective-permute-start(f32[48,256]{1,0:T(8,128)S(1)} %add.7.refs_0_), channel_id=1, source_target_pairs={{0,4},{1,5},{2,6},{3,7},{4,0},{5,1},{6,2},{7,3},{8,12},{9,13},{10,... | collective-permute-start | bytes 147464 | tf_op jit(solution)/shard_map/ppermute | solution.py:712
  44.0 4.5 %collective-permute-start.11 = (f32[48,256]{1,0:T(8,128)S(1)}, f32[48,256]{1,0:T(8,128)S(1)}, u32[]{:S(2)}, u32[]{:S(2)}) collective-permute-start(f32[48,256]{1,0:T(8,128)S(1)} %add.7.refs_0_), channel_id=1, source_target_pairs={{0,2},{1,3},{2,0},{3,1},{4,6},{5,7},{6,4},{7,5},{8,10},{9,11},{10,... | collective-permute-start | bytes 147464 | tf_op jit(solution)/shard_map/ppermute | solution.py:712
  52.2 9.1 %collective-permute-start.14 = (f32[80,512]{1,0:T(8,128)S(1)}, f32[80,512]{1,0:T(8,128)S(1)}, u32[]{:S(2)}, u32[]{:S(2)}) collective-permute-start(f32[80,512]{1,0:T(8,128)S(1)} %get-tuple-element.100), channel_id=1, source_target_pairs={{0,8},{8,0},{16,24},{24,16},{1,9},{9,1},{17,25},{25,17},{2,10},{10... | collective-permute-start | bytes 491528 | tf_op jit(solution)/shard_map/ppermute | solution.py:707
  52.7 8.6 %collective-permute-start.15 = (f32[80,512]{1,0:T(8,128)S(1)}, f32[80,512]{1,0:T(8,128)S(1)}, u32[]{:S(2)}, u32[]{:S(2)}) collective-permute-start(f32[80,512]{1,0:T(8,128)S(1)} %get-tuple-element.101), channel_id=1, source_target_pairs={{8,16},{16,8},{9,17},{17,9},{10,18},{18,10},{11,19},{19,11},{12,20... | collective-permute-start | bytes 491528 | tf_op jit(solution)/shard_map/ppermute | solution.py:707

commit v5 on v4

--- a/solution.py
+++ b/solution.py
@@ -375,15 +375,8 @@
     qy = qy * weight
     excess = (over * drift_sq - 4.0, -2.0 * over * ux, -2.0 * over * uy, over, over)
     amplitude = jnp.log(nu * density * over * k(1.0 / (2.0 * math.pi)))
-    exponent = (
-        amplitude - 0.5 * over * drift_sq,
-        over * ux,
-        over * uy,
-        -0.5 * over,
-        -0.5 * over,
-    )
     skew = (-(qx * ux + qy * uy), qx, qy)
-    return nu, (excess, exponent, skew)
+    return nu, amplitude - 2.0, (excess, skew)
 
 
 def spread(form, elems):
@@ -397,12 +390,13 @@
     return jnp.concatenate(pieces, axis=0).T.astype(bf16)
 
 
-def relaxed(forms, slot, row, chunk, vel, nu, inside):
+def relaxed(forms, slot, row, chunk, vel, nu, amplitude, inside):
     def form(i):
         return forms[i][pl.ds(row, SUB), pl.ds(slot * vel + chunk * LANE, LANE)]
 
-    skewed = jnp.minimum(jnp.maximum(form(2) * form(0), -skew_multiplier_limit), skew_multiplier_limit)
-    return jnp.exp(form(1)) * (1.0 + skewed) - nu * inside
+    excess = form(0)
+    skewed = jnp.minimum(jnp.maximum(form(1) * excess, -skew_multiplier_limit), skew_multiplier_limit)
+    return jnp.exp(amplitude - 0.5 * excess) * (1.0 + skewed) - nu * inside
 
 
 def form_kernel(*refs, parts, section):
@@ -414,8 +408,8 @@
     moments = mom_refs[0][...]
     for ref in mom_refs[1:]:
         moments = moments + ref[...]
-    nu, coefficients = node_parameters(moments, rate[...], elems, scale)
-    put_columns([nu[n : n + 1, :] for n in range(MODES)], nus)
+    nu, amplitude, coefficients = node_parameters(moments, rate[...], elems, scale)
+    put_columns([value[n : n + 1, :] for value in (nu, amplitude) for n in range(MODES)], nus)
     for i, form in enumerate(coefficients):
         spreads[i] = spread(form, elems)
         forms[i][...] = jnp.dot(spreads[i], basis[:, pl.ds(half, half)], preferred_element_type=f32)
@@ -477,8 +471,8 @@
 
 
 def mean_kernel(offsets, src, _, z_ref, own, near_in, far_in, cols, nus, *refs, section):
-    forms = refs[:3]
-    refs = refs[3:]
+    forms = refs[:2]
+    refs = refs[2:]
     tbl, mtbl, centre, high, near, far, stage_a, stage_b, stage = refs
     elems, vel = z_ref.shape[1:]
     chunks = vel // LANE
@@ -504,6 +498,7 @@
     def compute(row, stage):
         flows = flow_forms(cols, grid, row, section == 1)
         nu_cols = [nus[n, pl.ds(row, SUB), :] for n in range(3, MODES)]
+        amp_cols = [nus[MODES + n, pl.ds(row, SUB), :] for n in range(3, MODES)]
         for c in range(chunks):
             z0, z1, z2, z3, z4, z5 = modes_at(z_ref, row, c)
             through = None
@@ -521,7 +516,7 @@
                 e34 + o34,
                 a0 + z1 * k(N[5, 1]) + z3 * k(N[5, 3]) + z5 * k(N[5, 5]),
             )
-            H = [relaxed(forms, n, row, c, vel, nu_cols[n], inside[n]) for n in range(3)]
+            H = [relaxed(forms, n, row, c, vel, nu_cols[n], amp_cols[n], inside[n]) for n in range(3)]
             value = moved + (H[0] + H[1] + H[2]) * k(V[0, 3])
             centre[at(row, c)] = value
             mtbl[pl.ds(row * chunks + c, SUB, stride=chunks), :] = value
@@ -563,7 +558,7 @@
 
     over_groups(slots, fill_border)
 
-    for i in range(3):
+    for i in range(2):
         forms[i][...] = jnp.dot(
             spreads[i], basis[:, pl.ds(0, 3 * vel)], preferred_element_type=f32
         )
@@ -581,6 +576,7 @@
     def compute(row, stage):
         flows = flow_forms(cols, grid, row, section == 1)
         nu_cols = [nus[n, pl.ds(row, SUB), :] for n in range(3)]
+        amp_cols = [nus[MODES + n, pl.ds(row, SUB), :] for n in range(3)]
         for c in range(chunks):
             z = modes_at(z_ref, row, c)
             z0, z1, z2, z3, z4, z5 = z
@@ -598,7 +594,7 @@
             e02 = a0 + z1 * k(N[0, 1]) + z3 * k(N[0, 3]) + z5 * k(N[0, 5])
             o02 = z2 * k(N[2, 2]) + z4 * k(N[2, 4])
             inside = (e02 - o02, a0 + z1 * k(N[1, 1]) + z3 * k(N[1, 3]), e02 + o02)
-            H = [relaxed(forms, n, row, c, vel, nu_cols[n], inside[n]) for n in range(3)]
+            H = [relaxed(forms, n, row, c, vel, nu_cols[n], amp_cols[n], inside[n]) for n in range(3)]
             H += [high[(n, *at(row, c))] for n in range(3)]
             s02 = H[0] + H[2]
             d20 = H[2] - H[0]
@@ -747,7 +743,7 @@
         return pltpu.VMEM((count, LANE), f32)
 
     def evaluated():
-        return [pltpu.VMEM((elems, 3 * vel), f32) for _ in range(3)]
+        return [pltpu.VMEM((elems, 3 * vel), f32) for _ in range(2)]
 
     rate = collision_rate.reshape(1, elems)
     index = S(neighbour.shape, jnp.int32)
@@ -805,9 +801,10 @@
         )(current, cols, *base)
         spreads, nus, *forms = pl.pallas_call(
             lambda *refs, section=section: form_kernel(*refs, parts=len(parts), section=section),
-            out_shape=(S((3, elems, TERMS * SUB), bf16), S((modes, elems, LANE), f32)) + (S((elems, 3 * vel), f32),) * 3,
+            out_shape=(S((2, elems, TERMS * SUB), bf16), S((2 * modes, elems, LANE), f32))
+            + (S((elems, 3 * vel), f32),) * 2,
             in_specs=[vmem] * (len(parts) + 2),
-            out_specs=(vmem,) * 5,
+            out_specs=(vmem,) * 4,
             compiler_params=params(16),
             name=f"form{section}",
         )(*parts, rate, basis)
@@ -823,7 +820,7 @@
                 one,
             ),
             input_output_aliases={2: 0},
-            in_specs=[smem] * 2 + [vmem] * 10,
+            in_specs=[smem] * 2 + [vmem] * 9,
             out_specs=(vmem,) * 6,
             scratch_shapes=[buffer(3 * SUB * chunks)] * 2 + [buffer(2 * slots * chunks)],
             compiler_params=params(16),

time: 64.7 us -> 63.7 us (0.985)
  no operation moved by 1% of the time
where the time goes in v5:
time: 63.7 us; the launch traced here: 63.5 us
  Pallas kernels  35.1 us (55%)
  starting transfers between devices  24.6 us (39%)
  local copies, waits for them, and re-layouts  1.91 us (3%)
  waiting for transfers between devices  1.67 us (3%)
    ppermute x8, starting transfers between devices, traded(): return lax.ppermute(value, 'space', pairs)  14.8 us
    pallas_call x2, Pallas kernels, on_device(): pl.pallas_call(lambda *refs, section=section: rest_kernel(*refs, section=...  10.4 us
    ppermute x8, starting transfers between devices, swapped(): return lax.ppermute(value, 'vel', [(i, i ^ bits) for i in range(peers)])  9.82 us
    pallas_call x2, Pallas kernels, on_device(): pl.pallas_call(lambda *refs, section=section: limit_kernel(*refs, section...  6.07 us
    pallas_call x2, Pallas kernels, on_device(): pl.pallas_call(lambda *refs, section=section: mean_kernel(*refs, section=...  5.47 us
    pallas_call x2, Pallas kernels, on_device(): pl.pallas_call(lambda *refs, section=section: own_kernel(*refs, section=s...  5.04 us
    pallas_call x2, Pallas kernels, on_device(): pl.pallas_call(trace_kernel, out_shape=(S((rows * chunks, LANE), f32), S(...  4.43 us
    unnamed x12, local copies, waits for them, and re-layouts  1.91 us
  transfers between devices with their start and end apart: 16, of which 3 were waited for; matrix products, arithmetic and copies ran while one was open for 0% of the time, Pallas kernels for 36%

profile of v5, /device:TPU:1, one launch (start us, length us, event | category | flops | bytes accessed | tf_op | source)
XLA Modules:
  0.0 63.5 jit_solution(2725706183635613575)
XLA Ops:
  0.0 1.9 %copy-done = f32[6,256,512]{2,1,0:T(8,128)S(1)} copy-done((f32[6,256,512]{2,1,0:T(8,128)S(1)}, f32[6,256,512]{2,1,0:T(8,128)}, u32[]{:S(2)}) %copy-start) | copy-done | bytes 3145752
  1.9 1.0 %first.1 = f32[48,256]{1,0:T(8,128)S(1)} custom-call(f32[6,256,512]{2,1,0:T(8,128)S(1)} %copy-done), custom_call_target="tpu_custom_call" | custom-call | tf_op jit(solution)/shard_map/first/pallas_call | solution.py:767
  2.9 2.1 %collective-permute-start = (f32[48,256]{1,0:T(8,128)S(1)}, f32[48,256]{1,0:T(8,128)S(1)}, u32[]{:S(2)}, u32[]{:S(2)}) collective-permute-start(f32[48,256]{1,0:T(8,128)S(1)} %first.1), channel_id=1, source_target_pairs={{0,1},{1,0},{2,3},{3,2},{4,5},{5,4},{6,7},{7,6},{8,9},{9,8},{10,11... | collective-permute-start | bytes 147464 | tf_op jit(solution)/shard_map/ppermute | solution.py:708
  5.0 0.0 copy-done.4
  5.0 1.2 %prepare.1 = (s32[3,256]{1,0:T(4,128)S(1)}, s32[3,256]{1,0:T(4,128)S(1)}, s32[4,80]{1,0:T(4,128)S(1)}, bf16[256,3072]{1,0:T(8,128)(2,1)S(1)}, f32[4,256,128]{2,1,0:T(8,128)S(1)}, /*index=5*/bf16[32,512]{1,0:T(8,128)(2,1)S(1)}) custom-call(s32[2,80]{1,0:T(2,128)S(1)} %bitcast.6, s32[3,256]{1,0:T(4,128)S(1)} %copy-done.4, s32[2,80]{1,0:T(2,128)S(1)} %bitcast.7, ...), custom_call_target="tpu_custom_call" | custom-call | tf_op jit(solution)/shard_map/prepare/pallas_call | solution.py:750
  6.2 2.2 %trace.2 = (f32[3712,128]{1,0:T(8,128)S(1)}, f32[7424,128]{1,0:T(8,128)S(1)}, f32[3,80,512]{2,1,0:T(8,128)S(1)}, f32[3,80,512]{2,1,0:T(8,128)S(1)}) custom-call(s32[4,80]{1,0:T(4,128)S(1)} %get-tuple-element.53.offsets.refs_0_, f32[6,256,512]{2,1,0:T(8,128)S(1)} %copy-done.1), custom_call_target="tpu_custom_call" | custom-call | tf_op jit(solution)/shard_map/trace/pallas_call | solution.py:779
  8.4 0.0 collective-permute-done
  8.5 1.0 %collective-permute-start.1 = (f32[3,80,512]{2,1,0:T(8,128)S(1)}, f32[3,80,512]{2,1,0:T(8,128)S(1)}, u32[]{:S(2)}, u32[]{:S(2)}) collective-permute-start(f32[3,80,512]{2,1,0:T(8,128)S(1)} %get-tuple-element.59), channel_id=1, source_target_pairs={{0,8},{8,0},{16,24},{24,16},{1,9},{9,1},{17,25},{25,17},{2,10},{10... | collective-permute-start | bytes 1474568 | tf_op jit(solution)/shard_map/ppermute | solution.py:703
  9.5 3.0 %collective-permute-start.2 = (f32[3,80,512]{2,1,0:T(8,128)S(1)}, f32[3,80,512]{2,1,0:T(8,128)S(1)}, u32[]{:S(2)}, u32[]{:S(2)}) collective-permute-start(f32[3,80,512]{2,1,0:T(8,128)S(1)} %get-tuple-element.60), channel_id=1, source_target_pairs={{8,16},{16,8},{9,17},{17,9},{10,18},{18,10},{11,19},{19,11},{12,20... | collective-permute-start | bytes 1474568 | tf_op jit(solution)/shard_map/ppermute | solution.py:703
  12.5 3.4 %collective-permute-start.5 = (f32[48,256]{1,0:T(8,128)S(1)}, f32[48,256]{1,0:T(8,128)S(1)}, u32[]{:S(2)}, u32[]{:S(2)}) collective-permute-start(f32[48,256]{1,0:T(8,128)S(1)} %add.6.refs_0_), channel_id=1, source_target_pairs={{0,6},{1,7},{2,4},{3,5},{4,2},{5,3},{6,0},{7,1},{8,14},{9,15},{10,... | collective-permute-start | bytes 147464 | tf_op jit(solution)/shard_map/ppermute | solution.py:708
  15.9 0.0 collective-permute-start.4
  15.9 0.4 collective-permute-start.3
  16.3 2.4 %own0.1.refs_4_ = f32[6,256,512]{2,1,0:T(8,128)S(1)} custom-call(f32[6,256,512]{2,1,0:T(8,128)S(1)} %copy-done.1, f32[4,256,128]{2,1,0:T(8,128)S(1)} %get-tuple-element.56.refs_1_.refs_7_.refs_11_), custom_call_target="tpu_custom_call" | custom-call | tf_op jit(solution)/shard_map/own0/pallas_call | solution.py:794
  18.7 0.0 collective-permute-done.5.refs_3_
  18.7 1.0 %collective-permute-done.4.refs_2_ = f32[48,256]{1,0:T(8,128)S(1)} collective-permute-done((f32[48,256]{1,0:T(8,128)S(1)}, f32[48,256]{1,0:T(8,128)S(1)}, u32[]{:S(2)}, u32[]{:S(2)}) %collective-permute-start.4) | collective-permute-done | bytes 49184 | tf_op jit(solution)/shard_map/ppermute | solution.py:708
  19.8 0.0 collective-permute-done.3.refs_1_
  19.8 0.8 %form0.1 = (bf16[2,256,256]{2,1,0:T(8,128)(2,1)S(1)}, f32[12,256,128]{2,1,0:T(8,128)S(1)}, f32[256,1536]{1,0:T(8,128)S(1)}, f32[256,1536]{1,0:T(8,128)S(1)}) custom-call(f32[48,256]{1,0:T(8,128)S(1)} %add.6.refs_0_, f32[48,256]{1,0:T(8,128)S(1)} %collective-permute-done.3.refs_1_, f32[48,256]{1,0:T(8,128)S(1)} %collective-permute-done.4.refs_2_, ...), custom_call_target="tpu_custom_call" | custom-call | tf_op jit(solution)/shard_map/form0/pallas_call | solution.py:802
  20.5 0.0 collective-permute-done.1.refs_5_
  20.6 0.0 collective-permute-done.2.refs_6_
  20.6 2.7 %mean0.1 = (f32[3712,128]{1,0:T(8,128)S(1)}, f32[1664,128]{1,0:T(8,128)S(1)}, f32[256,512]{1,0:T(8,128)S(1)}, f32[3,256,512]{2,1,0:T(8,128)S(1)}, f32[80,512]{1,0:T(8,128)S(1)}, /*index=5*/f32[80,512]{1,0:T(8,128)S(1)}) custom-call(s32[4,80]{1,0:T(4,128)S(1)} %get-tuple-element.53.offsets.refs_0_, ...), custom_call_target="tpu_custom_call", output_to_operand_aliasing={{0}: (2, {})} | custom-call | tf_op jit(solution)/shard_map/mean0/pallas_call | solution.py:812
  23.3 0.1 collective-permute-start.6
  23.4 3.9 %collective-permute-start.7 = (f32[80,512]{1,0:T(8,128)S(1)}, f32[80,512]{1,0:T(8,128)S(1)}, u32[]{:S(2)}, u32[]{:S(2)}) collective-permute-start(f32[80,512]{1,0:T(8,128)S(1)} %get-tuple-element.75), channel_id=1, source_target_pairs={{8,16},{16,8},{9,17},{17,9},{10,18},{18,10},{11,19},{19,11},{12,20... | collective-permute-start | bytes 491528 | tf_op jit(solution)/shard_map/ppermute | solution.py:703
  27.3 5.2 %rest0.1 = (f32[7424,128]{1,0:T(8,128)S(1)}, f32[5,256,512]{2,1,0:T(8,128)S(1)}, f32[2,256,512]{2,1,0:T(8,128)S(1)}) custom-call(s32[3,256]{1,0:T(4,128)S(1)} %get-tuple-element.54.refs_1_.refs_0_, f32[3712,128]{1,0:T(8,128)S(1)} %get-tuple-element.68.refs_1_, f32[7424,128]{1,0:T(8,128)S(1)} %get-tuple-element.69.refs_2_, ...), custom_call_target="tpu_custom_call", output_to_operand_aliasing={{0}: (2, {})} | custom-call | tf_op jit(solution)/shard_map/rest0/pallas_call | solution.py:832
  32.5 0.0 collective-permute-done.6.refs_5_
  32.5 0.0 collective-permute-done.7.refs_6_
  32.5 3.0 %limit0.1 = (f32[1664,128]{1,0:T(8,128)S(1)}, f32[6,256,512]{2,1,0:T(8,128)S(1)}, f32[48,256]{1,0:T(8,128)S(1)}) custom-call(s32[3,256]{1,0:T(4,128)S(1)} %get-tuple-element.52.refs_0_, f32[1664,128]{1,0:T(8,128)S(1)} %get-tuple-element.66.refs_1_, f32[256,512]{1,0:T(8,128)S(1)} %get-tuple-element.67.refs_2_, ...), custom_call_target="tpu_custom_call", output_to_operand_aliasing={{0}: (1, {})} | custom-call | tf_op jit(solution)/shard_map/limit0/pallas_call | solution.py:846
  35.6 0.4 collective-permute-start.8
  36.0 2.2 %trace.3 = (f32[3712,128]{1,0:T(8,128)S(1)}, f32[7424,128]{1,0:T(8,128)S(1)}, f32[3,80,512]{2,1,0:T(8,128)S(1)}, f32[3,80,512]{2,1,0:T(8,128)S(1)}) custom-call(s32[4,80]{1,0:T(4,128)S(1)} %get-tuple-element.53.offsets.refs_0_, f32[6,256,512]{2,1,0:T(8,128)S(1)} %get-tuple-element.77.z_ref.refs_0_.refs_3_), custom_call_target="tpu_custom_call" | custom-call | tf_op jit(solution)/shard_map/trace/pallas_call | solution.py:779
  38.2 0.4 collective-permute-done.8
  38.6 0.1 collective-permute-start.9
  38.7 3.1 %collective-permute-start.10 = (f32[3,80,512]{2,1,0:T(8,128)S(1)}, f32[3,80,512]{2,1,0:T(8,128)S(1)}, u32[]{:S(2)}, u32[]{:S(2)}) collective-permute-start(f32[3,80,512]{2,1,0:T(8,128)S(1)} %get-tuple-element.83), channel_id=1, source_target_pairs={{8,16},{16,8},{9,17},{17,9},{10,18},{18,10},{11,19},{19,11},{12,20... | collective-permute-start | bytes 1474568 | tf_op jit(solution)/shard_map/ppermute | solution.py:703
  41.7 2.2 %collective-permute-start.13 = (f32[48,256]{1,0:T(8,128)S(1)}, f32[48,256]{1,0:T(8,128)S(1)}, u32[]{:S(2)}, u32[]{:S(2)}) collective-permute-start(f32[48,256]{1,0:T(8,128)S(1)} %add.7.refs_0_), channel_id=1, source_target_pairs={{0,6},{1,7},{2,4},{3,5},{4,2},{5,3},{6,0},{7,1},{8,14},{9,15},{10,... | collective-permute-start | bytes 147464 | tf_op jit(solution)/shard_map/ppermute | solution.py:708
  43.9 0.0 collective-permute-start.12
  43.9 1.5 %collective-permute-start.11 = (f32[48,256]{1,0:T(8,128)S(1)}, f32[48,256]{1,0:T(8,128)S(1)}, u32[]{:S(2)}, u32[]{:S(2)}) collective-permute-start(f32[48,256]{1,0:T(8,128)S(1)} %add.7.refs_0_), channel_id=1, source_target_pairs={{0,2},{1,3},{2,0},{3,1},{4,6},{5,7},{6,4},{7,5},{8,10},{9,11},{10,... | collective-permute-start | bytes 147464 | tf_op jit(solution)/shard_map/ppermute | solution.py:708
  45.4 2.6 %own1.1.refs_4_ = f32[6,256,512]{2,1,0:T(8,128)S(1)} custom-call(f32[6,256,512]{2,1,0:T(8,128)S(1)} %get-tuple-element.77.z_ref.refs_0_.refs_3_, f32[4,256,128]{2,1,0:T(8,128)S(1)} %get-tuple-element.56.refs_1_.refs_7_.refs_11_, f32[6,256,512]{2,1,0:T(8,128)S(1)} %copy-done.1), custom_call_target="tpu_custom_call" | custom-call | tf_op jit(solution)/shard_map/own1/pallas_call | solution.py:794
  48.0 0.0 collective-permute-done.13.refs_3_
  48.0 0.2 collective-permute-done.12.refs_2_
  48.2 0.0 collective-permute-done.11.refs_1_
  48.2 0.8 %form1.1 = (bf16[2,256,256]{2,1,0:T(8,128)(2,1)S(1)}, f32[12,256,128]{2,1,0:T(8,128)S(1)}, f32[256,1536]{1,0:T(8,128)S(1)}, f32[256,1536]{1,0:T(8,128)S(1)}) custom-call(f32[48,256]{1,0:T(8,128)S(1)} %add.7.refs_0_, f32[48,256]{1,0:T(8,128)S(1)} %collective-permute-done.11.refs_1_, f32[48,256]{1,0:T(8,128)S(1)} %collective-permute-done.12.refs_2_, ...), custom_call_target="tpu_custom_call" | custom-call | tf_op jit(solution)/shard_map/form1/pallas_call | solution.py:802
  49.0 0.0 collective-permute-done.9.refs_5_
  49.0 0.0 collective-permute-done.10.refs_6_
  49.0 2.7 %mean1.1 = (f32[3712,128]{1,0:T(8,128)S(1)}, f32[1664,128]{1,0:T(8,128)S(1)}, f32[256,512]{1,0:T(8,128)S(1)}, f32[3,256,512]{2,1,0:T(8,128)S(1)}, f32[80,512]{1,0:T(8,128)S(1)}, /*index=5*/f32[80,512]{1,0:T(8,128)S(1)}) custom-call(s32[4,80]{1,0:T(4,128)S(1)} %get-tuple-element.53.offsets.refs_0_, ...), custom_call_target="tpu_custom_call", output_to_operand_aliasing={{0}: (2, {})} | custom-call | tf_op jit(solution)/shard_map/mean1/pallas_call | solution.py:812
  51.7 0.3 collective-permute-start.14
  52.1 3.2 %collective-permute-start.15 = (f32[80,512]{1,0:T(8,128)S(1)}, f32[80,512]{1,0:T(8,128)S(1)}, u32[]{:S(2)}, u32[]{:S(2)}) collective-permute-start(f32[80,512]{1,0:T(8,128)S(1)} %get-tuple-element.97), channel_id=1, source_target_pairs={{8,16},{16,8},{9,17},{17,9},{10,18},{18,10},{11,19},{19,11},{12,20... | collective-permute-start | bytes 491528 | tf_op jit(solution)/shard_map/ppermute | solution.py:703
  55.3 5.2 %rest1.1 = (f32[7424,128]{1,0:T(8,128)S(1)}, f32[5,256,512]{2,1,0:T(8,128)S(1)}, f32[2,256,512]{2,1,0:T(8,128)S(1)}) custom-call(s32[3,256]{1,0:T(4,128)S(1)} %get-tuple-element.54.refs_1_.refs_0_, f32[3712,128]{1,0:T(8,128)S(1)} %get-tuple-element.90.refs_1_, f32[7424,128]{1,0:T(8,128)S(1)} %get-tuple-element.91.refs_2_, ...), custom_call_target="tpu_custom_call", output_to_operand_aliasing={{0}: (2, {})} | custom-call | tf_op jit(solution)/shard_map/rest1/pallas_call | solution.py:832
  60.5 0.0 collective-permute-done.14.refs_5_
  60.5 0.0 collective-permute-done.15.refs_6_
  60.5 3.0 %limit1.1 = (f32[1664,128]{1,0:T(8,128)S(1)}, f32[6,256,512]{2,1,0:T(8,128)}) custom-call(s32[3,256]{1,0:T(4,128)S(1)} %get-tuple-element.52.refs_0_, f32[1664,128]{1,0:T(8,128)S(1)} %get-tuple-element.88.refs_1_, f32[256,512]{1,0:T(8,128)S(1)} %get-tuple-element.89.refs_2_, ...), custom_call_target="tpu_custom_call", output_to_operand_aliasing={{0}: (1, {})} | custom-call | tf_op jit(solution)/shard_map/limit1/pallas_call | solution.py:846
  (12 shorter events, 0.0 us)
Async XLA Ops:
  0.0 1.9 %copy-start = (f32[6,256,512]{2,1,0:T(8,128)S(1)}, f32[6,256,512]{2,1,0:T(8,128)}, u32[]{:S(2)}) copy-start(f32[6,256,512]{2,1,0:T(8,128)} %refs_2_.1) | copy-start | bytes 9437188
  1.9 3.1 %copy-start.2 = (f32[2,3,256]{2,0,1:T(2,128)S(1)}, f32[2,3,256]{2,0,1:T(2,128)}, u32[]{:S(2)}) copy-start(f32[2,3,256]{2,0,1:T(2,128)} %param.6) | copy-start | bytes 18436
  1.9 3.1 %copy-start.4 = (s32[3,256]{1,0:T(4,128)S(1)}, s32[3,256]{1,0:T(4,128)}, u32[]{:S(2)}) copy-start(s32[3,256]{1,0:T(4,128)} %neigh_ref.1) | copy-start | bytes 9220
  1.9 3.1 %copy-start.5 = (s32[1,2,80]{2,1,0:T(2,128)S(1)}, s32[1,2,80]{2,1,0:T(2,128)}, u32[]{:S(2)}) copy-start(s32[1,2,80]{2,1,0:T(2,128)} %param.8) | copy-start | bytes 1924
  1.9 4.3 %copy-start.1 = (f32[6,256,512]{2,1,0:T(8,128)S(1)}, f32[6,256,512]{2,1,0:T(8,128)}, u32[]{:S(2)}) copy-start(f32[6,256,512]{2,1,0:T(8,128)} %refs_2_.1) | copy-start | bytes 9437188
  2.9 5.5 %collective-permute-start = (f32[48,256]{1,0:T(8,128)S(1)}, f32[48,256]{1,0:T(8,128)S(1)}, u32[]{:S(2)}, u32[]{:S(2)}) collective-permute-start(f32[48,256]{1,0:T(8,128)S(1)} %first.1), channel_id=1, source_target_pairs={{0,1},{1,0},{2,3},{3,2},{4,5},{5,4},{6,7},{7,6},{8,9},{9,8},{10,11... | collective-permute-start | bytes 147464 | tf_op jit(solution)/shard_map/ppermute | solution.py:708
  8.5 12.1 %collective-permute-start.1 = (f32[3,80,512]{2,1,0:T(8,128)S(1)}, f32[3,80,512]{2,1,0:T(8,128)S(1)}, u32[]{:S(2)}, u32[]{:S(2)}) collective-permute-start(f32[3,80,512]{2,1,0:T(8,128)S(1)} %get-tuple-element.59), channel_id=1, source_target_pairs={{0,8},{8,0},{16,24},{24,16},{1,9},{9,1},{17,25},{25,17},{2,10},{10... | collective-permute-start | bytes 1474568 | tf_op jit(solution)/shard_map/ppermute | solution.py:703
  9.5 11.1 %collective-permute-start.2 = (f32[3,80,512]{2,1,0:T(8,128)S(1)}, f32[3,80,512]{2,1,0:T(8,128)S(1)}, u32[]{:S(2)}, u32[]{:S(2)}) collective-permute-start(f32[3,80,512]{2,1,0:T(8,128)S(1)} %get-tuple-element.60), channel_id=1, source_target_pairs={{8,16},{16,8},{9,17},{17,9},{10,18},{18,10},{11,19},{19,11},{12,20... | collective-permute-start | bytes 1474568 | tf_op jit(solution)/shard_map/ppermute | solution.py:703
  12.5 6.2 %collective-permute-start.5 = (f32[48,256]{1,0:T(8,128)S(1)}, f32[48,256]{1,0:T(8,128)S(1)}, u32[]{:S(2)}, u32[]{:S(2)}) collective-permute-start(f32[48,256]{1,0:T(8,128)S(1)} %add.6.refs_0_), channel_id=1, source_target_pairs={{0,6},{1,7},{2,4},{3,5},{4,2},{5,3},{6,0},{7,1},{8,14},{9,15},{10,... | collective-permute-start | bytes 147464 | tf_op jit(solution)/shard_map/ppermute | solution.py:708
  15.9 3.8 %collective-permute-start.4 = (f32[48,256]{1,0:T(8,128)S(1)}, f32[48,256]{1,0:T(8,128)S(1)}, u32[]{:S(2)}, u32[]{:S(2)}) collective-permute-start(f32[48,256]{1,0:T(8,128)S(1)} %add.6.refs_0_), channel_id=1, source_target_pairs={{0,4},{1,5},{2,6},{3,7},{4,0},{5,1},{6,2},{7,3},{8,12},{9,13},{10,... | collective-permute-start | bytes 147464 | tf_op jit(solution)/shard_map/ppermute | solution.py:708
  15.9 3.8 %collective-permute-start.3 = (f32[48,256]{1,0:T(8,128)S(1)}, f32[48,256]{1,0:T(8,128)S(1)}, u32[]{:S(2)}, u32[]{:S(2)}) collective-permute-start(f32[48,256]{1,0:T(8,128)S(1)} %add.6.refs_0_), channel_id=1, source_target_pairs={{0,2},{1,3},{2,0},{3,1},{4,6},{5,7},{6,4},{7,5},{8,10},{9,11},{10,... | collective-permute-start | bytes 147464 | tf_op jit(solution)/shard_map/ppermute | solution.py:708
  16.3 3.5 %copy-start.3 = (f32[256]{0:T(256)S(1)}, f32[256]{0:T(256)}, u32[]{:S(2)}) copy-start(f32[256]{0:T(256)} %param.9) | copy-start | bytes 3076
  23.3 9.2 %collective-permute-start.6 = (f32[80,512]{1,0:T(8,128)S(1)}, f32[80,512]{1,0:T(8,128)S(1)}, u32[]{:S(2)}, u32[]{:S(2)}) collective-permute-start(f32[80,512]{1,0:T(8,128)S(1)} %get-tuple-element.74), channel_id=1, source_target_pairs={{0,8},{8,0},{16,24},{24,16},{1,9},{9,1},{17,25},{25,17},{2,10},{10... | collective-permute-start | bytes 491528 | tf_op jit(solution)/shard_map/ppermute | solution.py:703
  23.4 9.2 %collective-permute-start.7 = (f32[80,512]{1,0:T(8,128)S(1)}, f32[80,512]{1,0:T(8,128)S(1)}, u32[]{:S(2)}, u32[]{:S(2)}) collective-permute-start(f32[80,512]{1,0:T(8,128)S(1)} %get-tuple-element.75), channel_id=1, source_target_pairs={{8,16},{16,8},{9,17},{17,9},{10,18},{18,10},{11,19},{19,11},{12,20... | collective-permute-start | bytes 491528 | tf_op jit(solution)/shard_map/ppermute | solution.py:703
  35.6 3.0 %collective-permute-start.8 = (f32[48,256]{1,0:T(8,128)S(1)}, f32[48,256]{1,0:T(8,128)S(1)}, u32[]{:S(2)}, u32[]{:S(2)}) collective-permute-start(f32[48,256]{1,0:T(8,128)S(1)} %get-tuple-element.81), channel_id=1, source_target_pairs={{0,1},{1,0},{2,3},{3,2},{4,5},{5,4},{6,7},{7,6},{8,9},{9,8},{10,11... | collective-permute-start | bytes 147464 | tf_op jit(solution)/shard_map/ppermute | solution.py:708
  38.6 10.4 %collective-permute-start.9 = (f32[3,80,512]{2,1,0:T(8,128)S(1)}, f32[3,80,512]{2,1,0:T(8,128)S(1)}, u32[]{:S(2)}, u32[]{:S(2)}) collective-permute-start(f32[3,80,512]{2,1,0:T(8,128)S(1)} %get-tuple-element.82), channel_id=1, source_target_pairs={{0,8},{8,0},{16,24},{24,16},{1,9},{9,1},{17,25},{25,17},{2,10},{10... | collective-permute-start | bytes 1474568 | tf_op jit(solution)/shard_map/ppermute | solution.py:703
  38.7 10.3 %collective-permute-start.10 = (f32[3,80,512]{2,1,0:T(8,128)S(1)}, f32[3,80,512]{2,1,0:T(8,128)S(1)}, u32[]{:S(2)}, u32[]{:S(2)}) collective-permute-start(f32[3,80,512]{2,1,0:T(8,128)S(1)} %get-tuple-element.83), channel_id=1, source_target_pairs={{8,16},{16,8},{9,17},{17,9},{10,18},{18,10},{11,19},{19,11},{12,20... | collective-permute-start | bytes 1474568 | tf_op jit(solution)/shard_map/ppermute | solution.py:703
  41.7 6.2 %collective-permute-start.13 = (f32[48,256]{1,0:T(8,128)S(1)}, f32[48,256]{1,0:T(8,128)S(1)}, u32[]{:S(2)}, u32[]{:S(2)}) collective-permute-start(f32[48,256]{1,0:T(8,128)S(1)} %add.7.refs_0_), channel_id=1, source_target_pairs={{0,6},{1,7},{2,4},{3,5},{4,2},{5,3},{6,0},{7,1},{8,14},{9,15},{10,... | collective-permute-start | bytes 147464 | tf_op jit(solution)/shard_map/ppermute | solution.py:708
  43.9 4.3 %collective-permute-start.12 = (f32[48,256]{1,0:T(8,128)S(1)}, f32[48,256]{1,0:T(8,128)S(1)}, u32[]{:S(2)}, u32[]{:S(2)}) collective-permute-start(f32[48,256]{1,0:T(8,128)S(1)} %add.7.refs_0_), channel_id=1, source_target_pairs={{0,4},{1,5},{2,6},{3,7},{4,0},{5,1},{6,2},{7,3},{8,12},{9,13},{10,... | collective-permute-start | bytes 147464 | tf_op jit(solution)/shard_map/ppermute | solution.py:708
  43.9 4.3 %collective-permute-start.11 = (f32[48,256]{1,0:T(8,128)S(1)}, f32[48,256]{1,0:T(8,128)S(1)}, u32[]{:S(2)}, u32[]{:S(2)}) collective-permute-start(f32[48,256]{1,0:T(8,128)S(1)} %add.7.refs_0_), channel_id=1, source_target_pairs={{0,2},{1,3},{2,0},{3,1},{4,6},{5,7},{6,4},{7,5},{8,10},{9,11},{10,... | collective-permute-start | bytes 147464 | tf_op jit(solution)/shard_map/ppermute | solution.py:708
  51.7 8.8 %collective-permute-start.14 = (f32[80,512]{1,0:T(8,128)S(1)}, f32[80,512]{1,0:T(8,128)S(1)}, u32[]{:S(2)}, u32[]{:S(2)}) collective-permute-start(f32[80,512]{1,0:T(8,128)S(1)} %get-tuple-element.96), channel_id=1, source_target_pairs={{0,8},{8,0},{16,24},{24,16},{1,9},{9,1},{17,25},{25,17},{2,10},{10... | collective-permute-start | bytes 491528 | tf_op jit(solution)/shard_map/ppermute | solution.py:703
  52.1 8.4 %collective-permute-start.15 = (f32[80,512]{1,0:T(8,128)S(1)}, f32[80,512]{1,0:T(8,128)S(1)}, u32[]{:S(2)}, u32[]{:S(2)}) collective-permute-start(f32[80,512]{1,0:T(8,128)S(1)} %get-tuple-element.97), channel_id=1, source_target_pairs={{8,16},{16,8},{9,17},{17,9},{10,18},{18,10},{11,19},{19,11},{12,20... | collective-permute-start | bytes 491528 | tf_op jit(solution)/shard_map/ppermute | solution.py:703
